TPU v7x, 128 devices: a whole 4x4x4 slice. The times are simulated.
128 devices in a mesh: group: 2 (over x_lo), tile: 64 (over z, x_hi, y, core).
Axes of the slice: x: 4 (x_hi: 2, x_lo: 2; x = x_hi * 2 + x_lo), y: 4, z: 4, core: 2. Of those that a mesh axis runs over, the one named last changes fastest.
Arguments:
- east_wind: float32 [2, 8, 1024, 2048], P('group', None, 'tile'), may hold values from -6 to 6
- equator_wind: float32 [2, 8, 1024, 2048], P('group', None, 'tile'), may hold values from -6 to 6
- pressure: float32 [2, 8, 1024, 2048], P('group', None, 'tile'), may hold values from -6 to 6
- moisture: float32 [2, 8, 1024, 2048], P('group', None, 'tile'), may hold values from 0.05 to 0.5
- albedo: float32 [2, 1024, 2048], P('group', 'tile'), may hold values from 0.05 to 0.8
- courant: float32 [8], replicated, may hold values from 0.3 to 1.2
- sun_angles: float32 [2], replicated, may hold values from -3.140625 to 3.140625
- absorption: float32 [256], replicated, may hold values from 0.01 to 30
- solar_weights: float32 [256], replicated, may hold values from 0.05 to 5
Outputs:
- east_wind_next: float32 [2, 8, 1024, 2048], P('group', None, 'tile')
- equator_wind_next: float32 [2, 8, 1024, 2048], P('group', None, 'tile')
- pressure_next: float32 [2, 8, 1024, 2048], P('group', None, 'tile')
All inputs are finite; a program needn't handle non-finite values.
Results may differ from a plain program's by a relative error of at most 0.0001.
Values sent between devices are 32-bit elements; how exact they have to be, the bound alone decides.
No kernel may reach another device: no remote copies, remote signals or barrier semaphores. Data moves between devices by JAX's collectives and lax.ppermute only.
A program may use at most 128 MiB of HBM per device.

v0:
```python
import jax
import jax.numpy as jnp
from jax import lax
from jax.sharding import PartitionSpec as P

SUB = 6


HEAT_SCALE = 10.0
MU_OFFSET = 0.1
DIFFUSE = 1.66


def extended_2(x, sides, width):
    for axis, dim in sides:
        peers, length = (lax.axis_size(axis), x.shape[dim])
        up = [(i, (i + 1) % peers) for i in range(peers - 1)]
        down = [(j, i) for i, j in up]
        last = lax.slice_in_dim(x, length - width, length, axis=dim)
        leading = lax.slice_in_dim(x, 0, width, axis=dim)
        before = lax.ppermute(last, axis, up)
        after = lax.ppermute(leading, axis, down)
        x = jnp.concatenate([before, x, after], axis=dim)
    return x


def partner(block, axis, distance):
    count = lax.axis_size(axis)
    route = []
    for low in range(count):
        high = low | 1 << distance
        if high != low and high < count:
            route += [(low, high), (high, low)]
    return lax.ppermute(block, axis, route)


def radiate(absorber, sun_cos, surface, absorption, solar_weights):
    sunlit = jnp.maximum(sun_cos, 0.0)
    slant_path = 1.0 / (sunlit + MU_OFFSET)
    optical_depth = jnp.concatenate(
        [jnp.zeros_like(absorber[:1]), jnp.cumsum(absorber, axis=0)], axis=0
    )
    column_depth = optical_depth[-1:]
    coeffs = absorption.reshape((-1,) + (1,) * optical_depth.ndim)
    down_flux = jnp.exp(-coeffs * (optical_depth * slant_path))
    up_flux = jnp.exp(
        -coeffs * (column_depth * slant_path + DIFFUSE * (column_depth - optical_depth))
    )
    weights = (solar_weights / solar_weights.shape[0]).reshape(coeffs.shape)
    net_flux = jnp.sum(weights * (down_flux - surface * up_flux), axis=0) * sunlit
    return HEAT_SCALE * (net_flux[:-1] - net_flux[1:])


def sun_cosine(latitude, longitude, sun_angles):
    declination = 0.41 * jnp.sin(sun_angles[0])
    return jnp.sin(latitude)[:, None] * jnp.sin(declination) + jnp.cos(latitude)[:, None] * jnp.cos(
        declination
    ) * jnp.cos(longitude[None, :] - sun_angles[1])


def rims(fields, flip_signs, rim_width, is_last):
    extended = extended_2(fields, (("tile", 2),), rim_width)
    mirror = partner(fields[:, :, fields.shape[2] - rim_width :, :], "group", 0)
    mirror = jnp.flip(mirror, axis=2) * flip_signs[:, None, None, None]
    inner_rows = extended[:, :, : extended.shape[2] - rim_width, :]
    outer_rows = jnp.where(is_last, mirror, extended[:, :, extended.shape[2] - rim_width :, :])
    return jnp.concatenate([inner_rows, outer_rows], axis=2)


def to_blocks(values):
    leading = values.shape[:-1]
    split_last = values.reshape(leading + (values.shape[-1] // 128, 128))
    return jnp.moveaxis(split_last, -2, 0)


def from_blocks(values):
    merged = jnp.moveaxis(values, 0, -2)
    return merged.reshape(merged.shape[:-2] + (merged.shape[-2] * 128,))


def radiate_blocks(absorber, sun_cos, surface, absorption, solar_weights):

    def one_block(packed):
        block_absorber, block_sun, block_surface = packed
        return lax.cond(
            jnp.max(block_sun) > 0.0,
            lambda: radiate(block_absorber, block_sun, block_surface, absorption, solar_weights),
            lambda: jnp.zeros_like(block_absorber),
        )

    heat_blocks = lax.map(one_block, (to_blocks(absorber), to_blocks(sun_cos), to_blocks(surface)))
    return from_blocks(heat_blocks)


def shards(
    east_wind,
    equator_wind,
    pressure,
    moisture,
    albedo,
    courant,
    sun_angles,
    absorption,
    solar_weights,
):
    zonal_wind = east_wind[0]
    equator_flow = equator_wind[0]
    press_field = pressure[0]
    courant_col = courant[:, None, None]
    tile_index = lax.axis_index("tile")
    is_last = tile_index == lax.axis_size("tile") - 1
    minus_one = jnp.full((1,), -1.0, jnp.float32)
    plus_one = jnp.ones((1,), jnp.float32)
    for substep in range(SUB):
        flow_ext = rims(equator_flow[None], minus_one, 1, is_last)[0]
        divergence = 0.5 * (
            jnp.roll(zonal_wind, -1, 2)
            - jnp.roll(zonal_wind, 1, 2)
            + flow_ext[:, 2:, :]
            - flow_ext[:, :-2, :]
        )
        press_field = press_field - courant_col * divergence
        press_ext = rims(press_field[None], plus_one, 1, is_last)[0]
        zonal_wind = zonal_wind - courant_col * (
            0.5 * (jnp.roll(press_field, -1, 2) - jnp.roll(press_field, 1, 2))
        )
        equator_flow = equator_flow - courant_col * (
            0.5 * (press_ext[:, 2:, :] - press_ext[:, :-2, :])
        )
    moist_field = moisture[0]
    levels, row_count, col_count = moist_field.shape
    half_rows = row_count // 2
    half_cols = col_count // 2
    coarse_moist = moist_field.reshape(levels, half_rows, 2, half_cols, 2).mean(axis=(2, 4))
    coarse_albedo = albedo[0].reshape(half_rows, 2, half_cols, 2).mean(axis=(1, 3))
    total_rows = lax.axis_size("tile") * half_rows
    global_rows = tile_index * half_rows + jnp.arange(half_rows)
    colatitude = 1.0 - (global_rows.astype(jnp.float32) + 0.5) / total_rows
    longitude = 2.0 * jnp.pi * (jnp.arange(half_cols).astype(jnp.float32) + 0.5) / half_cols
    hemisphere = 2.0 * lax.axis_index("group").astype(jnp.float32) - 1.0
    latitude = hemisphere * (0.5 * jnp.pi) * colatitude
    sun_cos = sun_cosine(latitude, longitude, sun_angles)
    heating = radiate_blocks(coarse_moist, sun_cos, coarse_albedo, absorption, solar_weights)
    fine_heat = jnp.repeat(jnp.repeat(heating, 2, axis=1), 2, axis=2)
    return (zonal_wind[None], equator_flow[None], (press_field + fine_heat)[None])


def solution(mesh):
    return jax.shard_map(
        shards,
        mesh=mesh,
        in_specs=(
            P("group", None, "tile", None),
            P("group", None, "tile", None),
            P("group", None, "tile", None),
            P("group", None, "tile", None),
            P("group", "tile", None),
            P(),
            P(),
            P(),
            P(),
        ),
        out_specs=(
            P("group", None, "tile", None),
            P("group", None, "tile", None),
            P("group", None, "tile", None),
        ),
        check_vma=False,
    )
```

profile of v0, /device:TPU:29, one launch (start us, length us, event | category | flops | bytes accessed | tf_op | source)
XLA Modules:
  0.0 340.9 jit_solution(14403924081503291433)
XLA Ops:
  3.0 4.3 %collective-permute-start = (f32[1,8,1,2048]{3,1,2,0:T(8,128)S(1)}, f32[1,8,1,2048]{3,1,2,0:T(8,128)S(1)}, u32[]{:S(2)}, u32[]{:S(2)}) collective-permute-start(f32[1,8,1,2048]{3,1,2,0:T(8,128)S(1)} %copy.491), channel_id=1, source_target_pairs={{0,1},{1,2},{2,3},{3,4},{4,5},{5,6},{6,7},{7,8},{8,9},{9,10},{10,1... | collective-permute-start | bytes 196616 | tf_op jit(solution)/shard_map/ppermute | solution.py:21
  16.0 8.5 %copy.482 = f32[1,8,16,2048]{1,3,2,0:T(8,128)} copy(f32[1,8,16,2048]{3,2,1,0:T(8,128)S(1)} %copy-done.3) | data formatting | bytes 2097152 | tf_op args[3]
  24.6 46.7 %reduce_sum.29 = f32[8,8,1024]{0,2,1:T(8,128)} reduce(f32[8,8,2,1024,2]{0,4,3,2,1:T(2,128)} %bitcast.140, f32[]{:T(128)} %constant.93.clone.1), dimensions={2,4}, to_apply=%region_0.1 | reduce | flops 196608 | bytes 1310724 | tf_op jit(solution)/shard_map/reduce_sum | solution.py:134
  75.0 10.5 %reshape_squeeze.7 = f32[8,2,1024,2]{3,2,1,0:T(8,128)} reshape(f32[1,16,2048]{2,1,0:T(8,128)S(1)} %copy-done.5) | data formatting | bytes 262144 | tf_op jit(solution)/shard_map/reshape;squeeze | solution.py:135
  85.5 4.6 %reduce_sum.30 = f32[8,1024]{1,0:T(8,128)S(1)} reduce(f32[8,2,1024,2]{3,2,1,0:T(8,128)} %reshape_squeeze.7, f32[]{:T(128)} %constant.93.clone.1), dimensions={1,3}, to_apply=%region_1.2 | reduce | flops 24576 | bytes 163844 | tf_op jit(solution)/shard_map/reduce_sum | solution.py:135
  90.3 39.4 %while.10 = (s32[]{:T(128)}, f32[8,8,8,128]{3,2,1,0:T(8,128)S(1)}, f32[8,8,128]{2,1,0:T(8,128)S(1)}, f32[256]{0:T(256)S(1)}, f32[256]{0:T(256)S(1)}, /*index=5*/...) while((s32[]{:T(128)}, f32[8,8,8,128]{3,2,1,0:T(8,128)S(1)}, ...), condition=%wide.region_8.9_spmd, body=%wide.region_2.8_spmd.sunk | while | flops 14275075 | bytes 592063 | solution.py:91
  132.8 6.1 %broadcast_in_dim.84 = f32[8,16,1024,2]{1,0,3,2:T(8,128)} broadcast(f32[8,16,1024]{1,0,2:T(8,128)} %copy.487), dimensions={0,1,2} | broadcast | bytes 1572864 | tf_op jit(solution)/shard_map/broadcast_in_dim | solution.py:144
  138.9 5.4 %copy.488 = f32[8,16,2048]{2,1,0:T(8,128)S(1)} copy(f32[8,16,2048]{1,0,2:T(8,128)} %bitcast.141) | data formatting | bytes 2097152 | tf_op jit(solution)/shard_map/reshape | solution.py:144
  149.5 8.0 %collective-permute-start.3 = (f32[1,8,1,2048]{3,1,2,0:T(8,128)S(1)}, f32[1,8,1,2048]{3,1,2,0:T(8,128)S(1)}, u32[]{:S(2)}, u32[]{:S(2)}) collective-permute-start(f32[1,8,1,2048]{3,1,2,0:T(8,128)S(1)} %copy.417), channel_id=1, source_target_pairs={{0,1},{1,2},{2,3},{3,4},{4,5},{5,6},{6,7},{7,8},{8,9},{9,10},{10,1... | collective-permute-start | bytes 196616 | tf_op jit(solution)/shard_map/ppermute | solution.py:21
  162.3 8.4 %collective-permute-start.6 = (f32[1,8,1,2048]{3,1,2,0:T(8,128)S(1)}, f32[1,8,1,2048]{3,1,2,0:T(8,128)S(1)}, u32[]{:S(2)}, u32[]{:S(2)}) collective-permute-start(f32[1,8,1,2048]{3,1,2,0:T(8,128)S(1)} %copy.422), channel_id=1, source_target_pairs={{0,1},{1,2},{2,3},{3,4},{4,5},{5,6},{6,7},{7,8},{8,9},{9,10},{10,1... | collective-permute-start | bytes 196616 | tf_op jit(solution)/shard_map/ppermute | solution.py:21
  173.1 7.7 %collective-permute-done.8 = f32[1,8,1,2048]{3,1,2,0:T(8,128)S(1)} collective-permute-done((f32[1,8,1,2048]{3,1,2,0:T(8,128)S(1)}, f32[1,8,1,2048]{3,1,2,0:T(8,128)S(1)}, u32[]{:S(2)}, u32[]{:S(2)}) %collective-permute-start.8) | collective-permute-done | bytes 65568 | tf_op jit(solution)/shard_map/ppermute | solution.py:22
  185.1 8.2 %collective-permute-start.9 = (f32[1,8,1,2048]{3,1,2,0:T(8,128)S(1)}, f32[1,8,1,2048]{3,1,2,0:T(8,128)S(1)}, u32[]{:S(2)}, u32[]{:S(2)}) collective-permute-start(f32[1,8,1,2048]{3,1,2,0:T(8,128)S(1)} %copy.429), channel_id=1, source_target_pairs={{0,1},{1,2},{2,3},{3,4},{4,5},{5,6},{6,7},{7,8},{8,9},{9,10},{10,1... | collective-permute-start | bytes 196616 | tf_op jit(solution)/shard_map/ppermute | solution.py:21
  196.9 8.4 %collective-permute-start.12 = (f32[1,8,1,2048]{3,1,2,0:T(8,128)S(1)}, f32[1,8,1,2048]{3,1,2,0:T(8,128)S(1)}, u32[]{:S(2)}, u32[]{:S(2)}) collective-permute-start(f32[1,8,1,2048]{3,1,2,0:T(8,128)S(1)} %copy.434), channel_id=1, source_target_pairs={{0,1},{1,2},{2,3},{3,4},{4,5},{5,6},{6,7},{7,8},{8,9},{9,10},{10,1... | collective-permute-start | bytes 196616 | tf_op jit(solution)/shard_map/ppermute | solution.py:21
  207.8 7.7 %collective-permute-done.14 = f32[1,8,1,2048]{3,1,2,0:T(8,128)S(1)} collective-permute-done((f32[1,8,1,2048]{3,1,2,0:T(8,128)S(1)}, f32[1,8,1,2048]{3,1,2,0:T(8,128)S(1)}, u32[]{:S(2)}, u32[]{:S(2)}) %collective-permute-start.14) | collective-permute-done | bytes 65568 | tf_op jit(solution)/shard_map/ppermute | solution.py:22
  220.9 8.2 %collective-permute-start.15 = (f32[1,8,1,2048]{3,1,2,0:T(8,128)S(1)}, f32[1,8,1,2048]{3,1,2,0:T(8,128)S(1)}, u32[]{:S(2)}, u32[]{:S(2)}) collective-permute-start(f32[1,8,1,2048]{3,1,2,0:T(8,128)S(1)} %copy.441), channel_id=1, source_target_pairs={{0,1},{1,2},{2,3},{3,4},{4,5},{5,6},{6,7},{7,8},{8,9},{9,10},{10,1... | collective-permute-start | bytes 196616 | tf_op jit(solution)/shard_map/ppermute | solution.py:21
  231.5 8.8 %collective-permute-start.18 = (f32[1,8,1,2048]{3,1,2,0:T(8,128)S(1)}, f32[1,8,1,2048]{3,1,2,0:T(8,128)S(1)}, u32[]{:S(2)}, u32[]{:S(2)}) collective-permute-start(f32[1,8,1,2048]{3,1,2,0:T(8,128)S(1)} %copy.446), channel_id=1, source_target_pairs={{0,1},{1,2},{2,3},{3,4},{4,5},{5,6},{6,7},{7,8},{8,9},{9,10},{10,1... | collective-permute-start | bytes 196616 | tf_op jit(solution)/shard_map/ppermute | solution.py:21
  243.0 7.5 %collective-permute-done.20 = f32[1,8,1,2048]{3,1,2,0:T(8,128)S(1)} collective-permute-done((f32[1,8,1,2048]{3,1,2,0:T(8,128)S(1)}, f32[1,8,1,2048]{3,1,2,0:T(8,128)S(1)}, u32[]{:S(2)}, u32[]{:S(2)}) %collective-permute-start.20) | collective-permute-done | bytes 65568 | tf_op jit(solution)/shard_map/ppermute | solution.py:22
  256.5 8.2 %collective-permute-start.21 = (f32[1,8,1,2048]{3,1,2,0:T(8,128)S(1)}, f32[1,8,1,2048]{3,1,2,0:T(8,128)S(1)}, u32[]{:S(2)}, u32[]{:S(2)}) collective-permute-start(f32[1,8,1,2048]{3,1,2,0:T(8,128)S(1)} %copy.453), channel_id=1, source_target_pairs={{0,1},{1,2},{2,3},{3,4},{4,5},{5,6},{6,7},{7,8},{8,9},{9,10},{10,1... | collective-permute-start | bytes 196616 | tf_op jit(solution)/shard_map/ppermute | solution.py:21
  267.3 8.8 %collective-permute-start.24 = (f32[1,8,1,2048]{3,1,2,0:T(8,128)S(1)}, f32[1,8,1,2048]{3,1,2,0:T(8,128)S(1)}, u32[]{:S(2)}, u32[]{:S(2)}) collective-permute-start(f32[1,8,1,2048]{3,1,2,0:T(8,128)S(1)} %copy.458), channel_id=1, source_target_pairs={{0,1},{1,2},{2,3},{3,4},{4,5},{5,6},{6,7},{7,8},{8,9},{9,10},{10,1... | collective-permute-start | bytes 196616 | tf_op jit(solution)/shard_map/ppermute | solution.py:21
  278.5 7.7 %collective-permute-done.26 = f32[1,8,1,2048]{3,1,2,0:T(8,128)S(1)} collective-permute-done((f32[1,8,1,2048]{3,1,2,0:T(8,128)S(1)}, f32[1,8,1,2048]{3,1,2,0:T(8,128)S(1)}, u32[]{:S(2)}, u32[]{:S(2)}) %collective-permute-start.26) | collective-permute-done | bytes 65568 | tf_op jit(solution)/shard_map/ppermute | solution.py:22
  292.3 8.2 %collective-permute-start.27 = (f32[1,8,1,2048]{3,1,2,0:T(8,128)S(1)}, f32[1,8,1,2048]{3,1,2,0:T(8,128)S(1)}, u32[]{:S(2)}, u32[]{:S(2)}) collective-permute-start(f32[1,8,1,2048]{3,1,2,0:T(8,128)S(1)} %copy.465), channel_id=1, source_target_pairs={{0,1},{1,2},{2,3},{3,4},{4,5},{5,6},{6,7},{7,8},{8,9},{9,10},{10,1... | collective-permute-start | bytes 196616 | tf_op jit(solution)/shard_map/ppermute | solution.py:21
  303.0 8.8 %collective-permute-start.30 = (f32[1,8,1,2048]{3,1,2,0:T(8,128)S(1)}, f32[1,8,1,2048]{3,1,2,0:T(8,128)S(1)}, u32[]{:S(2)}, u32[]{:S(2)}) collective-permute-start(f32[1,8,1,2048]{3,1,2,0:T(8,128)S(1)} %copy.470), channel_id=1, source_target_pairs={{0,1},{1,2},{2,3},{3,4},{4,5},{5,6},{6,7},{7,8},{8,9},{9,10},{10,1... | collective-permute-start | bytes 196616 | tf_op jit(solution)/shard_map/ppermute | solution.py:21
  314.1 7.7 %collective-permute-done.32 = f32[1,8,1,2048]{3,1,2,0:T(8,128)S(1)} collective-permute-done((f32[1,8,1,2048]{3,1,2,0:T(8,128)S(1)}, f32[1,8,1,2048]{3,1,2,0:T(8,128)S(1)}, u32[]{:S(2)}, u32[]{:S(2)}) %collective-permute-start.32) | collective-permute-done | bytes 65568 | tf_op jit(solution)/shard_map/ppermute | solution.py:22
  334.9 4.1 %collective-permute-done.35 = f32[1,8,1,2048]{3,1,2,0:T(8,128)S(1)} collective-permute-done((f32[1,8,1,2048]{3,1,2,0:T(8,128)S(1)}, f32[1,8,1,2048]{3,1,2,0:T(8,128)S(1)}, u32[]{:S(2)}, u32[]{:S(2)}) %collective-permute-start.35) | collective-permute-done | bytes 65568 | tf_op jit(solution)/shard_map/ppermute | solution.py:22
  (307 shorter events, 149.8 us)
Async XLA Ops:
  2.0 142.3 %collective-permute-start.1 = (f32[1,8,1,2048]{3,1,2,0:T(8,128)S(1)}, f32[1,8,1,2048]{3,1,2,0:T(8,128)S(1)}, u32[]{:S(2)}, u32[]{:S(2)}) collective-permute-start(f32[1,8,1,2048]{3,1,2,0:T(8,128)S(1)} %copy.491), channel_id=1, source_target_pairs={{0,64},{64,0},{1,65},{65,1},{2,66},{66,2},{3,67},{67,3},{4,68},{68... | collective-permute-start | bytes 196616 | tf_op jit(solution)/shard_map/ppermute | solution.py:34
  3.0 141.4 %collective-permute-start = (f32[1,8,1,2048]{3,1,2,0:T(8,128)S(1)}, f32[1,8,1,2048]{3,1,2,0:T(8,128)S(1)}, u32[]{:S(2)}, u32[]{:S(2)}) collective-permute-start(f32[1,8,1,2048]{3,1,2,0:T(8,128)S(1)} %copy.491), channel_id=1, source_target_pairs={{0,1},{1,2},{2,3},{3,4},{4,5},{5,6},{6,7},{7,8},{8,9},{9,10},{10,1... | collective-permute-start | bytes 196616 | tf_op jit(solution)/shard_map/ppermute | solution.py:21
  7.9 136.4 %collective-permute-start.2 = (f32[1,8,1,2048]{3,1,2,0:T(8,128)}, f32[1,8,1,2048]{3,1,2,0:T(8,128)S(1)}, u32[]{:S(2)}, u32[]{:S(2)}) collective-permute-start(f32[1,8,1,2048]{3,1,2,0:T(8,128)} %copy.492), channel_id=1, source_target_pairs={{1,0},{2,1},{3,2},{4,3},{5,4},{6,5},{7,6},{8,7},{9,8},{10,9},{11,1... | collective-permute-start | bytes 196616 | tf_op jit(solution)/shard_map/ppermute | solution.py:22
  147.1 10.5 %collective-permute-start.4 = (f32[1,8,1,2048]{3,1,2,0:T(8,128)S(1)}, f32[1,8,1,2048]{3,1,2,0:T(8,128)S(1)}, u32[]{:S(2)}, u32[]{:S(2)}) collective-permute-start(f32[1,8,1,2048]{3,1,2,0:T(8,128)S(1)} %copy.417), channel_id=1, source_target_pairs={{0,64},{64,0},{1,65},{65,1},{2,66},{66,2},{3,67},{67,3},{4,68},{68... | collective-permute-start | bytes 196616 | tf_op jit(solution)/shard_map/ppermute | solution.py:34
  147.2 10.3 %collective-permute-start.5 = (f32[1,8,1,2048]{3,1,2,0:T(8,128)S(1)}, f32[1,8,1,2048]{3,1,2,0:T(8,128)S(1)}, u32[]{:S(2)}, u32[]{:S(2)}) collective-permute-start(f32[1,8,1,2048]{3,1,2,0:T(8,128)S(1)} %copy.419), channel_id=1, source_target_pairs={{1,0},{2,1},{3,2},{4,3},{5,4},{6,5},{7,6},{8,7},{9,8},{10,9},{11,1... | collective-permute-start | bytes 196616 | tf_op jit(solution)/shard_map/ppermute | solution.py:22
  159.9 21.0 %collective-permute-start.7 = (f32[1,8,1,2048]{3,1,2,0:T(8,128)S(1)}, f32[1,8,1,2048]{3,1,2,0:T(8,128)S(1)}, u32[]{:S(2)}, u32[]{:S(2)}) collective-permute-start(f32[1,8,1,2048]{3,1,2,0:T(8,128)S(1)} %copy.422), channel_id=1, source_target_pairs={{0,64},{64,0},{1,65},{65,1},{2,66},{66,2},{3,67},{67,3},{4,68},{68... | collective-permute-start | bytes 196616 | tf_op jit(solution)/shard_map/ppermute | solution.py:34
  162.3 18.7 %collective-permute-start.6 = (f32[1,8,1,2048]{3,1,2,0:T(8,128)S(1)}, f32[1,8,1,2048]{3,1,2,0:T(8,128)S(1)}, u32[]{:S(2)}, u32[]{:S(2)}) collective-permute-start(f32[1,8,1,2048]{3,1,2,0:T(8,128)S(1)} %copy.422), channel_id=1, source_target_pairs={{0,1},{1,2},{2,3},{3,4},{4,5},{5,6},{6,7},{7,8},{8,9},{9,10},{10,1... | collective-permute-start | bytes 196616 | tf_op jit(solution)/shard_map/ppermute | solution.py:21
  182.6 10.6 %collective-permute-start.10 = (f32[1,8,1,2048]{3,1,2,0:T(8,128)S(1)}, f32[1,8,1,2048]{3,1,2,0:T(8,128)S(1)}, u32[]{:S(2)}, u32[]{:S(2)}) collective-permute-start(f32[1,8,1,2048]{3,1,2,0:T(8,128)S(1)} %copy.429), channel_id=1, source_target_pairs={{0,64},{64,0},{1,65},{65,1},{2,66},{66,2},{3,67},{67,3},{4,68},{68... | collective-permute-start | bytes 196616 | tf_op jit(solution)/shard_map/ppermute | solution.py:34
  183.1 10.2 %collective-permute-start.11 = (f32[1,8,1,2048]{3,1,2,0:T(8,128)S(1)}, f32[1,8,1,2048]{3,1,2,0:T(8,128)S(1)}, u32[]{:S(2)}, u32[]{:S(2)}) collective-permute-start(f32[1,8,1,2048]{3,1,2,0:T(8,128)S(1)} %copy.431), channel_id=1, source_target_pairs={{1,0},{2,1},{3,2},{4,3},{5,4},{6,5},{7,6},{8,7},{9,8},{10,9},{11,1... | collective-permute-start | bytes 196616 | tf_op jit(solution)/shard_map/ppermute | solution.py:22
  195.8 19.8 %collective-permute-start.13 = (f32[1,8,1,2048]{3,1,2,0:T(8,128)S(1)}, f32[1,8,1,2048]{3,1,2,0:T(8,128)S(1)}, u32[]{:S(2)}, u32[]{:S(2)}) collective-permute-start(f32[1,8,1,2048]{3,1,2,0:T(8,128)S(1)} %copy.434), channel_id=1, source_target_pairs={{0,64},{64,0},{1,65},{65,1},{2,66},{66,2},{3,67},{67,3},{4,68},{68... | collective-permute-start | bytes 196616 | tf_op jit(solution)/shard_map/ppermute | solution.py:34
  196.9 18.7 %collective-permute-start.12 = (f32[1,8,1,2048]{3,1,2,0:T(8,128)S(1)}, f32[1,8,1,2048]{3,1,2,0:T(8,128)S(1)}, u32[]{:S(2)}, u32[]{:S(2)}) collective-permute-start(f32[1,8,1,2048]{3,1,2,0:T(8,128)S(1)} %copy.434), channel_id=1, source_target_pairs={{0,1},{1,2},{2,3},{3,4},{4,5},{5,6},{6,7},{7,8},{8,9},{9,10},{10,1... | collective-permute-start | bytes 196616 | tf_op jit(solution)/shard_map/ppermute | solution.py:21
  217.2 11.8 %collective-permute-start.16 = (f32[1,8,1,2048]{3,1,2,0:T(8,128)S(1)}, f32[1,8,1,2048]{3,1,2,0:T(8,128)S(1)}, u32[]{:S(2)}, u32[]{:S(2)}) collective-permute-start(f32[1,8,1,2048]{3,1,2,0:T(8,128)S(1)} %copy.441), channel_id=1, source_target_pairs={{0,64},{64,0},{1,65},{65,1},{2,66},{66,2},{3,67},{67,3},{4,68},{68... | collective-permute-start | bytes 196616 | tf_op jit(solution)/shard_map/ppermute | solution.py:34
  218.8 10.2 %collective-permute-start.17 = (f32[1,8,1,2048]{3,1,2,0:T(8,128)S(1)}, f32[1,8,1,2048]{3,1,2,0:T(8,128)S(1)}, u32[]{:S(2)}, u32[]{:S(2)}) collective-permute-start(f32[1,8,1,2048]{3,1,2,0:T(8,128)S(1)} %copy.443), channel_id=1, source_target_pairs={{1,0},{2,1},{3,2},{4,3},{5,4},{6,5},{7,6},{8,7},{9,8},{10,9},{11,1... | collective-permute-start | bytes 196616 | tf_op jit(solution)/shard_map/ppermute | solution.py:22
  231.5 19.0 %collective-permute-start.19 = (f32[1,8,1,2048]{3,1,2,0:T(8,128)S(1)}, f32[1,8,1,2048]{3,1,2,0:T(8,128)S(1)}, u32[]{:S(2)}, u32[]{:S(2)}) collective-permute-start(f32[1,8,1,2048]{3,1,2,0:T(8,128)S(1)} %copy.446), channel_id=1, source_target_pairs={{0,64},{64,0},{1,65},{65,1},{2,66},{66,2},{3,67},{67,3},{4,68},{68... | collective-permute-start | bytes 196616 | tf_op jit(solution)/shard_map/ppermute | solution.py:34
  231.5 19.0 %collective-permute-start.18 = (f32[1,8,1,2048]{3,1,2,0:T(8,128)S(1)}, f32[1,8,1,2048]{3,1,2,0:T(8,128)S(1)}, u32[]{:S(2)}, u32[]{:S(2)}) collective-permute-start(f32[1,8,1,2048]{3,1,2,0:T(8,128)S(1)} %copy.446), channel_id=1, source_target_pairs={{0,1},{1,2},{2,3},{3,4},{4,5},{5,6},{6,7},{7,8},{8,9},{9,10},{10,1... | collective-permute-start | bytes 196616 | tf_op jit(solution)/shard_map/ppermute | solution.py:21
  252.1 12.6 %collective-permute-start.22 = (f32[1,8,1,2048]{3,1,2,0:T(8,128)S(1)}, f32[1,8,1,2048]{3,1,2,0:T(8,128)S(1)}, u32[]{:S(2)}, u32[]{:S(2)}) collective-permute-start(f32[1,8,1,2048]{3,1,2,0:T(8,128)S(1)} %copy.453), channel_id=1, source_target_pairs={{0,64},{64,0},{1,65},{65,1},{2,66},{66,2},{3,67},{67,3},{4,68},{68... | collective-permute-start | bytes 196616 | tf_op jit(solution)/shard_map/ppermute | solution.py:34
  254.5 10.2 %collective-permute-start.23 = (f32[1,8,1,2048]{3,1,2,0:T(8,128)S(1)}, f32[1,8,1,2048]{3,1,2,0:T(8,128)S(1)}, u32[]{:S(2)}, u32[]{:S(2)}) collective-permute-start(f32[1,8,1,2048]{3,1,2,0:T(8,128)S(1)} %copy.455), channel_id=1, source_target_pairs={{1,0},{2,1},{3,2},{4,3},{5,4},{6,5},{7,6},{8,7},{9,8},{10,9},{11,1... | collective-permute-start | bytes 196616 | tf_op jit(solution)/shard_map/ppermute | solution.py:22
  267.2 19.0 %collective-permute-start.25 = (f32[1,8,1,2048]{3,1,2,0:T(8,128)S(1)}, f32[1,8,1,2048]{3,1,2,0:T(8,128)S(1)}, u32[]{:S(2)}, u32[]{:S(2)}) collective-permute-start(f32[1,8,1,2048]{3,1,2,0:T(8,128)S(1)} %copy.458), channel_id=1, source_target_pairs={{0,64},{64,0},{1,65},{65,1},{2,66},{66,2},{3,67},{67,3},{4,68},{68... | collective-permute-start | bytes 196616 | tf_op jit(solution)/shard_map/ppermute | solution.py:34
  267.3 19.0 %collective-permute-start.24 = (f32[1,8,1,2048]{3,1,2,0:T(8,128)S(1)}, f32[1,8,1,2048]{3,1,2,0:T(8,128)S(1)}, u32[]{:S(2)}, u32[]{:S(2)}) collective-permute-start(f32[1,8,1,2048]{3,1,2,0:T(8,128)S(1)} %copy.458), channel_id=1, source_target_pairs={{0,1},{1,2},{2,3},{3,4},{4,5},{5,6},{6,7},{7,8},{8,9},{9,10},{10,1... | collective-permute-start | bytes 196616 | tf_op jit(solution)/shard_map/ppermute | solution.py:21
  287.9 12.6 %collective-permute-start.28 = (f32[1,8,1,2048]{3,1,2,0:T(8,128)S(1)}, f32[1,8,1,2048]{3,1,2,0:T(8,128)S(1)}, u32[]{:S(2)}, u32[]{:S(2)}) collective-permute-start(f32[1,8,1,2048]{3,1,2,0:T(8,128)S(1)} %copy.465), channel_id=1, source_target_pairs={{0,64},{64,0},{1,65},{65,1},{2,66},{66,2},{3,67},{67,3},{4,68},{68... | collective-permute-start | bytes 196616 | tf_op jit(solution)/shard_map/ppermute | solution.py:34
  302.9 19.0 %collective-permute-start.31 = (f32[1,8,1,2048]{3,1,2,0:T(8,128)S(1)}, f32[1,8,1,2048]{3,1,2,0:T(8,128)S(1)}, u32[]{:S(2)}, u32[]{:S(2)}) collective-permute-start(f32[1,8,1,2048]{3,1,2,0:T(8,128)S(1)} %copy.470), channel_id=1, source_target_pairs={{0,64},{64,0},{1,65},{65,1},{2,66},{66,2},{3,67},{67,3},{4,68},{68... | collective-permute-start | bytes 196616 | tf_op jit(solution)/shard_map/ppermute | solution.py:34
  303.0 19.0 %collective-permute-start.30 = (f32[1,8,1,2048]{3,1,2,0:T(8,128)S(1)}, f32[1,8,1,2048]{3,1,2,0:T(8,128)S(1)}, u32[]{:S(2)}, u32[]{:S(2)}) collective-permute-start(f32[1,8,1,2048]{3,1,2,0:T(8,128)S(1)} %copy.470), channel_id=1, source_target_pairs={{0,1},{1,2},{2,3},{3,4},{4,5},{5,6},{6,7},{7,8},{8,9},{9,10},{10,1... | collective-permute-start | bytes 196616 | tf_op jit(solution)/shard_map/ppermute | solution.py:21
  324.5 10.4 %collective-permute-start.34 = (f32[1,8,1,2048]{3,1,2,0:T(8,128)S(1)}, f32[1,8,1,2048]{3,1,2,0:T(8,128)S(1)}, u32[]{:S(2)}, u32[]{:S(2)}) collective-permute-start(f32[1,8,1,2048]{3,1,2,0:T(8,128)S(1)} %copy.477), channel_id=1, source_target_pairs={{0,64},{64,0},{1,65},{65,1},{2,66},{66,2},{3,67},{67,3},{4,68},{68... | collective-permute-start | bytes 196616 | tf_op jit(solution)/shard_map/ppermute | solution.py:34
  326.9 12.1 %collective-permute-start.33 = (f32[1,8,1,2048]{3,1,2,0:T(8,128)S(1)}, f32[1,8,1,2048]{3,1,2,0:T(8,128)S(1)}, u32[]{:S(2)}, u32[]{:S(2)}) collective-permute-start(f32[1,8,1,2048]{3,1,2,0:T(8,128)S(1)} %copy.477), channel_id=1, source_target_pairs={{0,1},{1,2},{2,3},{3,4},{4,5},{5,6},{6,7},{7,8},{8,9},{9,10},{10,1... | collective-permute-start | bytes 196616 | tf_op jit(solution)/shard_map/ppermute | solution.py:21
  (22 other events, 194.0 us)
where the time goes:
time: 342 us; the launch traced here: 341 us
  starting transfers between devices  128 us (37%)
  other arithmetic  102 us (30%)
  local copies, waits for them, and re-layouts  53.9 us (16%)
  waiting for transfers between devices  48.5 us (14%)
  loops' own time  5.49 us (2%)
    ppermute x12, starting transfers between devices, extended_2(): before = lax.ppermute(last, axis, up)  90 us
    reduce_sum x1, other arithmetic, shards(): moist_field.reshape(levels, half_rows, 2, half_cols, 2).mean(axis=(2, 4))  46.7 us
    ppermute x12, waiting for transfers between devices, extended_2(): after = lax.ppermute(leading, axis, down)  42.5 us
    reduce_sum x8, other arithmetic, radiate(): jnp.sum(weights * (down_flux - surface * up_flux), axis=0) * sunlit  28.4 us
    ppermute x12, starting transfers between devices, extended_2(): after = lax.ppermute(leading, axis, down)  24 us
    ppermute x12, starting transfers between devices, partner(): return lax.ppermute(block, axis, route)  14.3 us
    unnamed x24, local copies, waits for them, and re-layouts  11.1 us
    another operation x1, local copies, waits for them, and re-layouts, shards(): albedo[0].reshape(half_rows, 2, half_cols, 2).mean(axis=(1, 3))  10.5 us
  transfers between devices with their start and end apart: 36, of which 11 were waited for; matrix products, arithmetic and copies ran while one was open for 40% of the time, Pallas kernels for 0%

commit v1 on v0

v1 whole, which is shorter than its diff:
```python
import functools
import math

import jax
import jax.numpy as jnp
from jax import lax
from jax.experimental import pallas as pl
from jax.experimental.pallas import tpu as pltpu
from jax.sharding import PartitionSpec as P

SUB = 6
HEAT_SCALE = 10.0
MU_OFFSET = 0.1
DIFFUSE = 1.66
LOG2E = 1.4426950408889634
LANES = 128
OFF = 8

VMEM = pltpu.VMEM
SMEM = pltpu.SMEM
F32 = jnp.float32


def lane_iota(dtype=jnp.int32):
    return lax.broadcasted_iota(dtype, (8, LANES), 1)


def sub_iota():
    return lax.broadcasted_iota(jnp.int32, (8, LANES), 0)


def coarsen_kernel(moist, albedo, keep, send):
    width = moist.shape[-1]
    half = keep.shape[-1] // LANES
    even_row = sub_iota() % 2 == 0
    even_lane = lane_iota() % 2 == 0

    def fold(top, bottom):
        return jnp.where(
            even_row, top + pltpu.roll(top, 7, 0), bottom + pltpu.roll(bottom, 1, 0)
        )

    def pack(left, right):
        return jnp.where(
            even_lane,
            left + pltpu.roll(left, LANES - 1, 1),
            right + pltpu.roll(right, 1, 1),
        )

    for level in range(9):
        for block in range(width // (2 * LANES)):
            parts = []
            for side in range(2):
                cols = pl.ds((2 * block + side) * LANES, LANES)
                if level < 8:
                    parts.append((moist[level, 0:8, cols], moist[level, 8:16, cols]))
                else:
                    parts.append((albedo[0:8, cols], albedo[8:16, cols]))
            top = pack(parts[0][0], parts[1][0])
            bottom = pack(parts[0][1], parts[1][1])
            value = fold(top, bottom) * 0.25
            if block < half:
                keep[level, :, pl.ds(block * LANES, LANES)] = value
            else:
                send[level, :, pl.ds((block - half) * LANES, LANES)] = value


def radiate_kernel(
    rows_total, cols_total, sun, absorption, weights, own, other, heat_own, heat_other
):
    group = lax.axis_index("group")
    tile = lax.axis_index("tile")
    sublane = sub_iota()
    lane = lane_iota()
    row = tile * 8 + sublane // 2 + 4 * (sublane % 2)
    colatitude = 1.0 - (row.astype(F32) + 0.5) / rows_total
    hemisphere = 2.0 * group.astype(F32) - 1.0
    latitude = hemisphere * (0.5 * math.pi) * colatitude
    declination = 0.41 * jnp.sin(jnp.full((8, LANES), sun[0], F32))
    sine = jnp.sin(latitude) * jnp.sin(declination)
    cosine = jnp.cos(latitude) * jnp.cos(declination)
    n_g = absorption.shape[0]

    for block in range(own.shape[-1] // LANES):
        cols = pl.ds(block * LANES, LANES)
        column = block * LANES + lane // 2 + 64 * (lane % 2)
        longitude = 2.0 * math.pi * (column.astype(F32) + 0.5) / cols_total
        mu = sine + cosine * jnp.cos(longitude - sun[1])
        lit = mu > 0.0
        sunlit = jnp.abs(mu)
        slant = 1.0 / (sunlit + MU_OFFSET)
        depth = [jnp.zeros((8, LANES), F32)]
        for level in range(8):
            layer = jnp.where(lit, own[level, :, cols], other[level, :, cols])
            depth.append(depth[-1] + layer)
        surface = jnp.where(lit, own[8, :, cols], other[8, :, cols])
        total = depth[8]
        direct = total * slant
        paths = [depth[j] * slant for j in range(1, 9)]
        paths += [direct + DIFFUSE * (total - depth[j]) for j in range(8)]

        def body(g, carry):
            rate = absorption[g] * (-LOG2E)
            weight = weights[g]
            sums, whole = carry[:-1], carry[-1]
            sums = tuple(a + weight * jnp.exp2(rate * p) for a, p in zip(sums, paths))
            return sums + (whole + weight,)

        zero = jnp.zeros((8, LANES), F32)
        sums = lax.fori_loop(0, n_g, body, (zero,) * 17, unroll=32)
        down = (sums[16],) + sums[:8]
        up = sums[8:16] + (sums[7],)
        scale = sunlit * (HEAT_SCALE / n_g)
        net = [scale * (down[j] - surface * up[j]) for j in range(9)]
        for level in range(8):
            heat = net[level] - net[level + 1]
            heat_own[level, :, cols] = jnp.where(lit, heat, 0.0)
            heat_other[level, :, cols] = jnp.where(lit, 0.0, heat)


def courant_half(courant):
    level = sub_iota()
    value = jnp.full((8, LANES), courant[7], F32)
    for index in range(7):
        value = jnp.where(level == index, courant[index], value)
    return 0.5 * value


def load_row(ref, row):
    return [ref[row, :, pl.ds(j * LANES, LANES)] for j in range(ref.shape[-1] // LANES)]


def store_row(ref, row, values):
    for j, value in enumerate(values):
        ref[row, :, pl.ds(j * LANES, LANES)] = value


def shifted(values, by):
    count = len(values)
    turned = [pltpu.roll(v, (-by) % LANES, 1) for v in values]
    lane = lane_iota()
    if by > 0:
        edge = lane >= LANES - by
        return [jnp.where(edge, turned[(j + 1) % count], turned[j]) for j in range(count)]
    edge = lane < -by
    return [jnp.where(edge, turned[j - 1], turned[j]) for j in range(count)]


def stage(east_in, flow_in, press_in, east, flow, press, half):
    for block in range(2):
        rows = pl.ds(8 * block, 8)
        inner = pl.ds(OFF + 8 * block, 8)
        flow[inner] = jnp.swapaxes(flow_in[:, rows, :], 0, 1)
        east[inner] = jnp.swapaxes(east_in[:, rows, :], 0, 1)
        press[inner] = jnp.swapaxes(press_in[:, rows, :], 0, 1)
    for row in range(OFF, OFF + 16):
        store_row(east, row, shifted(load_row(east, row), 1))
        store_row(press, row, [half * v for v in load_row(press, row)])


def press_rows(rows, east, flow, press, rate):
    for row in rows:
        here = load_row(east, row)
        back = shifted(here, -2)
        ahead, behind = load_row(flow, row + 1), load_row(flow, row - 1)
        old = load_row(press, row)
        store_row(
            press,
            row,
            [
                p - rate * ((e - b) + (n - s))
                for p, e, b, n, s in zip(old, here, back, ahead, behind)
            ],
        )


def east_rows(rows, east, press):
    for row in rows:
        here = load_row(press, row)
        ahead = shifted(here, 2)
        old = load_row(east, row)
        store_row(east, row, [e - (a - p) for e, a, p in zip(old, ahead, here)])


def flow_rows(rows, flow, press):
    for row in rows:
        ahead, behind = load_row(press, row + 1), load_row(press, row - 1)
        old = load_row(flow, row)
        store_row(flow, row, [q - (n - s) for q, n, s in zip(old, ahead, behind)])


def spans(*pairs):
    return [OFF + row for low, high in pairs for row in range(low, high + 1)]


PRESS_SPANS = [
    spans((-1, 16)),
    spans((-3, 18)),
    spans((-5, 6), (9, 20)),
    spans((-5, 4), (11, 20)),
    spans((-3, 2), (13, 18)),
    spans((-1, 0), (15, 16)),
]
EAST_SPANS = [
    spans((-1, 16)),
    spans((-3, 6), (9, 18)),
    spans((-5, 4), (11, 20)),
    spans((-3, 2), (13, 18)),
    spans((-1, 0), (15, 16)),
]
FLOW_SPANS = [
    spans((-2, 17)),
    spans((-4, 19)),
    spans((-6, 5), (10, 21)),
    spans((-4, 3), (12, 19)),
    spans((-2, 1), (14, 17)),
]


def alone_kernel(
    courant, east_in, flow_in, press_in, low_out, high_out, up, down, east, flow, press
):
    group = lax.axis_index("group")
    half = courant_half(courant)
    rate = half * half
    zero = jnp.zeros((8, LANES), F32)
    count = east.shape[-1] // LANES
    for row in spans((-8, -1), (16, 23)):
        for ref in (east, flow, press):
            store_row(ref, row, [zero] * count)
    stage(east_in, flow_in, press_in, east, flow, press, half)

    def record(slot, ref):
        store_row(low_out, slot, load_row(ref, OFF - 1))
        store_row(high_out, slot, load_row(ref, OFF + 16))
        first, last = load_row(ref, OFF), load_row(ref, OFF + 15)

        @pl.when(group == 0)
        def _():
            store_row(up, slot, last)
            store_row(down, slot, first)

        @pl.when(group != 0)
        def _():
            store_row(up, slot, first)
            store_row(down, slot, last)

    for step in range(SUB):
        record(step, flow)
        press_rows(PRESS_SPANS[step], east, flow, press, rate)
        record(SUB + step, press)
        if step < SUB - 1:
            east_rows(EAST_SPANS[step], east, press)
            flow_rows(FLOW_SPANS[step], flow, press)


def joined_kernel(
    n_tiles,
    courant,
    east_in,
    flow_in,
    press_in,
    low_own,
    high_own,
    from_before,
    from_after,
    east_out,
    flow_out,
    press_out,
    east,
    flow,
    press,
):
    group = lax.axis_index("group")
    tile = lax.axis_index("tile")
    half = courant_half(courant)
    rate = half * half
    stage(east_in, flow_in, press_in, east, flow, press, half)
    inner = range(OFF, OFF + 16)
    south = group == 0
    keep_low = jnp.where(tile == 0, 0.0, 1.0)
    turn = jnp.where(tile == n_tiles - 1, -1.0, 1.0)

    def border(slot, ref, sign):
        before, after = load_row(from_before, slot), load_row(from_after, slot)
        own_low, own_high = load_row(low_own, slot), load_row(high_own, slot)
        low, high = [], []
        for b, a, l, h in zip(before, after, own_low, own_high):
            low.append(keep_low * l + jnp.where(south, b, a))
            high.append(h + sign * jnp.where(south, a, b))
        store_row(ref, OFF - 1, low)
        store_row(ref, OFF + 16, high)

    def substep(step, carry):
        border(step, flow, turn)
        press_rows(inner, east, flow, press, rate)
        border(SUB + step, press, 1.0)
        east_rows(inner, east, press)
        flow_rows(inner, flow, press)
        return carry

    lax.fori_loop(0, SUB, substep, 0)
    inverse = 1.0 / half
    for row in inner:
        store_row(east, row, shifted(load_row(east, row), -1))
        store_row(press_out, row - OFF, [inverse * v for v in load_row(press, row)])
    for block in range(2):
        rows = pl.ds(8 * block, 8)
        source = pl.ds(OFF + 8 * block, 8)
        east_out[:, rows, :] = jnp.swapaxes(east[source], 0, 1)
        flow_out[:, rows, :] = jnp.swapaxes(flow[source], 0, 1)


def spread_kernel(press, heat_own, heat_back, out, heat_rows, sums):
    even_lane = lane_iota() % 2 == 0
    for source, part in enumerate((heat_own, heat_back)):
        width = part.shape[-1]
        heat_rows[:, :, pl.ds(source * width, width)] = jnp.swapaxes(part[...], 0, 1)
    for sublane in range(8):
        coarse = sublane // 2 + 4 * (sublane % 2)
        for block, value in enumerate(load_row(heat_rows, sublane)):
            left = jnp.where(even_lane, value, pltpu.roll(value, 1, 1))
            right = jnp.where(even_lane, pltpu.roll(value, LANES - 1, 1), value)
            for side, heat in enumerate((left, right)):
                cols = pl.ds((2 * block + side) * LANES, LANES)
                for row in (2 * coarse, 2 * coarse + 1):
                    sums[row, :, cols] = press[row, :, cols] + heat
    for block in range(2):
        rows = pl.ds(8 * block, 8)
        out[:, rows, :] = jnp.swapaxes(sums[rows], 0, 1)


def call(kernel, name, outs, n_smem, n_vmem, scratch=()):
    return pl.pallas_call(
        kernel,
        name=name,
        out_shape=[jax.ShapeDtypeStruct(s, F32) for s in outs],
        in_specs=[pl.BlockSpec(memory_space=SMEM)] * n_smem
        + [pl.BlockSpec(memory_space=VMEM)] * n_vmem,
        out_specs=[pl.BlockSpec(memory_space=VMEM)] * len(outs),
        scratch_shapes=[VMEM(s, F32) for s in scratch],
        cost_estimate=pl.CostEstimate(
            flops=10**7, bytes_accessed=10**7, transcendentals=0
        ),
    )


def shards(
    east_wind, equator_wind, pressure, moisture, albedo, courant, sun_angles, absorption, solar_weights
):
    east, flow, press, moist = east_wind[0], equator_wind[0], pressure[0], moisture[0]
    levels, rows, cols = east.shape
    n_tiles = lax.axis_size("tile")
    half_cols = cols // 4
    last = 2 * n_tiles - 1
    line = [t for t in range(n_tiles)] + [2 * n_tiles - 1 - t for t in range(n_tiles)]
    upward = [(line[i], line[i + 1]) for i in range(last)]
    downward = [(line[i + 1], line[i]) for i in range(last)]
    swap = [(0, 1), (1, 0)]

    coarse = (9, 8, half_cols)
    keep, send = call(coarsen_kernel, "coarsen", [coarse, coarse], 0, 2)(moist, albedo[0])
    other = lax.ppermute(send, "group", swap)

    series = (2 * SUB, 8, cols)
    work = [(rows + 2 * OFF, 8, cols)] * 3
    low, high, up, down = call(alone_kernel, "alone", [series] * 4, 1, 3, work)(
        courant, east, flow, press
    )
    from_before = lax.ppermute(up, ("group", "tile"), upward)
    from_after = lax.ppermute(down, ("group", "tile"), downward)

    heat = (8, 8, half_cols)
    heat_own, heat_other = call(
        functools.partial(radiate_kernel, n_tiles * rows // 2, cols // 2),
        "radiate",
        [heat, heat],
        3,
        2,
    )(sun_angles, absorption, solar_weights, keep, other)
    heat_back = lax.ppermute(heat_other, "group", swap)

    field = (levels, rows, cols)
    east, flow, press = call(
        functools.partial(joined_kernel, n_tiles),
        "joined",
        [field, field, (rows, 8, cols)],
        1,
        7,
        work,
    )(courant, east, flow, press, low, high, from_before, from_after)
    (press,) = call(
        spread_kernel, "spread", [field], 0, 3, [(8, 8, cols // 2), (rows, 8, cols)]
    )(press, heat_own, heat_back)
    return east[None], flow[None], press[None]


def solution(mesh):
    field = P("group", None, "tile", None)
    return jax.shard_map(
        shards,
        mesh=mesh,
        in_specs=(field,) * 4 + (P("group", "tile", None),) + (P(),) * 4,
        out_specs=(field,) * 3,
        check_vma=False,
    )
```

time: 342 us -> 59.9 us (0.18)
  starting transfers between devices: 128 us -> 11.1 us
  other arithmetic: 102 us -> 0 us
  local copies, waits for them, and re-layouts: 53.9 us -> 2.41 us
  waiting for transfers between devices: 48.5 us -> 9.85 us
  Pallas kernels: 0 us -> 35.1 us
  loops' own time: 5.49 us -> 0 us
    ppermute x36 -> x4, starting transfers between devices: 128 us -> 11.1 us  [the longest x1 5.43 us: shards(): other = lax.ppermute(send, 'group', swap)]
    reduce_sum x10 -> x0, other arithmetic: 79.6 us -> none  [the longest x1 46.7 us: shards(): moist_field.reshape(levels, half_rows, 2, half_cols, 2).mean(axis=(2, 4))]
    ppermute x36 -> x4, waiting for transfers between devices: 48.5 us -> 9.85 us  [the longest x1 9.85 us: shards(): other = lax.ppermute(send, 'group', swap)]
    pallas_call x0 -> x5, Pallas kernels: none -> 35.1 us  [the longest x1 11.3 us: shards(): call(functools.partial(radiate_kernel, n_tiles * rows // 2, cols // 2), '...]
    slice x57 -> x0, local copies, waits for them, and re-layouts: 12.7 us -> none  [the longest x10 5.68 us: shards(): jnp.roll(zonal_wind, 1, 2)]
    another operation x1 -> x0, local copies, waits for them, and re-layouts: 10.5 us -> none  [shards(): albedo[0].reshape(half_rows, 2, half_cols, 2).mean(axis=(1, 3))]
    sub x11 -> x0, other arithmetic: 9.65 us -> none  [the longest x6 6.89 us: shards(): zonal_wind - courant_col * (0.5 * (jnp.roll(press_field, -1, 2) - jnp.rol...]
    unnamed x24 -> x8, local copies, waits for them, and re-layouts: 11.1 us -> 2.41 us
  transfers between devices with their start and end apart: 36 -> 4, of which waited for: 11 -> 1; matrix products, arithmetic and copies ran while one was open for 40% -> 0% of each run, Pallas kernels for 0% -> 40%
where the time goes in v1:
time: 59.9 us; the launch traced here: 59.1 us
  Pallas kernels  35.1 us (59%)
  starting transfers between devices  11.1 us (19%)
  waiting for transfers between devices  9.85 us (16%)
  local copies, waits for them, and re-layouts  2.41 us (4%)
  between operations  0.68 us (1%)
    pallas_call x1, Pallas kernels, shards(): call(functools.partial(radiate_kernel, n_tiles * rows // 2, cols // 2), '...  11.3 us
    pallas_call x1, Pallas kernels, shards(): call(functools.partial(joined_kernel, n_tiles), 'joined', [field, field,...  10.1 us
    ppermute x1, waiting for transfers between devices, shards(): other = lax.ppermute(send, 'group', swap)  9.85 us
    pallas_call x1, Pallas kernels, shards(): call(alone_kernel, 'alone', [series] * 4, 1, 3, work)  8.71 us
    ppermute x1, starting transfers between devices, shards(): other = lax.ppermute(send, 'group', swap)  5.43 us
    ppermute x1, starting transfers between devices, shards(): from_before = lax.ppermute(up, ('group', 'tile'), upward)  3.7 us
    pallas_call x1, Pallas kernels, shards(): call(spread_kernel, 'spread', [field], 0, 3, [(8, 8, cols // 2), (rows, 8...  2.62 us
    unnamed x8, local copies, waits for them, and re-layouts  2.41 us
  transfers between devices with their start and end apart: 4, of which 1 were waited for; matrix products, arithmetic and copies ran while one was open for 0% of the time, Pallas kernels for 40%

profile of v1, /device:TPU:29, one launch (start us, length us, event | category | flops | bytes accessed | tf_op | source)
XLA Modules:
  0.0 59.1 jit_solution(1385938160184869020)
XLA Ops:
  0.6 8.7 %alone.1 = (f32[12,8,2048]{2,1,0:T(8,128)}, f32[12,8,2048]{2,1,0:T(8,128)}, f32[12,8,2048]{2,1,0:T(8,128)}, f32[12,8,2048]{2,1,0:T(8,128)}) custom-call(f32[8]{0:T(128)} %courant.3, f32[8,16,2048]{2,1,0:T(8,128)} %bitcast.8, f32[8,16,2048]{2,1,0:T(8,128)} %bitcast.10, f32[8,16,2048]{2,1,0:T(8,128)} %bitcast.12), custom_call_target="tpu_custom_call" | custom-call | flops 10000000 | bytes 10000000 | tf_op jit(solution)/shard_map/alone/pallas_call | solution.py:367
  9.3 3.7 %collective-permute-start = (f32[12,8,2048]{2,1,0:T(8,128)}, f32[12,8,2048]{2,1,0:T(8,128)S(1)}, u32[]{:S(2)}, u32[]{:S(2)}) collective-permute-start(f32[12,8,2048]{2,1,0:T(8,128)} %get-tuple-element.16), channel_id=1, source_target_pairs={{0,1},{1,2},{2,3},{3,4},{4,5},{5,6},{6,7},{7,8},{8,9},{9,10},{10,1... | collective-permute-start | bytes 2359304 | tf_op jit(solution)/shard_map/ppermute | solution.py:370
  13.0 1.9 %collective-permute-start.1 = (f32[12,8,2048]{2,1,0:T(8,128)}, f32[12,8,2048]{2,1,0:T(8,128)S(1)}, u32[]{:S(2)}, u32[]{:S(2)}) collective-permute-start(f32[12,8,2048]{2,1,0:T(8,128)} %get-tuple-element.17), channel_id=1, source_target_pairs={{1,0},{2,1},{3,2},{4,3},{5,4},{6,5},{7,6},{8,7},{9,8},{10,9},{11,1... | collective-permute-start | bytes 2359304 | tf_op jit(solution)/shard_map/ppermute | solution.py:371
  15.0 2.3 %coarsen.1 = (f32[9,8,512]{2,1,0:T(8,128)}, f32[9,8,512]{2,1,0:T(8,128)}) custom-call(f32[8,16,2048]{2,1,0:T(8,128)} %bitcast.14, f32[16,2048]{1,0:T(8,128)} %bitcast.16), custom_call_target="tpu_custom_call" | custom-call | flops 10000000 | bytes 10000000 | tf_op jit(solution)/shard_map/coarsen/pallas_call | solution.py:362
  17.3 5.4 %collective-permute-start.2 = (f32[9,8,512]{2,1,0:T(8,128)}, f32[9,8,512]{2,1,0:T(8,128)S(1)}, u32[]{:S(2)}, u32[]{:S(2)}) collective-permute-start(f32[9,8,512]{2,1,0:T(8,128)} %get-tuple-element.22), channel_id=1, source_target_pairs={{0,64},{64,0},{1,65},{65,1},{2,66},{66,2},{3,67},{67,3},{4,68},{68... | collective-permute-start | bytes 442376 | tf_op jit(solution)/shard_map/ppermute | solution.py:363
  22.7 9.8 %collective-permute-done.2.other = f32[9,8,512]{2,1,0:T(8,128)S(1)} collective-permute-done((f32[9,8,512]{2,1,0:T(8,128)}, f32[9,8,512]{2,1,0:T(8,128)S(1)}, u32[]{:S(2)}, u32[]{:S(2)}) %collective-permute-start.2) | collective-permute-done | bytes 147488 | tf_op jit(solution)/shard_map/ppermute | solution.py:363
  32.5 0.0 copy-start.2
  32.5 0.6 %copy-done.2 = f32[9,8,512]{2,1,0:T(8,128)} copy-done((f32[9,8,512]{2,1,0:T(8,128)}, f32[9,8,512]{2,1,0:T(8,128)S(1)}, u32[]{:S(2)}) %copy-start.2) | copy-done | bytes 147480
  33.2 11.3 %radiate.1 = (f32[8,8,512]{2,1,0:T(8,128)}, f32[8,8,512]{2,1,0:T(8,128)}) custom-call(f32[2]{0:T(128)} %sun.1, f32[256]{0:T(256)} %absorption.1, f32[256]{0:T(256)} %weights.1, f32[9,8,512]{2,1,0:T(8,128)} %get-tuple-element.21.own, f32[9,8,512]{2,1,0:T(8,128)} %copy-done.2), custom_call_target="tpu_custom_call" | custom-call | flops 10000000 | bytes 10000000 | tf_op jit(solution)/shard_map/radiate/pallas_call | solution.py:374
  44.5 0.0 collective-permute-start.3
  44.5 0.0 collective-permute-done.from_before
  44.5 0.0 copy-start
  44.6 0.0 collective-permute-done.1.from_after
  44.6 0.0 copy-start.1
  44.6 0.9 %copy-done = f32[12,8,2048]{2,1,0:T(8,128)} copy-done((f32[12,8,2048]{2,1,0:T(8,128)}, f32[12,8,2048]{2,1,0:T(8,128)S(1)}, u32[]{:S(2)}) %copy-start) | copy-done | bytes 786456
  45.4 0.3 copy-done.1
  45.7 10.1 %joined.1 = (f32[8,16,2048]{2,1,0:T(8,128)}, f32[8,16,2048]{2,1,0:T(8,128)}, f32[16,8,2048]{2,1,0:T(8,128)}) custom-call(f32[8]{0:T(128)} %courant.3, f32[8,16,2048]{2,1,0:T(8,128)} %bitcast.9, f32[8,16,2048]{2,1,0:T(8,128)} %bitcast.11, f32[8,16,2048]{2,1,0:T(8,128)} %bitcast.13, f32[12,8,2048]{2,1,0:T(8,128)} %get-tuple-element.14.low_own, ...), custom_call_target="tpu_custom_call" | custom-call | flops 10000000 | bytes 10000000 | tf_op jit(solution)/shard_map/joined/pallas_call | solution.py:384
  55.8 0.0 collective-permute-done.3.heat_back
  55.8 0.0 copy-start.3
  55.8 0.6 %copy-done.3 = f32[8,8,512]{2,1,0:T(8,128)} copy-done((f32[8,8,512]{2,1,0:T(8,128)}, f32[8,8,512]{2,1,0:T(8,128)S(1)}, u32[]{:S(2)}) %copy-start.3) | copy-done | bytes 131096
  56.4 2.6 %spread.1 = f32[8,16,2048]{2,1,0:T(8,128)} custom-call(f32[16,8,2048]{2,1,0:T(8,128)} %get-tuple-element.20.press, f32[8,8,512]{2,1,0:T(8,128)} %get-tuple-element.23.heat_own, f32[8,8,512]{2,1,0:T(8,128)} %copy-done.3), custom_call_target="tpu_custom_call" | custom-call | flops 10000000 | bytes 10000000 | tf_op jit(solution)/shard_map/spread/pallas_call | solution.py:392
Async XLA Ops:
  9.3 35.2 %collective-permute-start = (f32[12,8,2048]{2,1,0:T(8,128)}, f32[12,8,2048]{2,1,0:T(8,128)S(1)}, u32[]{:S(2)}, u32[]{:S(2)}) collective-permute-start(f32[12,8,2048]{2,1,0:T(8,128)} %get-tuple-element.16), channel_id=1, source_target_pairs={{0,1},{1,2},{2,3},{3,4},{4,5},{5,6},{6,7},{7,8},{8,9},{9,10},{10,1... | collective-permute-start | bytes 2359304 | tf_op jit(solution)/shard_map/ppermute | solution.py:370
  13.0 31.5 %collective-permute-start.1 = (f32[12,8,2048]{2,1,0:T(8,128)}, f32[12,8,2048]{2,1,0:T(8,128)S(1)}, u32[]{:S(2)}, u32[]{:S(2)}) collective-permute-start(f32[12,8,2048]{2,1,0:T(8,128)} %get-tuple-element.17), channel_id=1, source_target_pairs={{1,0},{2,1},{3,2},{4,3},{5,4},{6,5},{7,6},{8,7},{9,8},{10,9},{11,1... | collective-permute-start | bytes 2359304 | tf_op jit(solution)/shard_map/ppermute | solution.py:371
  17.3 15.3 %collective-permute-start.2 = (f32[9,8,512]{2,1,0:T(8,128)}, f32[9,8,512]{2,1,0:T(8,128)S(1)}, u32[]{:S(2)}, u32[]{:S(2)}) collective-permute-start(f32[9,8,512]{2,1,0:T(8,128)} %get-tuple-element.22), channel_id=1, source_target_pairs={{0,64},{64,0},{1,65},{65,1},{2,66},{66,2},{3,67},{67,3},{4,68},{68... | collective-permute-start | bytes 442376 | tf_op jit(solution)/shard_map/ppermute | solution.py:363
  32.5 0.6 %copy-start.2 = (f32[9,8,512]{2,1,0:T(8,128)}, f32[9,8,512]{2,1,0:T(8,128)S(1)}, u32[]{:S(2)}) copy-start(f32[9,8,512]{2,1,0:T(8,128)S(1)} %collective-permute-done.2.other) | copy-start | bytes 442372
  44.5 11.2 %collective-permute-start.3 = (f32[8,8,512]{2,1,0:T(8,128)}, f32[8,8,512]{2,1,0:T(8,128)S(1)}, u32[]{:S(2)}, u32[]{:S(2)}) collective-permute-start(f32[8,8,512]{2,1,0:T(8,128)} %get-tuple-element.24), channel_id=1, source_target_pairs={{0,64},{64,0},{1,65},{65,1},{2,66},{66,2},{3,67},{67,3},{4,68},{68... | collective-permute-start | bytes 393224 | tf_op jit(solution)/shard_map/ppermute | solution.py:381
  44.5 0.9 %copy-start = (f32[12,8,2048]{2,1,0:T(8,128)}, f32[12,8,2048]{2,1,0:T(8,128)S(1)}, u32[]{:S(2)}) copy-start(f32[12,8,2048]{2,1,0:T(8,128)S(1)} %collective-permute-done.from_before) | copy-start | bytes 2359300
  44.6 1.1 %copy-start.1 = (f32[12,8,2048]{2,1,0:T(8,128)}, f32[12,8,2048]{2,1,0:T(8,128)S(1)}, u32[]{:S(2)}) copy-start(f32[12,8,2048]{2,1,0:T(8,128)S(1)} %collective-permute-done.1.from_after) | copy-start | bytes 2359300
  55.8 0.6 %copy-start.3 = (f32[8,8,512]{2,1,0:T(8,128)}, f32[8,8,512]{2,1,0:T(8,128)S(1)}, u32[]{:S(2)}) copy-start(f32[8,8,512]{2,1,0:T(8,128)S(1)} %collective-permute-done.3.heat_back) | copy-start | bytes 393220

commit v2 on v1

--- a/solution.py
+++ b/solution.py
@@ -7,6 +7,7 @@
 from jax.experimental import pallas as pl
 from jax.experimental.pallas import tpu as pltpu
 from jax.sharding import PartitionSpec as P
+
 
 SUB = 6
 HEAT_SCALE = 10.0
@@ -146,51 +147,55 @@
     return [jnp.where(edge, turned[j - 1], turned[j]) for j in range(count)]
 
 
-def stage(east_in, flow_in, press_in, east, flow, press, half):
-    for block in range(2):
-        rows = pl.ds(8 * block, 8)
-        inner = pl.ds(OFF + 8 * block, 8)
-        flow[inner] = jnp.swapaxes(flow_in[:, rows, :], 0, 1)
-        east[inner] = jnp.swapaxes(east_in[:, rows, :], 0, 1)
-        press[inner] = jnp.swapaxes(press_in[:, rows, :], 0, 1)
-    for row in range(OFF, OFF + 16):
-        store_row(east, row, shifted(load_row(east, row), 1))
-        store_row(press, row, [half * v for v in load_row(press, row)])
-
-
-def press_rows(rows, east, flow, press, rate):
-    for row in rows:
-        here = load_row(east, row)
-        back = shifted(here, -2)
-        ahead, behind = load_row(flow, row + 1), load_row(flow, row - 1)
-        old = load_row(press, row)
-        store_row(
-            press,
-            row,
-            [
-                p - rate * ((e - b) + (n - s))
-                for p, e, b, n, s in zip(old, here, back, ahead, behind)
-            ],
-        )
-
-
-def east_rows(rows, east, press):
-    for row in rows:
-        here = load_row(press, row)
-        ahead = shifted(here, 2)
-        old = load_row(east, row)
-        store_row(east, row, [e - (a - p) for e, a, p in zip(old, ahead, here)])
-
-
-def flow_rows(rows, flow, press):
-    for row in rows:
-        ahead, behind = load_row(press, row + 1), load_row(press, row - 1)
-        old = load_row(flow, row)
-        store_row(flow, row, [q - (n - s) for q, n, s in zip(old, ahead, behind)])
+def plus(values, others, sign=1.0):
+    if others is None:
+        return values
+    if values is None:
+        return others if sign > 0 else [-o for o in others]
+    if sign > 0:
+        return [v + o for v, o in zip(values, others)]
+    return [v - o for v, o in zip(values, others)]
+
+
+class Rows:
+    def __init__(self, ref, first, rows=()):
+        self.ref, self.first, self.known = ref, first, dict.fromkeys(rows)
+
+    def get(self, row):
+        if row not in self.known:
+            return None
+        if self.known[row] is not None:
+            return self.known[row]
+        return load_row(self.ref, row - self.first)
+
+    def put(self, row, values):
+        store_row(self.ref, row - self.first, values)
+        self.known[row] = None
+
+
+def substep(old, new, press_rows, flow_rows, east_rows, rate):
+    east, flow, press = old
+    new_east, new_flow, new_press = new
+    every = sorted(set(press_rows) | {r + 1 for r in flow_rows} | {r + 2 for r in east_rows})
+    for row in every:
+        if row in press_rows:
+            change = plus(flow.get(row + 1), flow.get(row - 1), -1.0)
+            here = east.get(row)
+            if here is not None:
+                change = plus([e - b for e, b in zip(here, shifted(here, -2))], change)
+            change = [rate * c for c in change]
+            new_press.put(row, plus(press.get(row), change, -1.0))
+        if row - 1 in flow_rows:
+            slope = plus(new_press.get(row), new_press.get(row - 2), -1.0)
+            new_flow.put(row - 1, plus(flow.get(row - 1), slope, -1.0))
+        if row - 2 in east_rows:
+            here = new_press.get(row - 2)
+            slope = [a - p for a, p in zip(shifted(here, 2), here)]
+            new_east.put(row - 2, plus(east.get(row - 2), slope, -1.0))
 
 
 def spans(*pairs):
-    return [OFF + row for low, high in pairs for row in range(low, high + 1)]
+    return [row for low, high in pairs for row in range(low, high + 1)]
 
 
 PRESS_SPANS = [
@@ -207,6 +212,7 @@
     spans((-5, 4), (11, 20)),
     spans((-3, 2), (13, 18)),
     spans((-1, 0), (15, 16)),
+    [],
 ]
 FLOW_SPANS = [
     spans((-2, 17)),
@@ -214,56 +220,77 @@
     spans((-6, 5), (10, 21)),
     spans((-4, 3), (12, 19)),
     spans((-2, 1), (14, 17)),
+    [],
 ]
 
 
 def alone_kernel(
-    courant, east_in, flow_in, press_in, low_out, high_out, up, down, east, flow, press
-):
-    group = lax.axis_index("group")
-    half = courant_half(courant)
-    rate = half * half
-    zero = jnp.zeros((8, LANES), F32)
-    count = east.shape[-1] // LANES
-    for row in spans((-8, -1), (16, 23)):
-        for ref in (east, flow, press):
-            store_row(ref, row, [zero] * count)
-    stage(east_in, flow_in, press_in, east, flow, press, half)
-
-    def record(slot, ref):
-        store_row(low_out, slot, load_row(ref, OFF - 1))
-        store_row(high_out, slot, load_row(ref, OFF + 16))
-        first, last = load_row(ref, OFF), load_row(ref, OFF + 15)
-
-        @pl.when(group == 0)
-        def _():
-            store_row(up, slot, last)
-            store_row(down, slot, first)
-
-        @pl.when(group != 0)
-        def _():
-            store_row(up, slot, first)
-            store_row(down, slot, last)
-
-    for step in range(SUB):
-        record(step, flow)
-        press_rows(PRESS_SPANS[step], east, flow, press, rate)
-        record(SUB + step, press)
-        if step < SUB - 1:
-            east_rows(EAST_SPANS[step], east, press)
-            flow_rows(FLOW_SPANS[step], flow, press)
-
-
-def joined_kernel(
-    n_tiles,
     courant,
     east_in,
     flow_in,
     press_in,
+    east_0,
+    flow_0,
+    press_0,
+    low_out,
+    high_out,
+    mate,
+    far,
+    east,
+    flow,
+    press,
+):
+    even = lax.axis_index("tile") % 2 == 0
+    half = courant_half(courant)
+    rate = half * half
+    count = east.shape[-1] // LANES
+    for block in range(2):
+        rows = pl.ds(8 * block, 8)
+        flow_0[rows] = jnp.swapaxes(flow_in[:, rows, :], 0, 1)
+        east_0[rows] = jnp.swapaxes(east_in[:, rows, :], 0, 1)
+        press_0[rows] = jnp.swapaxes(press_in[:, rows, :], 0, 1)
+    inner = range(16)
+    for row in inner:
+        store_row(east_0, row, shifted(load_row(east_0, row), 1))
+        store_row(press_0, row, [half * v for v in load_row(press_0, row)])
+
+    def record(slot, rows):
+        low, first, last, high = [rows.get(r) for r in (-1, 0, 15, 16)]
+        zero = [jnp.zeros((8, LANES), F32)] * count
+        store_row(low_out, slot, low or zero)
+        store_row(high_out, slot, high or zero)
+
+        @pl.when(even)
+        def _():
+            store_row(mate, slot, last)
+            store_row(far, slot, first)
+
+        @pl.when(jnp.logical_not(even))
+        def _():
+            store_row(mate, slot, first)
+            store_row(far, slot, last)
+
+    state = [Rows(ref, 0, inner) for ref in (east_0, flow_0, press_0)]
+    work = [Rows(ref, -OFF) for ref in (east, flow, press)]
+    for step in range(SUB):
+        record(step, state[1])
+        substep(
+            state, work, PRESS_SPANS[step], FLOW_SPANS[step], EAST_SPANS[step], rate
+        )
+        state = work
+        record(SUB + step, state[2])
+
+
+def joined_kernel(
+    n_tiles,
+    courant,
+    east_0,
+    flow_0,
+    press_0,
     low_own,
     high_own,
-    from_before,
-    from_after,
+    from_mate,
+    from_far,
     east_out,
     flow_out,
     press_out,
@@ -271,44 +298,39 @@
     flow,
     press,
 ):
-    group = lax.axis_index("group")
     tile = lax.axis_index("tile")
+    even = tile % 2 == 0
     half = courant_half(courant)
     rate = half * half
-    stage(east_in, flow_in, press_in, east, flow, press, half)
-    inner = range(OFF, OFF + 16)
-    south = group == 0
+    inner = range(16)
     keep_low = jnp.where(tile == 0, 0.0, 1.0)
     turn = jnp.where(tile == n_tiles - 1, -1.0, 1.0)
 
-    def border(slot, ref, sign):
-        before, after = load_row(from_before, slot), load_row(from_after, slot)
+    def border(slot, rows, sign):
+        mate, far = load_row(from_mate, slot), load_row(from_far, slot)
         own_low, own_high = load_row(low_own, slot), load_row(high_own, slot)
-        low, high = [], []
-        for b, a, l, h in zip(before, after, own_low, own_high):
-            low.append(keep_low * l + jnp.where(south, b, a))
-            high.append(h + sign * jnp.where(south, a, b))
-        store_row(ref, OFF - 1, low)
-        store_row(ref, OFF + 16, high)
-
-    def substep(step, carry):
-        border(step, flow, turn)
-        press_rows(inner, east, flow, press, rate)
-        border(SUB + step, press, 1.0)
-        east_rows(inner, east, press)
-        flow_rows(inner, flow, press)
-        return carry
-
-    lax.fori_loop(0, SUB, substep, 0)
+        rows.known[-1] = [
+            keep_low * o + jnp.where(even, f, m) for o, m, f in zip(own_low, mate, far)
+        ]
+        rows.known[16] = [
+            o + sign * jnp.where(even, m, f) for o, m, f in zip(own_high, mate, far)
+        ]
+
+    state = [Rows(ref, 0, inner) for ref in (east_0, flow_0, press_0)]
+    work = [Rows(ref, 0) for ref in (east, flow, press)]
+    for step in range(SUB):
+        border(step, state[1], turn)
+        border(SUB + step, work[2], 1.0)
+        substep(state, work, inner, inner, inner, rate)
+        state = work
     inverse = 1.0 / half
     for row in inner:
         store_row(east, row, shifted(load_row(east, row), -1))
-        store_row(press_out, row - OFF, [inverse * v for v in load_row(press, row)])
+        store_row(press_out, row, [inverse * v for v in load_row(press, row)])
     for block in range(2):
         rows = pl.ds(8 * block, 8)
-        source = pl.ds(OFF + 8 * block, 8)
-        east_out[:, rows, :] = jnp.swapaxes(east[source], 0, 1)
-        flow_out[:, rows, :] = jnp.swapaxes(flow[source], 0, 1)
+        east_out[:, rows, :] = jnp.swapaxes(east[rows], 0, 1)
+        flow_out[:, rows, :] = jnp.swapaxes(flow[rows], 0, 1)
 
 
 def spread_kernel(press, heat_own, heat_back, out, heat_rows, sums):
@@ -330,15 +352,15 @@
         out[:, rows, :] = jnp.swapaxes(sums[rows], 0, 1)
 
 
-def call(kernel, name, outs, n_smem, n_vmem, scratch=()):
+def call(kernel, outs, n_smem, n_vmem, scratch=(), limit=16):
     return pl.pallas_call(
         kernel,
-        name=name,
         out_shape=[jax.ShapeDtypeStruct(s, F32) for s in outs],
         in_specs=[pl.BlockSpec(memory_space=SMEM)] * n_smem
         + [pl.BlockSpec(memory_space=VMEM)] * n_vmem,
         out_specs=[pl.BlockSpec(memory_space=VMEM)] * len(outs),
         scratch_shapes=[VMEM(s, F32) for s in scratch],
+        compiler_params=pltpu.CompilerParams(vmem_limit_bytes=limit << 20),
         cost_estimate=pl.CostEstimate(
             flops=10**7, bytes_accessed=10**7, transcendentals=0
         ),
@@ -352,28 +374,36 @@
     levels, rows, cols = east.shape
     n_tiles = lax.axis_size("tile")
     half_cols = cols // 4
-    last = 2 * n_tiles - 1
-    line = [t for t in range(n_tiles)] + [2 * n_tiles - 1 - t for t in range(n_tiles)]
-    upward = [(line[i], line[i + 1]) for i in range(last)]
-    downward = [(line[i + 1], line[i]) for i in range(last)]
     swap = [(0, 1), (1, 0)]
 
+    def both_ways(pairs):
+        return [pair for a, b in pairs for pair in ((a, b), (b, a))]
+
+    mates = both_ways((t, t + 1) for t in range(0, n_tiles, 2))
+    fars = both_ways(
+        [
+            (g * n_tiles + t, g * n_tiles + t + 1)
+            for g in range(2)
+            for t in range(1, n_tiles - 1, 2)
+        ]
+        + [(n_tiles - 1, 2 * n_tiles - 1)]
+    )
+
     coarse = (9, 8, half_cols)
-    keep, send = call(coarsen_kernel, "coarsen", [coarse, coarse], 0, 2)(moist, albedo[0])
+    keep, send = call(coarsen_kernel, [coarse, coarse], 0, 2)(moist, albedo[0])
     other = lax.ppermute(send, "group", swap)
 
     series = (2 * SUB, 8, cols)
-    work = [(rows + 2 * OFF, 8, cols)] * 3
-    low, high, up, down = call(alone_kernel, "alone", [series] * 4, 1, 3, work)(
-        courant, east, flow, press
-    )
-    from_before = lax.ppermute(up, ("group", "tile"), upward)
-    from_after = lax.ppermute(down, ("group", "tile"), downward)
+    staged = (rows, 8, cols)
+    east, flow, press, low, high, mate, far = call(
+        alone_kernel, [staged] * 3 + [series] * 4, 1, 3, [(rows + 2 * OFF, 8, cols)] * 3
+    )(courant, east, flow, press)
+    from_far = lax.ppermute(far, ("group", "tile"), fars)
+    from_mate = lax.ppermute(mate, "tile", mates)
 
     heat = (8, 8, half_cols)
     heat_own, heat_other = call(
         functools.partial(radiate_kernel, n_tiles * rows // 2, cols // 2),
-        "radiate",
         [heat, heat],
         3,
         2,
@@ -383,14 +413,13 @@
     field = (levels, rows, cols)
     east, flow, press = call(
         functools.partial(joined_kernel, n_tiles),
-        "joined",
-        [field, field, (rows, 8, cols)],
+        [field, field, staged],
         1,
         7,
-        work,
-    )(courant, east, flow, press, low, high, from_before, from_after)
+        [staged] * 3,
+    )(courant, east, flow, press, low, high, from_mate, from_far)
     (press,) = call(
-        spread_kernel, "spread", [field], 0, 3, [(8, 8, cols // 2), (rows, 8, cols)]
+        spread_kernel, [field], 0, 3, [(8, 8, cols // 2), staged]
     )(press, heat_own, heat_back)
     return east[None], flow[None], press[None]
 

time: 59.9 us -> 49.1 us (0.82)
  the two profiles are of different devices: /device:TPU:29 before, /device:TPU:96 now
where the time goes in v2:
time: 49.1 us; the launch traced here: 48.9 us
  Pallas kernels  23 us (47%)
  waiting for transfers between devices  11 us (22%)
  starting transfers between devices  9.76 us (20%)
  local copies, waits for them, and re-layouts  4.35 us (9%)
  between operations  0.73 us (1%)
    ppermute x1, waiting for transfers between devices, shards(): other = lax.ppermute(send, 'group', swap)  11 us
    pallas_call x1, Pallas kernels, shards(): call(functools.partial(radiate_kernel, n_tiles * rows // 2, cols // 2), [...  10.2 us
    ppermute x1, starting transfers between devices, shards(): from_far = lax.ppermute(far, ('group', 'tile'), fars)  7.31 us
    pallas_call x1, Pallas kernels, shards(): call(functools.partial(joined_kernel, n_tiles), [field, field, staged], 1...  6.04 us
    pallas_call x1, Pallas kernels, shards(): call(alone_kernel, [staged] * 3 + [series] * 4, 1, 3, [(rows + 2 * OFF, 8...  5.08 us
    unnamed x18, local copies, waits for them, and re-layouts  4.35 us
    ppermute x1, starting transfers between devices, shards(): heat_back = lax.ppermute(heat_other, 'group', swap)  1.69 us
    pallas_call x1, Pallas kernels, shards(): call(spread_kernel, [field], 0, 3, [(8, 8, cols // 2), staged])  1.33 us
  transfers between devices with their start and end apart: 4, of which 1 were waited for; matrix products, arithmetic and copies ran while one was open for 0% of the time, Pallas kernels for 34%

profile of v2, /device:TPU:96, one launch (start us, length us, event | category | flops | bytes accessed | tf_op | source)
XLA Modules:
  0.0 48.9 jit_solution(263298145430501214)
XLA Ops:
  0.6 0.0 copy-start.5
  0.6 0.6 %copy-done.5 = f32[8]{0:T(128)S(1)} copy-done((f32[8]{0:T(128)S(1)}, f32[8]{0:T(128)}, u32[]{:S(2)}) %copy-start.5) | copy-done | bytes 56
  1.3 1.2 %copy-done.1 = f32[1,8,16,2048]{3,2,1,0:T(8,128)S(1)} copy-done((f32[1,8,16,2048]{3,2,1,0:T(8,128)S(1)}, f32[1,8,16,2048]{3,2,1,0:T(8,128)}, u32[]{:S(2)}) %copy-start.1) | copy-done | bytes 1048600
  2.5 1.2 %copy-done.2 = f32[1,8,16,2048]{3,2,1,0:T(8,128)S(1)} copy-done((f32[1,8,16,2048]{3,2,1,0:T(8,128)S(1)}, f32[1,8,16,2048]{3,2,1,0:T(8,128)}, u32[]{:S(2)}) %copy-start.2) | copy-done | bytes 1048600
  3.7 1.2 %copy-done.3 = f32[1,8,16,2048]{3,2,1,0:T(8,128)S(1)} copy-done((f32[1,8,16,2048]{3,2,1,0:T(8,128)S(1)}, f32[1,8,16,2048]{3,2,1,0:T(8,128)}, u32[]{:S(2)}) %copy-start.3) | copy-done | bytes 1048600
  5.0 5.1 %shard_map.112 = (f32[16,8,2048]{2,1,0:T(8,128)S(1)}, f32[16,8,2048]{2,1,0:T(8,128)S(1)}, f32[16,8,2048]{2,1,0:T(8,128)S(1)}, f32[12,8,2048]{2,1,0:T(8,128)S(1)}...) custom-call(f32[8]{0:T(128)S(1)} %copy-done.5, f32[8,16,2048]{2,1,0:T(8,128)S(1)} %bitcast.9, ...), custom_call_target="tpu_custom_call" | custom-call | flops 10000000 | bytes 10000000 | tf_op jit(solution)/shard_map/pallas_call | solution.py:398
  10.1 0.1 collective-permute-start
  10.1 7.3 %collective-permute-start.1 = (f32[12,8,2048]{2,1,0:T(8,128)S(1)}, f32[12,8,2048]{2,1,0:T(8,128)S(1)}, u32[]{:S(2)}, u32[]{:S(2)}) collective-permute-start(f32[12,8,2048]{2,1,0:T(8,128)S(1)} %get-tuple-element.23), channel_id=1, source_target_pairs={{1,2},{2,1},{3,4},{4,3},{5,6},{6,5},{7,8},{8,7},{9,10},{10,9},{11,... | collective-permute-start | bytes 2359304 | tf_op jit(solution)/shard_map/ppermute | solution.py:401
  17.5 0.0 copy-done
  17.5 0.0 copy-done.4
  17.5 0.4 shard_map.114
  17.9 0.0 copy-start.7
  17.9 0.0 copy-start.6
  17.9 0.0 copy-start.8
  17.9 0.7 %collective-permute-start.2 = (f32[9,8,512]{2,1,0:T(8,128)S(1)}, f32[9,8,512]{2,1,0:T(8,128)S(1)}, u32[]{:S(2)}, u32[]{:S(2)}) collective-permute-start(f32[9,8,512]{2,1,0:T(8,128)S(1)} %get-tuple-element.28), channel_id=1, source_target_pairs={{0,64},{64,0},{1,65},{65,1},{2,66},{66,2},{3,67},{67,3},{4,68},{68... | collective-permute-start | bytes 442376 | tf_op jit(solution)/shard_map/ppermute | solution.py:394
  18.6 11.0 %collective-permute-done.2.other = f32[9,8,512]{2,1,0:T(8,128)S(1)} collective-permute-done((f32[9,8,512]{2,1,0:T(8,128)S(1)}, f32[9,8,512]{2,1,0:T(8,128)S(1)}, u32[]{:S(2)}, u32[]{:S(2)}) %collective-permute-start.2) | collective-permute-done | bytes 147488 | tf_op jit(solution)/shard_map/ppermute | solution.py:394
  29.6 0.0 copy-done.8
  29.6 10.2 %shard_map.115 = (f32[8,8,512]{2,1,0:T(8,128)S(1)}, f32[8,8,512]{2,1,0:T(8,128)S(1)}) custom-call(f32[2]{0:T(128)S(1)} %copy-done.8, f32[256]{0:T(256)S(1)} %copy-done.6, f32[256]{0:T(256)S(1)} %copy-done.7, f32[9,8,512]{2,1,0:T(8,128)S(1)} %get-tuple-element.27.own, f32[9,8,512]{2,1,0:T(8,128)S(1)} %collective-permute-done.2.other), custom_call_target="tpu_custom_call" | custom-call | flops 10000000 | bytes 10000000 | tf_op jit(solution)/shard_map/pallas_call | solution.py:405
  39.8 1.7 %collective-permute-start.3 = (f32[8,8,512]{2,1,0:T(8,128)S(1)}, f32[8,8,512]{2,1,0:T(8,128)S(1)}, u32[]{:S(2)}, u32[]{:S(2)}) collective-permute-start(f32[8,8,512]{2,1,0:T(8,128)S(1)} %get-tuple-element.30), channel_id=1, source_target_pairs={{0,64},{64,0},{1,65},{65,1},{2,66},{66,2},{3,67},{67,3},{4,68},{68... | collective-permute-start | bytes 393224 | tf_op jit(solution)/shard_map/ppermute | solution.py:411
  41.5 0.0 collective-permute-done.from_mate
  41.5 0.0 collective-permute-done.1.from_far
  41.5 6.0 %shard_map.113 = (f32[8,16,2048]{2,1,0:T(8,128)}, f32[8,16,2048]{2,1,0:T(8,128)}, f32[16,8,2048]{2,1,0:T(8,128)S(1)}) custom-call(f32[8]{0:T(128)S(1)} %copy-done.5, f32[16,8,2048]{2,1,0:T(8,128)S(1)} %get-tuple-element.17.east_0, f32[16,8,2048]{2,1,0:T(8,128)S(1)} %get-tuple-element.18.flow_0, f32[16,8,2048]{2,1,0:T(8,128)S(1)} %get-tuple-element.19.press_0, ...), custom_call_target="tpu_custom_call" | custom-call | flops 10000000 | bytes 10000000 | tf_op jit(solution)/shard_map/pallas_call | solution.py:414
  47.5 0.0 collective-permute-done.3.heat_back
  47.5 1.3 %shard_map.116 = f32[8,16,2048]{2,1,0:T(8,128)} custom-call(f32[16,8,2048]{2,1,0:T(8,128)S(1)} %get-tuple-element.26.press, f32[8,8,512]{2,1,0:T(8,128)S(1)} %get-tuple-element.29.heat_own, f32[8,8,512]{2,1,0:T(8,128)S(1)} %collective-permute-done.3.heat_back), custom_call_target="tpu_custom_call" | custom-call | flops 10000000 | bytes 10000000 | tf_op jit(solution)/shard_map/pallas_call | solution.py:421
  (7 shorter events, 0.0 us)
Async XLA Ops:
  0.6 0.7 %copy-start.5 = (f32[8]{0:T(128)S(1)}, f32[8]{0:T(128)}, u32[]{:S(2)}) copy-start(f32[8]{0:T(128)} %courant.3) | copy-start | bytes 100
  1.3 1.2 %copy-start.1 = (f32[1,8,16,2048]{3,2,1,0:T(8,128)S(1)}, f32[1,8,16,2048]{3,2,1,0:T(8,128)}, u32[]{:S(2)}) copy-start(f32[1,8,16,2048]{3,2,1,0:T(8,128)} %param.9) | copy-start | bytes 3145732
  2.5 1.2 %copy-start.2 = (f32[1,8,16,2048]{3,2,1,0:T(8,128)S(1)}, f32[1,8,16,2048]{3,2,1,0:T(8,128)}, u32[]{:S(2)}) copy-start(f32[1,8,16,2048]{3,2,1,0:T(8,128)} %param.10) | copy-start | bytes 3145732
  3.7 1.2 %copy-start.3 = (f32[1,8,16,2048]{3,2,1,0:T(8,128)S(1)}, f32[1,8,16,2048]{3,2,1,0:T(8,128)}, u32[]{:S(2)}) copy-start(f32[1,8,16,2048]{3,2,1,0:T(8,128)} %param.11) | copy-start | bytes 3145732
  5.0 12.5 %copy-start = (f32[1,8,16,2048]{3,2,1,0:T(8,128)S(1)}, f32[1,8,16,2048]{3,2,1,0:T(8,128)}, u32[]{:S(2)}) copy-start(f32[1,8,16,2048]{3,2,1,0:T(8,128)} %param.12) | copy-start | bytes 3145732
  5.0 12.5 %copy-start.4 = (f32[1,16,2048]{2,1,0:T(8,128)S(1)}, f32[1,16,2048]{2,1,0:T(8,128)}, u32[]{:S(2)}) copy-start(f32[1,16,2048]{2,1,0:T(8,128)} %param.13) | copy-start | bytes 393220
  10.1 31.4 %collective-permute-start = (f32[12,8,2048]{2,1,0:T(8,128)S(1)}, f32[12,8,2048]{2,1,0:T(8,128)S(1)}, u32[]{:S(2)}, u32[]{:S(2)}) collective-permute-start(f32[12,8,2048]{2,1,0:T(8,128)S(1)} %get-tuple-element.22), channel_id=1, source_target_pairs={{0,1},{1,0},{2,3},{3,2},{4,5},{5,4},{6,7},{7,6},{8,9},{9,8},{10,11... | collective-permute-start | bytes 2359304 | tf_op jit(solution)/shard_map/ppermute | solution.py:402
  10.1 31.3 %collective-permute-start.1 = (f32[12,8,2048]{2,1,0:T(8,128)S(1)}, f32[12,8,2048]{2,1,0:T(8,128)S(1)}, u32[]{:S(2)}, u32[]{:S(2)}) collective-permute-start(f32[12,8,2048]{2,1,0:T(8,128)S(1)} %get-tuple-element.23), channel_id=1, source_target_pairs={{1,2},{2,1},{3,4},{4,3},{5,6},{6,5},{7,8},{8,7},{9,10},{10,9},{11,... | collective-permute-start | bytes 2359304 | tf_op jit(solution)/shard_map/ppermute | solution.py:401
  17.9 11.7 %copy-start.7 = (f32[256]{0:T(256)S(1)}, f32[256]{0:T(256)}, u32[]{:S(2)}) copy-start(f32[256]{0:T(256)} %weights.1) | copy-start | bytes 3076
  17.9 11.7 %copy-start.6 = (f32[256]{0:T(256)S(1)}, f32[256]{0:T(256)}, u32[]{:S(2)}) copy-start(f32[256]{0:T(256)} %absorption.1) | copy-start | bytes 3076
  17.9 11.7 %copy-start.8 = (f32[2]{0:T(128)S(1)}, f32[2]{0:T(128)}, u32[]{:S(2)}) copy-start(f32[2]{0:T(128)} %sun.1) | copy-start | bytes 28
  17.9 11.7 %collective-permute-start.2 = (f32[9,8,512]{2,1,0:T(8,128)S(1)}, f32[9,8,512]{2,1,0:T(8,128)S(1)}, u32[]{:S(2)}, u32[]{:S(2)}) collective-permute-start(f32[9,8,512]{2,1,0:T(8,128)S(1)} %get-tuple-element.28), channel_id=1, source_target_pairs={{0,64},{64,0},{1,65},{65,1},{2,66},{66,2},{3,67},{67,3},{4,68},{68... | collective-permute-start | bytes 442376 | tf_op jit(solution)/shard_map/ppermute | solution.py:394
  39.8 7.7 %collective-permute-start.3 = (f32[8,8,512]{2,1,0:T(8,128)S(1)}, f32[8,8,512]{2,1,0:T(8,128)S(1)}, u32[]{:S(2)}, u32[]{:S(2)}) collective-permute-start(f32[8,8,512]{2,1,0:T(8,128)S(1)} %get-tuple-element.30), channel_id=1, source_target_pairs={{0,64},{64,0},{1,65},{65,1},{2,66},{66,2},{3,67},{67,3},{4,68},{68... | collective-permute-start | bytes 393224 | tf_op jit(solution)/shard_map/ppermute | solution.py:411

commit v3 on v2

--- a/solution.py
+++ b/solution.py
@@ -19,6 +19,7 @@
 
 VMEM = pltpu.VMEM
 SMEM = pltpu.SMEM
+HBM = pltpu.HBM
 F32 = jnp.float32
 
 
@@ -30,7 +31,7 @@
     return lax.broadcasted_iota(jnp.int32, (8, LANES), 0)
 
 
-def coarsen_kernel(moist, albedo, keep, send):
+def coarsen(moist, albedo, keep, send):
     width = moist.shape[-1]
     half = keep.shape[-1] // LANES
     even_row = sub_iota() % 2 == 0
@@ -53,10 +54,9 @@
             parts = []
             for side in range(2):
                 cols = pl.ds((2 * block + side) * LANES, LANES)
-                if level < 8:
-                    parts.append((moist[level, 0:8, cols], moist[level, 8:16, cols]))
-                else:
-                    parts.append((albedo[0:8, cols], albedo[8:16, cols]))
+                source = moist if level < 8 else albedo
+                index = (level,) if level < 8 else ()
+                parts.append((source[(*index, slice(0, 8), cols)], source[(*index, slice(8, 16), cols)]))
             top = pack(parts[0][0], parts[1][0])
             bottom = pack(parts[0][1], parts[1][1])
             value = fold(top, bottom) * 0.25
@@ -64,6 +64,87 @@
                 keep[level, :, pl.ds(block * LANES, LANES)] = value
             else:
                 send[level, :, pl.ds((block - half) * LANES, LANES)] = value
+
+
+def turn_in(source, rows, target, turned, scale=None):
+    by_row = jnp.swapaxes(source[:, pl.ds(rows, 8), :], 0, 1)
+    for row in range(8):
+        blocks = [by_row[row][:, b * LANES : (b + 1) * LANES] for b in range(16)]
+        turned[rows + row] = jnp.concatenate(blocks, axis=0).T
+        for i in range(16):
+            value = turned[rows + row, pl.ds(i, 8, stride=16), :]
+            if scale is not None:
+                value = scale * value
+            target[rows + row, pl.ds(8 * i, 8), :] = value
+
+
+def turn_out(source, rows, target, turned, by_row, scale=None):
+    for row in range(rows, rows + 8):
+        for i in range(16):
+            value = source[row, pl.ds(8 * i, 8), :]
+            if scale is not None:
+                value = scale * value
+            turned[row, pl.ds(i, 8, stride=16), :] = value
+        blocks = turned[row].T
+        for b in range(16):
+            by_row[row, :, pl.ds(b * LANES, LANES)] = blocks[8 * b : 8 * b + 8]
+    target[:, pl.ds(rows, 8), :] = jnp.swapaxes(by_row[pl.ds(rows, 8)], 0, 1)
+
+
+def prepare_kernel(
+    courant_in,
+    moist_in,
+    albedo_in,
+    east_in,
+    flow_in,
+    press_in,
+    keep,
+    send,
+    east_0,
+    flow_0,
+    press_0,
+    moist,
+    albedo,
+    east,
+    flow,
+    press,
+    turned,
+    sems,
+    courant,
+):
+    pairs = [(moist_in, moist), (flow_in, flow), (east_in, east), (press_in, press)]
+    parts = 4
+    copies = {}
+    for n, (source, target) in enumerate(pairs):
+        for part in range(parts):
+            some = pl.ds(2 * part, 2)
+            copies[n, part] = pltpu.make_async_copy(
+                source.at[some], target.at[some], sems.at[n, part]
+            )
+        if n == 0:
+            copies[4, 0] = pltpu.make_async_copy(albedo_in, albedo, sems.at[4, 0])
+    copies[5, 0] = pltpu.make_async_copy(courant_in, courant, sems.at[4, 1])
+    for copy in copies.values():
+        copy.start()
+
+    def wait(n):
+        for (field, _), copy in copies.items():
+            if field == n:
+                copy.wait()
+
+    wait(0)
+    wait(4)
+    coarsen(moist, albedo, keep, send)
+    wait(5)
+    half = courant_half(courant)
+    for n, field, target, scale in (
+        (1, flow, flow_0, None),
+        (2, east, east_0, None),
+        (3, press, press_0, half),
+    ):
+        wait(n)
+        for rows in (0, 8):
+            turn_in(field, rows, target, turned, scale)
 
 
 def radiate_kernel(
@@ -120,7 +201,7 @@
 
 
 def courant_half(courant):
-    level = sub_iota()
+    level = lane_iota() % 8
     value = jnp.full((8, LANES), courant[7], F32)
     for index in range(7):
         value = jnp.where(level == index, courant[index], value)
@@ -128,23 +209,23 @@
 
 
 def load_row(ref, row):
-    return [ref[row, :, pl.ds(j * LANES, LANES)] for j in range(ref.shape[-1] // LANES)]
+    return [ref[row, pl.ds(8 * i, 8), :] for i in range(16)]
 
 
 def store_row(ref, row, values):
-    for j, value in enumerate(values):
-        ref[row, :, pl.ds(j * LANES, LANES)] = value
-
-
-def shifted(values, by):
-    count = len(values)
-    turned = [pltpu.roll(v, (-by) % LANES, 1) for v in values]
-    lane = lane_iota()
-    if by > 0:
-        edge = lane >= LANES - by
-        return [jnp.where(edge, turned[(j + 1) % count], turned[j]) for j in range(count)]
-    edge = lane < -by
-    return [jnp.where(edge, turned[j - 1], turned[j]) for j in range(count)]
+    for i, value in enumerate(values):
+        if value is not None:
+            ref[row, pl.ds(8 * i, 8), :] = value
+
+
+def past_end(first):
+    up = pltpu.roll(first, 7, 0)
+    return jnp.where(sub_iota() == 7, pltpu.roll(up, LANES - 8, 1), up)
+
+
+def before_start(last):
+    down = pltpu.roll(last, 1, 0)
+    return jnp.where(sub_iota() == 0, pltpu.roll(down, 8, 1), down)
 
 
 def plus(values, others, sign=1.0):
@@ -176,22 +257,49 @@
 def substep(old, new, press_rows, flow_rows, east_rows, rate):
     east, flow, press = old
     new_east, new_flow, new_press = new
-    every = sorted(set(press_rows) | {r + 1 for r in flow_rows} | {r + 2 for r in east_rows})
+    every = sorted(set(press_rows) | {r + 1 for r in flow_rows})
+    waiting = []
+
+    def ends():
+        row, before, after, pressures, winds = waiting.pop(0)
+        low, high = pressures[0] - before, after - pressures[1]
+        if winds is not None:
+            low, high = winds[0] - low, winds[1] - high
+        else:
+            low, high = -low, -high
+        new_east.put(row, [low] + [None] * 14 + [high])
+
     for row in every:
         if row in press_rows:
             change = plus(flow.get(row + 1), flow.get(row - 1), -1.0)
-            here = east.get(row)
-            if here is not None:
-                change = plus([e - b for e, b in zip(here, shifted(here, -2))], change)
+            winds = east.get(row)
+            if winds is not None:
+                ahead = winds[1:] + [past_end(winds[0])]
+                behind = [before_start(winds[15])] + winds[:-1]
+                change = plus([a - b for a, b in zip(ahead, behind)], change)
             change = [rate * c for c in change]
-            new_press.put(row, plus(press.get(row), change, -1.0))
+            here = plus(press.get(row), change, -1.0)
+            new_press.put(row, here)
+            if row in east_rows:
+                slope = [here[i + 1] - here[i - 1] for i in range(1, 15)]
+                inside = plus(winds and winds[1:15], slope, -1.0)
+                new_east.put(row, [None] + inside + [None])
+                waiting.append(
+                    (
+                        row,
+                        before_start(here[15]),
+                        past_end(here[0]),
+                        (here[1], here[14]),
+                        winds and (winds[0], winds[15]),
+                    )
+                )
         if row - 1 in flow_rows:
             slope = plus(new_press.get(row), new_press.get(row - 2), -1.0)
             new_flow.put(row - 1, plus(flow.get(row - 1), slope, -1.0))
-        if row - 2 in east_rows:
-            here = new_press.get(row - 2)
-            slope = [a - p for a, p in zip(shifted(here, 2), here)]
-            new_east.put(row - 2, plus(east.get(row - 2), slope, -1.0))
+        if len(waiting) > 2:
+            ends()
+    while waiting:
+        ends()
 
 
 def spans(*pairs):
@@ -225,38 +333,16 @@
 
 
 def alone_kernel(
-    courant,
-    east_in,
-    flow_in,
-    press_in,
-    east_0,
-    flow_0,
-    press_0,
-    low_out,
-    high_out,
-    mate,
-    far,
-    east,
-    flow,
-    press,
+    courant, east_0, flow_0, press_0, low_out, high_out, mate, far, east, flow, press
 ):
     even = lax.axis_index("tile") % 2 == 0
     half = courant_half(courant)
     rate = half * half
-    count = east.shape[-1] // LANES
-    for block in range(2):
-        rows = pl.ds(8 * block, 8)
-        flow_0[rows] = jnp.swapaxes(flow_in[:, rows, :], 0, 1)
-        east_0[rows] = jnp.swapaxes(east_in[:, rows, :], 0, 1)
-        press_0[rows] = jnp.swapaxes(press_in[:, rows, :], 0, 1)
     inner = range(16)
-    for row in inner:
-        store_row(east_0, row, shifted(load_row(east_0, row), 1))
-        store_row(press_0, row, [half * v for v in load_row(press_0, row)])
 
     def record(slot, rows):
         low, first, last, high = [rows.get(r) for r in (-1, 0, 15, 16)]
-        zero = [jnp.zeros((8, LANES), F32)] * count
+        zero = [jnp.zeros((8, LANES), F32)] * 16
         store_row(low_out, slot, low or zero)
         store_row(high_out, slot, high or zero)
 
@@ -297,6 +383,11 @@
     east,
     flow,
     press,
+    turned,
+    by_row,
+    ready_east,
+    ready_flow,
+    sems,
 ):
     tile = lax.axis_index("tile")
     even = tile % 2 == 0
@@ -323,43 +414,60 @@
         border(SUB + step, work[2], 1.0)
         substep(state, work, inner, inner, inner, rate)
         state = work
-    inverse = 1.0 / half
-    for row in inner:
-        store_row(east, row, shifted(load_row(east, row), -1))
-        store_row(press_out, row, [inverse * v for v in load_row(press, row)])
-    for block in range(2):
-        rows = pl.ds(8 * block, 8)
-        east_out[:, rows, :] = jnp.swapaxes(east[rows], 0, 1)
-        flow_out[:, rows, :] = jnp.swapaxes(flow[rows], 0, 1)
-
-
-def spread_kernel(press, heat_own, heat_back, out, heat_rows, sums):
+    copies = []
+    for field, ready, out in (
+        (flow, ready_flow, flow_out),
+        (east, ready_east, east_out),
+    ):
+        for rows in (0, 8):
+            turn_out(field, rows, ready, turned, by_row)
+            some = pl.ds(rows, 8)
+            copies.append(
+                pltpu.make_async_copy(
+                    ready.at[:, some], out.at[:, some], sems.at[len(copies)]
+                )
+            )
+            copies[-1].start()
+    for rows in (0, 8):
+        turn_out(press, rows, press_out, turned, by_row, 1.0 / half)
+    for copy in copies:
+        copy.wait()
+
+
+def spread_kernel(press, heat_own, heat_back, out, ready, sems):
     even_lane = lane_iota() % 2 == 0
-    for source, part in enumerate((heat_own, heat_back)):
-        width = part.shape[-1]
-        heat_rows[:, :, pl.ds(source * width, width)] = jnp.swapaxes(part[...], 0, 1)
-    for sublane in range(8):
-        coarse = sublane // 2 + 4 * (sublane % 2)
-        for block, value in enumerate(load_row(heat_rows, sublane)):
+    even_row = sub_iota() % 2 == 0
+    blocks = heat_own.shape[-1] // LANES
+    copies = []
+    for level in range(8):
+        for block in range(2 * blocks):
+            part = heat_own if block < blocks else heat_back
+            value = part[level, :, pl.ds(block % blocks * LANES, LANES)]
             left = jnp.where(even_lane, value, pltpu.roll(value, 1, 1))
             right = jnp.where(even_lane, pltpu.roll(value, LANES - 1, 1), value)
             for side, heat in enumerate((left, right)):
                 cols = pl.ds((2 * block + side) * LANES, LANES)
-                for row in (2 * coarse, 2 * coarse + 1):
-                    sums[row, :, cols] = press[row, :, cols] + heat
-    for block in range(2):
-        rows = pl.ds(8 * block, 8)
-        out[:, rows, :] = jnp.swapaxes(sums[rows], 0, 1)
-
-
-def call(kernel, outs, n_smem, n_vmem, scratch=(), limit=16):
+                top = jnp.where(even_row, heat, pltpu.roll(heat, 1, 0))
+                bottom = jnp.where(even_row, pltpu.roll(heat, 7, 0), heat)
+                ready[level, 0:8, cols] = press[level, 0:8, cols] + top
+                ready[level, 8:16, cols] = press[level, 8:16, cols] + bottom
+        copies.append(
+            pltpu.make_async_copy(ready.at[level], out.at[level], sems.at[level])
+        )
+        copies[-1].start()
+    for copy in copies:
+        copy.wait()
+
+
+def call(kernel, ins, outs, scratch=(), sems=None, more=(), limit=16):
     return pl.pallas_call(
         kernel,
-        out_shape=[jax.ShapeDtypeStruct(s, F32) for s in outs],
-        in_specs=[pl.BlockSpec(memory_space=SMEM)] * n_smem
-        + [pl.BlockSpec(memory_space=VMEM)] * n_vmem,
-        out_specs=[pl.BlockSpec(memory_space=VMEM)] * len(outs),
-        scratch_shapes=[VMEM(s, F32) for s in scratch],
+        out_shape=[jax.ShapeDtypeStruct(shape, F32) for shape, _ in outs],
+        in_specs=[pl.BlockSpec(memory_space=space) for space in ins],
+        out_specs=[pl.BlockSpec(memory_space=space) for _, space in outs],
+        scratch_shapes=[VMEM(shape, F32) for shape in scratch]
+        + ([pltpu.SemaphoreType.DMA(sems)] if sems else [])
+        + list(more),
         compiler_params=pltpu.CompilerParams(vmem_limit_bytes=limit << 20),
         cost_estimate=pl.CostEstimate(
             flops=10**7, bytes_accessed=10**7, transcendentals=0
@@ -389,37 +497,52 @@
         + [(n_tiles - 1, 2 * n_tiles - 1)]
     )
 
+    field = (levels, rows, cols)
     coarse = (9, 8, half_cols)
-    keep, send = call(coarsen_kernel, [coarse, coarse], 0, 2)(moist, albedo[0])
+    staged = (rows, LANES, LANES)
+    series = (2 * SUB, LANES, LANES)
+    heat = (8, 8, half_cols)
+
+    keep, send, east, flow, press = call(
+        prepare_kernel,
+        [HBM] * 6,
+        [(coarse, VMEM)] * 2 + [(staged, VMEM)] * 3,
+        [field, albedo.shape[1:], field, field, field, staged],
+        (5, 4),
+        [SMEM(courant.shape, F32)],
+    )(
+        *(
+            pltpu.with_memory_space_constraint(x, HBM)
+            for x in (courant, moist, albedo[0], east, flow, press)
+        )
+    )
     other = lax.ppermute(send, "group", swap)
 
-    series = (2 * SUB, 8, cols)
-    staged = (rows, 8, cols)
-    east, flow, press, low, high, mate, far = call(
-        alone_kernel, [staged] * 3 + [series] * 4, 1, 3, [(rows + 2 * OFF, 8, cols)] * 3
+    low, high, mate, far = call(
+        alone_kernel,
+        [SMEM] + [VMEM] * 3,
+        [(series, VMEM)] * 4,
+        [(rows + 2 * OFF, LANES, LANES)] * 3,
     )(courant, east, flow, press)
     from_far = lax.ppermute(far, ("group", "tile"), fars)
     from_mate = lax.ppermute(mate, "tile", mates)
 
-    heat = (8, 8, half_cols)
     heat_own, heat_other = call(
         functools.partial(radiate_kernel, n_tiles * rows // 2, cols // 2),
-        [heat, heat],
-        3,
-        2,
+        [SMEM] * 3 + [VMEM] * 2,
+        [(heat, VMEM)] * 2,
     )(sun_angles, absorption, solar_weights, keep, other)
     heat_back = lax.ppermute(heat_other, "group", swap)
 
-    field = (levels, rows, cols)
     east, flow, press = call(
         functools.partial(joined_kernel, n_tiles),
-        [field, field, staged],
-        1,
-        7,
-        [staged] * 3,
+        [SMEM] + [VMEM] * 7,
+        [(field, HBM)] * 2 + [(field, VMEM)],
+        [staged] * 4 + [(rows, 8, cols)] + [field] * 2,
+        (4,),
     )(courant, east, flow, press, low, high, from_mate, from_far)
     (press,) = call(
-        spread_kernel, [field], 0, 3, [(8, 8, cols // 2), staged]
+        spread_kernel, [VMEM] * 3, [(field, HBM)], [field], (8,)
     )(press, heat_own, heat_back)
     return east[None], flow[None], press[None]
 

time: 49.1 us -> 45.8 us (0.933)
  local copies, waits for them, and re-layouts: 4.35 us -> 0.67 us
    unnamed x18 -> x8, local copies, waits for them, and re-layouts: 4.35 us -> 0.67 us
where the time goes in v3:
time: 45.8 us; the launch traced here: 45.7 us
  Pallas kernels  23.3 us (51%)
  waiting for transfers between devices  11.4 us (25%)
  starting transfers between devices  9.58 us (21%)
  between operations  0.72 us (2%)
  local copies, waits for them, and re-layouts  0.67 us (1%)
    ppermute x1, waiting for transfers between devices, shards(): other = lax.ppermute(send, 'group', swap)  11.4 us
    pallas_call x1, Pallas kernels, shards(): call(functools.partial(radiate_kernel, n_tiles * rows // 2, cols // 2), [...  10.2 us
    ppermute x1, starting transfers between devices, shards(): from_far = lax.ppermute(far, ('group', 'tile'), fars)  7.31 us
    pallas_call x1, Pallas kernels, shards(): call(functools.partial(joined_kernel, n_tiles), [SMEM] + [VMEM] * 7, [(fi...  5.54 us
    pallas_call x1, Pallas kernels, shards(): call(prepare_kernel, [HBM] * 6, [(coarse, VMEM)] * 2 + [(staged, VMEM)] *...  3.52 us
    pallas_call x1, Pallas kernels, shards(): call(alone_kernel, [SMEM] + [VMEM] * 3, [(series, VMEM)] * 4, [(rows + 2...  2.92 us
    ppermute x1, starting transfers between devices, shards(): heat_back = lax.ppermute(heat_other, 'group', swap)  1.51 us
    pallas_call x1, Pallas kernels, shards(): call(spread_kernel, [VMEM] * 3, [(field, HBM)], [field], (8,))  1.12 us
  transfers between devices with their start and end apart: 4, of which 1 were waited for; matrix products, arithmetic and copies ran while one was open for 0% of the time, Pallas kernels for 34%

profile of v3, /device:TPU:96, one launch (start us, length us, event | category | flops | bytes accessed | tf_op | source)
XLA Modules:
  0.0 45.7 jit_solution(6410444369269562098)
XLA Ops:
  0.6 3.5 %shard_map.112 = (f32[9,8,512]{2,1,0:T(8,128)S(1)}, f32[9,8,512]{2,1,0:T(8,128)S(1)}, f32[16,128,128]{2,1,0:T(8,128)S(1)}, f32[16,128,128]{2,1,0:T(8,128)S(1)}, f32[16,128,128]{2,1,0:T(8,128)S(1)}) custom-call(f32[8]{0:T(128)} %courant.3, f32[8,16,2048]{2,1,0:T(8,128)} %bitcast.8, f32[16,2048]{1,0:T(8,128)} %bitcast.13, f32[8,16,2048]{2,1,0:T(8,128)} %bitcast.9, ...), custom_call_target="tpu_custom_call" | custom-call | flops 10000000 | bytes 10000000 | tf_op jit(solution)/shard_map/pallas_call | solution.py:506
  4.2 0.0 copy-start
  4.2 0.6 %copy-done = f32[8]{0:T(128)S(1)} copy-done((f32[8]{0:T(128)S(1)}, f32[8]{0:T(128)}, u32[]{:S(2)}) %copy-start) | copy-done | bytes 56
  4.8 2.9 %shard_map.113 = (f32[12,128,128]{2,1,0:T(8,128)S(1)}, f32[12,128,128]{2,1,0:T(8,128)S(1)}, f32[12,128,128]{2,1,0:T(8,128)S(1)}, f32[12,128,128]{2,1,0:T(8,128)S(1)}) custom-call(f32[8]{0:T(128)S(1)} %copy-done, f32[16,128,128]{2,1,0:T(8,128)S(1)} %get-tuple-element.17.east_0, f32[16,128,128]{2,1,0:T(8,128)S(1)} %get-tuple-element.18.flow_0, ...), custom_call_target="tpu_custom_call" | custom-call | flops 10000000 | bytes 10000000 | tf_op jit(solution)/shard_map/pallas_call | solution.py:521
  7.7 0.1 collective-permute-start
  7.8 7.3 %collective-permute-start.1 = (f32[12,128,128]{2,1,0:T(8,128)S(1)}, f32[12,128,128]{2,1,0:T(8,128)S(1)}, u32[]{:S(2)}, u32[]{:S(2)}) collective-permute-start(f32[12,128,128]{2,1,0:T(8,128)S(1)} %get-tuple-element.23), channel_id=1, source_target_pairs={{1,2},{2,1},{3,4},{4,3},{5,6},{6,5},{7,8},{8,7},{9,10},{10,9},{11,... | collective-permute-start | bytes 2359304 | tf_op jit(solution)/shard_map/ppermute | solution.py:527
  15.2 0.0 copy-start.2
  15.2 0.0 copy-start.1
  15.2 0.0 copy-start.3
  15.2 0.7 %collective-permute-start.2 = (f32[9,8,512]{2,1,0:T(8,128)S(1)}, f32[9,8,512]{2,1,0:T(8,128)S(1)}, u32[]{:S(2)}, u32[]{:S(2)}) collective-permute-start(f32[9,8,512]{2,1,0:T(8,128)S(1)} %get-tuple-element.28), channel_id=1, source_target_pairs={{0,64},{64,0},{1,65},{65,1},{2,66},{66,2},{3,67},{67,3},{4,68},{68... | collective-permute-start | bytes 442376 | tf_op jit(solution)/shard_map/ppermute | solution.py:519
  15.9 11.4 %collective-permute-done.2.other = f32[9,8,512]{2,1,0:T(8,128)S(1)} collective-permute-done((f32[9,8,512]{2,1,0:T(8,128)S(1)}, f32[9,8,512]{2,1,0:T(8,128)S(1)}, u32[]{:S(2)}, u32[]{:S(2)}) %collective-permute-start.2) | collective-permute-done | bytes 147488 | tf_op jit(solution)/shard_map/ppermute | solution.py:519
  27.3 0.0 copy-done.2
  27.3 0.0 copy-done.1
  27.3 0.0 copy-done.3
  27.3 10.2 %shard_map.115 = (f32[8,8,512]{2,1,0:T(8,128)S(1)}, f32[8,8,512]{2,1,0:T(8,128)S(1)}) custom-call(f32[2]{0:T(128)S(1)} %copy-done.3, f32[256]{0:T(256)S(1)} %copy-done.1, f32[256]{0:T(256)S(1)} %copy-done.2, f32[9,8,512]{2,1,0:T(8,128)S(1)} %get-tuple-element.27.own, f32[9,8,512]{2,1,0:T(8,128)S(1)} %collective-permute-done.2.other), custom_call_target="tpu_custom_call" | custom-call | flops 10000000 | bytes 10000000 | tf_op jit(solution)/shard_map/pallas_call | solution.py:530
  37.5 1.5 %collective-permute-start.3 = (f32[8,8,512]{2,1,0:T(8,128)S(1)}, f32[8,8,512]{2,1,0:T(8,128)S(1)}, u32[]{:S(2)}, u32[]{:S(2)}) collective-permute-start(f32[8,8,512]{2,1,0:T(8,128)S(1)} %get-tuple-element.30), channel_id=1, source_target_pairs={{0,64},{64,0},{1,65},{65,1},{2,66},{66,2},{3,67},{67,3},{4,68},{68... | collective-permute-start | bytes 393224 | tf_op jit(solution)/shard_map/ppermute | solution.py:535
  39.0 0.0 collective-permute-done.from_mate
  39.0 0.0 collective-permute-done.1.from_far
  39.0 5.5 %shard_map.114 = (f32[8,16,2048]{2,1,0:T(8,128)}, f32[8,16,2048]{2,1,0:T(8,128)}, f32[8,16,2048]{2,1,0:T(8,128)S(1)}) custom-call(f32[8]{0:T(128)S(1)} %copy-done, f32[16,128,128]{2,1,0:T(8,128)S(1)} %get-tuple-element.17.east_0, f32[16,128,128]{2,1,0:T(8,128)S(1)} %get-tuple-element.18.flow_0, f32[16,128,128]{2,1,0:T(8,128)S(1)} %get-tuple-element.19.press_0, ...), custom_call_target="tpu_custom_call" | custom-call | flops 10000000 | bytes 10000000 | tf_op jit(solution)/shard_map/pallas_call | solution.py:537
  44.5 0.0 collective-permute-done.3.heat_back
  44.6 1.1 %shard_map.116 = f32[8,16,2048]{2,1,0:T(8,128)} custom-call(f32[8,16,2048]{2,1,0:T(8,128)S(1)} %get-tuple-element.26.press, f32[8,8,512]{2,1,0:T(8,128)S(1)} %get-tuple-element.29.heat_own, f32[8,8,512]{2,1,0:T(8,128)S(1)} %collective-permute-done.3.heat_back), custom_call_target="tpu_custom_call" | custom-call | flops 10000000 | bytes 10000000 | tf_op jit(solution)/shard_map/pallas_call | solution.py:544
Async XLA Ops:
  4.2 0.7 %copy-start = (f32[8]{0:T(128)S(1)}, f32[8]{0:T(128)}, u32[]{:S(2)}) copy-start(f32[8]{0:T(128)} %courant.3) | copy-start | bytes 100
  7.7 31.3 %collective-permute-start = (f32[12,128,128]{2,1,0:T(8,128)S(1)}, f32[12,128,128]{2,1,0:T(8,128)S(1)}, u32[]{:S(2)}, u32[]{:S(2)}) collective-permute-start(f32[12,128,128]{2,1,0:T(8,128)S(1)} %get-tuple-element.22), channel_id=1, source_target_pairs={{0,1},{1,0},{2,3},{3,2},{4,5},{5,4},{6,7},{7,6},{8,9},{9,8},{10,11... | collective-permute-start | bytes 2359304 | tf_op jit(solution)/shard_map/ppermute | solution.py:528
  7.8 31.2 %collective-permute-start.1 = (f32[12,128,128]{2,1,0:T(8,128)S(1)}, f32[12,128,128]{2,1,0:T(8,128)S(1)}, u32[]{:S(2)}, u32[]{:S(2)}) collective-permute-start(f32[12,128,128]{2,1,0:T(8,128)S(1)} %get-tuple-element.23), channel_id=1, source_target_pairs={{1,2},{2,1},{3,4},{4,3},{5,6},{6,5},{7,8},{8,7},{9,10},{10,9},{11,... | collective-permute-start | bytes 2359304 | tf_op jit(solution)/shard_map/ppermute | solution.py:527
  15.2 12.1 %copy-start.2 = (f32[256]{0:T(256)S(1)}, f32[256]{0:T(256)}, u32[]{:S(2)}) copy-start(f32[256]{0:T(256)} %weights.1) | copy-start | bytes 3076
  15.2 12.1 %copy-start.1 = (f32[256]{0:T(256)S(1)}, f32[256]{0:T(256)}, u32[]{:S(2)}) copy-start(f32[256]{0:T(256)} %absorption.1) | copy-start | bytes 3076
  15.2 12.1 %copy-start.3 = (f32[2]{0:T(128)S(1)}, f32[2]{0:T(128)}, u32[]{:S(2)}) copy-start(f32[2]{0:T(128)} %sun.1) | copy-start | bytes 28
  15.2 12.1 %collective-permute-start.2 = (f32[9,8,512]{2,1,0:T(8,128)S(1)}, f32[9,8,512]{2,1,0:T(8,128)S(1)}, u32[]{:S(2)}, u32[]{:S(2)}) collective-permute-start(f32[9,8,512]{2,1,0:T(8,128)S(1)} %get-tuple-element.28), channel_id=1, source_target_pairs={{0,64},{64,0},{1,65},{65,1},{2,66},{66,2},{3,67},{67,3},{4,68},{68... | collective-permute-start | bytes 442376 | tf_op jit(solution)/shard_map/ppermute | solution.py:519
  37.5 7.1 %collective-permute-start.3 = (f32[8,8,512]{2,1,0:T(8,128)S(1)}, f32[8,8,512]{2,1,0:T(8,128)S(1)}, u32[]{:S(2)}, u32[]{:S(2)}) collective-permute-start(f32[8,8,512]{2,1,0:T(8,128)S(1)} %get-tuple-element.30), channel_id=1, source_target_pairs={{0,64},{64,0},{1,65},{65,1},{2,66},{66,2},{3,67},{67,3},{4,68},{68... | collective-permute-start | bytes 393224 | tf_op jit(solution)/shard_map/ppermute | solution.py:535

commit v4 on v3

--- a/solution.py
+++ b/solution.py
@@ -103,6 +103,7 @@
     east_0,
     flow_0,
     press_0,
+    half_out,
     moist,
     albedo,
     east,
@@ -112,39 +113,39 @@
     sems,
     courant,
 ):
-    pairs = [(moist_in, moist), (flow_in, flow), (east_in, east), (press_in, press)]
-    parts = 4
-    copies = {}
-    for n, (source, target) in enumerate(pairs):
-        for part in range(parts):
-            some = pl.ds(2 * part, 2)
-            copies[n, part] = pltpu.make_async_copy(
-                source.at[some], target.at[some], sems.at[n, part]
+    fields = [(flow_in, flow), (east_in, east), (press_in, press)]
+    copies = {("courant", 0): pltpu.make_async_copy(courant_in, courant, sems.at[0, 0])}
+    for n, (source, target) in enumerate(fields):
+        for part in range(4):
+            some = (pl.ds(part % 2 * 4, 4), pl.ds(part // 2 * 8, 8))
+            copies[n, part // 2, part % 2] = pltpu.make_async_copy(
+                source.at[some], target.at[some], sems.at[n + 1, part]
             )
-        if n == 0:
-            copies[4, 0] = pltpu.make_async_copy(albedo_in, albedo, sems.at[4, 0])
-    copies[5, 0] = pltpu.make_async_copy(courant_in, courant, sems.at[4, 1])
+    for part in range(4):
+        some = pl.ds(2 * part, 2)
+        copies["coarse", part] = pltpu.make_async_copy(
+            moist_in.at[some], moist.at[some], sems.at[4, part]
+        )
+    copies["coarse", 4] = pltpu.make_async_copy(albedo_in, albedo, sems.at[0, 1])
     for copy in copies.values():
         copy.start()
 
-    def wait(n):
-        for (field, _), copy in copies.items():
-            if field == n:
+    def wait(*key):
+        for name, copy in copies.items():
+            if name[: len(key)] == key:
                 copy.wait()
 
-    wait(0)
-    wait(4)
+    wait("courant")
+    half = courant_half(courant)
+    half_out[...] = half
+    for n, (field, target, scale) in enumerate(
+        ((flow, flow_0, None), (east, east_0, None), (press, press_0, half))
+    ):
+        for part in range(2):
+            wait(n, part)
+            turn_in(field, 8 * part, target, turned, scale)
+    wait("coarse")
     coarsen(moist, albedo, keep, send)
-    wait(5)
-    half = courant_half(courant)
-    for n, field, target, scale in (
-        (1, flow, flow_0, None),
-        (2, east, east_0, None),
-        (3, press, press_0, half),
-    ):
-        wait(n)
-        for rows in (0, 8):
-            turn_in(field, rows, target, turned, scale)
 
 
 def radiate_kernel(
@@ -333,11 +334,10 @@
 
 
 def alone_kernel(
-    courant, east_0, flow_0, press_0, low_out, high_out, mate, far, east, flow, press
+    half, east_0, flow_0, press_0, low_out, high_out, mate, far, east, flow, press
 ):
     even = lax.axis_index("tile") % 2 == 0
-    half = courant_half(courant)
-    rate = half * half
+    rate = half[...] * half[...]
     inner = range(16)
 
     def record(slot, rows):
@@ -369,7 +369,7 @@
 
 def joined_kernel(
     n_tiles,
-    courant,
+    half,
     east_0,
     flow_0,
     press_0,
@@ -391,8 +391,7 @@
 ):
     tile = lax.axis_index("tile")
     even = tile % 2 == 0
-    half = courant_half(courant)
-    rate = half * half
+    rate = half[...] * half[...]
     inner = range(16)
     keep_low = jnp.where(tile == 0, 0.0, 1.0)
     turn = jnp.where(tile == n_tiles - 1, -1.0, 1.0)
@@ -429,7 +428,7 @@
             )
             copies[-1].start()
     for rows in (0, 8):
-        turn_out(press, rows, press_out, turned, by_row, 1.0 / half)
+        turn_out(press, rows, press_out, turned, by_row, 1.0 / half[...])
     for copy in copies:
         copy.wait()
 
@@ -503,10 +502,10 @@
     series = (2 * SUB, LANES, LANES)
     heat = (8, 8, half_cols)
 
-    keep, send, east, flow, press = call(
+    keep, send, east, flow, press, half = call(
         prepare_kernel,
         [HBM] * 6,
-        [(coarse, VMEM)] * 2 + [(staged, VMEM)] * 3,
+        [(coarse, VMEM)] * 2 + [(staged, VMEM)] * 3 + [((8, LANES), VMEM)],
         [field, albedo.shape[1:], field, field, field, staged],
         (5, 4),
         [SMEM(courant.shape, F32)],
@@ -520,10 +519,10 @@
 
     low, high, mate, far = call(
         alone_kernel,
-        [SMEM] + [VMEM] * 3,
+        [VMEM] * 4,
         [(series, VMEM)] * 4,
         [(rows + 2 * OFF, LANES, LANES)] * 3,
-    )(courant, east, flow, press)
+    )(half, east, flow, press)
     from_far = lax.ppermute(far, ("group", "tile"), fars)
     from_mate = lax.ppermute(mate, "tile", mates)
 
@@ -536,11 +535,11 @@
 
     east, flow, press = call(
         functools.partial(joined_kernel, n_tiles),
-        [SMEM] + [VMEM] * 7,
+        [VMEM] * 8,
         [(field, HBM)] * 2 + [(field, VMEM)],
         [staged] * 4 + [(rows, 8, cols)] + [field] * 2,
         (4,),
-    )(courant, east, flow, press, low, high, from_mate, from_far)
+    )(half, east, flow, press, low, high, from_mate, from_far)
     (press,) = call(
         spread_kernel, [VMEM] * 3, [(field, HBM)], [field], (8,)
     )(press, heat_own, heat_back)

time: 45.8 us -> 43.9 us (0.959)
  Pallas kernels: 23.3 us -> 22.1 us
  local copies, waits for them, and re-layouts: 0.67 us -> 0.02 us
    pallas_call x2, Pallas kernels: 8.46 us -> 7.37 us  [the longest x1 4.98 us: shards(): call(functools.partial(joined_kernel, n_tiles), [VMEM] * 8, [(field, HBM)...]
    unnamed x8 -> x6, local copies, waits for them, and re-layouts: 0.67 us -> 0.02 us
  transfers between devices with their start and end apart: 4 -> 4, of which waited for: 1 -> 1; matrix products, arithmetic and copies ran while one was open for 0% -> 0% of each run, Pallas kernels for 34% -> 35%
where the time goes in v4:
time: 43.9 us; the launch traced here: 43.8 us
  Pallas kernels  22.1 us (50%)
  waiting for transfers between devices  11.4 us (26%)
  starting transfers between devices  9.58 us (22%)
  between operations  0.72 us (2%)
    ppermute x1, waiting for transfers between devices, shards(): other = lax.ppermute(send, 'group', swap)  11.4 us
    pallas_call x1, Pallas kernels, shards(): call(functools.partial(radiate_kernel, n_tiles * rows // 2, cols // 2), [...  10.2 us
    ppermute x1, starting transfers between devices, shards(): from_far = lax.ppermute(far, ('group', 'tile'), fars)  7.31 us
    pallas_call x1, Pallas kernels, shards(): call(functools.partial(joined_kernel, n_tiles), [VMEM] * 8, [(field, HBM)...  4.98 us
    pallas_call x1, Pallas kernels, shards(): call(prepare_kernel, [HBM] * 6, [(coarse, VMEM)] * 2 + [(staged, VMEM)] *...  3.41 us
    pallas_call x1, Pallas kernels, shards(): call(alone_kernel, [VMEM] * 4, [(series, VMEM)] * 4, [(rows + 2 * OFF, LA...  2.39 us
    ppermute x1, starting transfers between devices, shards(): heat_back = lax.ppermute(heat_other, 'group', swap)  1.51 us
    pallas_call x1, Pallas kernels, shards(): call(spread_kernel, [VMEM] * 3, [(field, HBM)], [field], (8,))  1.12 us
  transfers between devices with their start and end apart: 4, of which 1 were waited for; matrix products, arithmetic and copies ran while one was open for 0% of the time, Pallas kernels for 35%

profile of v4, /device:TPU:96, one launch (start us, length us, event | category | flops | bytes accessed | tf_op | source)
XLA Modules:
  0.0 43.8 jit_solution(13050426932263888878)
XLA Ops:
  0.6 3.4 %shard_map.112 = (f32[9,8,512]{2,1,0:T(8,128)S(1)}, f32[9,8,512]{2,1,0:T(8,128)S(1)}, f32[16,128,128]{2,1,0:T(8,128)S(1)}, f32[16,128,128]{2,1,0:T(8,128)S(1)}, ...) custom-call(f32[8]{0:T(128)} %courant_in.1, f32[8,16,2048]{2,1,0:T(8,128)} %bitcast.8, f32[16,2048]{1,0:T(8,128)} %bitcast.13, ...), custom_call_target="tpu_custom_call" | custom-call | flops 10000000 | bytes 10000000 | tf_op jit(solution)/shard_map/pallas_call | solution.py:505
  4.0 2.4 %shard_map.113 = (f32[12,128,128]{2,1,0:T(8,128)S(1)}, f32[12,128,128]{2,1,0:T(8,128)S(1)}, f32[12,128,128]{2,1,0:T(8,128)S(1)}, f32[12,128,128]{2,1,0:T(8,128)S(1)}) custom-call(f32[8,128]{1,0:T(8,128)S(1)} %get-tuple-element.18.half, f32[16,128,128]{2,1,0:T(8,128)S(1)} %get-tuple-element.19.east_0, f32[16,128,128]{2,1,0:T(8,128)S(1)} %get-tuple-element.20.flow_0, ...), custom_call_target="tpu_custom_call" | custom-call | flops 10000000 | bytes 10000000 | tf_op jit(solution)/shard_map/pallas_call | solution.py:520
  6.4 0.1 collective-permute-start
  6.5 7.3 %collective-permute-start.1 = (f32[12,128,128]{2,1,0:T(8,128)S(1)}, f32[12,128,128]{2,1,0:T(8,128)S(1)}, u32[]{:S(2)}, u32[]{:S(2)}) collective-permute-start(f32[12,128,128]{2,1,0:T(8,128)S(1)} %get-tuple-element.25), channel_id=1, source_target_pairs={{1,2},{2,1},{3,4},{4,3},{5,6},{6,5},{7,8},{8,7},{9,10},{10,9},{11,... | collective-permute-start | bytes 2359304 | tf_op jit(solution)/shard_map/ppermute | solution.py:526
  13.9 0.0 copy-start.1
  13.9 0.0 copy-start
  13.9 0.0 copy-start.2
  13.9 0.7 %collective-permute-start.2 = (f32[9,8,512]{2,1,0:T(8,128)S(1)}, f32[9,8,512]{2,1,0:T(8,128)S(1)}, u32[]{:S(2)}, u32[]{:S(2)}) collective-permute-start(f32[9,8,512]{2,1,0:T(8,128)S(1)} %get-tuple-element.30), channel_id=1, source_target_pairs={{0,64},{64,0},{1,65},{65,1},{2,66},{66,2},{3,67},{67,3},{4,68},{68... | collective-permute-start | bytes 442376 | tf_op jit(solution)/shard_map/ppermute | solution.py:518
  14.6 11.4 %collective-permute-done.2.other = f32[9,8,512]{2,1,0:T(8,128)S(1)} collective-permute-done((f32[9,8,512]{2,1,0:T(8,128)S(1)}, f32[9,8,512]{2,1,0:T(8,128)S(1)}, u32[]{:S(2)}, u32[]{:S(2)}) %collective-permute-start.2) | collective-permute-done | bytes 147488 | tf_op jit(solution)/shard_map/ppermute | solution.py:518
  26.0 0.0 copy-done.1
  26.0 0.0 copy-done
  26.0 0.0 copy-done.2
  26.0 10.2 %shard_map.115 = (f32[8,8,512]{2,1,0:T(8,128)S(1)}, f32[8,8,512]{2,1,0:T(8,128)S(1)}) custom-call(f32[2]{0:T(128)S(1)} %copy-done.2, f32[256]{0:T(256)S(1)} %copy-done, f32[256]{0:T(256)S(1)} %copy-done.1, f32[9,8,512]{2,1,0:T(8,128)S(1)} %get-tuple-element.29.own, f32[9,8,512]{2,1,0:T(8,128)S(1)} %collective-permute-done.2.other), custom_call_target="tpu_custom_call" | custom-call | flops 10000000 | bytes 10000000 | tf_op jit(solution)/shard_map/pallas_call | solution.py:529
  36.2 1.5 %collective-permute-start.3 = (f32[8,8,512]{2,1,0:T(8,128)S(1)}, f32[8,8,512]{2,1,0:T(8,128)S(1)}, u32[]{:S(2)}, u32[]{:S(2)}) collective-permute-start(f32[8,8,512]{2,1,0:T(8,128)S(1)} %get-tuple-element.32), channel_id=1, source_target_pairs={{0,64},{64,0},{1,65},{65,1},{2,66},{66,2},{3,67},{67,3},{4,68},{68... | collective-permute-start | bytes 393224 | tf_op jit(solution)/shard_map/ppermute | solution.py:534
  37.7 0.0 collective-permute-done.from_mate
  37.7 0.0 collective-permute-done.1.from_far
  37.7 5.0 %shard_map.114 = (f32[8,16,2048]{2,1,0:T(8,128)}, f32[8,16,2048]{2,1,0:T(8,128)}, f32[8,16,2048]{2,1,0:T(8,128)S(1)}) custom-call(f32[8,128]{1,0:T(8,128)S(1)} %get-tuple-element.18.half, f32[16,128,128]{2,1,0:T(8,128)S(1)} %get-tuple-element.19.east_0, f32[16,128,128]{2,1,0:T(8,128)S(1)} %get-tuple-element.20.flow_0, ...), custom_call_target="tpu_custom_call" | custom-call | flops 10000000 | bytes 10000000 | tf_op jit(solution)/shard_map/pallas_call | solution.py:536
  42.7 0.0 collective-permute-done.3.heat_back
  42.7 1.1 %shard_map.116 = f32[8,16,2048]{2,1,0:T(8,128)} custom-call(f32[8,16,2048]{2,1,0:T(8,128)S(1)} %get-tuple-element.28.press, f32[8,8,512]{2,1,0:T(8,128)S(1)} %get-tuple-element.31.heat_own, f32[8,8,512]{2,1,0:T(8,128)S(1)} %collective-permute-done.3.heat_back), custom_call_target="tpu_custom_call" | custom-call | flops 10000000 | bytes 10000000 | tf_op jit(solution)/shard_map/pallas_call | solution.py:543
Async XLA Ops:
  6.4 31.3 %collective-permute-start = (f32[12,128,128]{2,1,0:T(8,128)S(1)}, f32[12,128,128]{2,1,0:T(8,128)S(1)}, u32[]{:S(2)}, u32[]{:S(2)}) collective-permute-start(f32[12,128,128]{2,1,0:T(8,128)S(1)} %get-tuple-element.24), channel_id=1, source_target_pairs={{0,1},{1,0},{2,3},{3,2},{4,5},{5,4},{6,7},{7,6},{8,9},{9,8},{10,11... | collective-permute-start | bytes 2359304 | tf_op jit(solution)/shard_map/ppermute | solution.py:527
  6.5 31.2 %collective-permute-start.1 = (f32[12,128,128]{2,1,0:T(8,128)S(1)}, f32[12,128,128]{2,1,0:T(8,128)S(1)}, u32[]{:S(2)}, u32[]{:S(2)}) collective-permute-start(f32[12,128,128]{2,1,0:T(8,128)S(1)} %get-tuple-element.25), channel_id=1, source_target_pairs={{1,2},{2,1},{3,4},{4,3},{5,6},{6,5},{7,8},{8,7},{9,10},{10,9},{11,... | collective-permute-start | bytes 2359304 | tf_op jit(solution)/shard_map/ppermute | solution.py:526
  13.9 12.1 %copy-start.1 = (f32[256]{0:T(256)S(1)}, f32[256]{0:T(256)}, u32[]{:S(2)}) copy-start(f32[256]{0:T(256)} %weights.1) | copy-start | bytes 3076
  13.9 12.1 %copy-start = (f32[256]{0:T(256)S(1)}, f32[256]{0:T(256)}, u32[]{:S(2)}) copy-start(f32[256]{0:T(256)} %absorption.1) | copy-start | bytes 3076
  13.9 12.1 %copy-start.2 = (f32[2]{0:T(128)S(1)}, f32[2]{0:T(128)}, u32[]{:S(2)}) copy-start(f32[2]{0:T(128)} %sun.1) | copy-start | bytes 28
  13.9 12.1 %collective-permute-start.2 = (f32[9,8,512]{2,1,0:T(8,128)S(1)}, f32[9,8,512]{2,1,0:T(8,128)S(1)}, u32[]{:S(2)}, u32[]{:S(2)}) collective-permute-start(f32[9,8,512]{2,1,0:T(8,128)S(1)} %get-tuple-element.30), channel_id=1, source_target_pairs={{0,64},{64,0},{1,65},{65,1},{2,66},{66,2},{3,67},{67,3},{4,68},{68... | collective-permute-start | bytes 442376 | tf_op jit(solution)/shard_map/ppermute | solution.py:518
  36.2 6.5 %collective-permute-start.3 = (f32[8,8,512]{2,1,0:T(8,128)S(1)}, f32[8,8,512]{2,1,0:T(8,128)S(1)}, u32[]{:S(2)}, u32[]{:S(2)}) collective-permute-start(f32[8,8,512]{2,1,0:T(8,128)S(1)} %get-tuple-element.32), channel_id=1, source_target_pairs={{0,64},{64,0},{1,65},{65,1},{2,66},{66,2},{3,67},{67,3},{4,68},{68... | collective-permute-start | bytes 393224 | tf_op jit(solution)/shard_map/ppermute | solution.py:534

commit v5 on v4

--- a/solution.py
+++ b/solution.py
@@ -66,26 +66,29 @@
                 send[level, :, pl.ds((block - half) * LANES, LANES)] = value
 
 
-def turn_in(source, rows, target, turned, scale=None):
+def turn_in(source, rows, target, scale=None):
     by_row = jnp.swapaxes(source[:, pl.ds(rows, 8), :], 0, 1)
     for row in range(8):
         blocks = [by_row[row][:, b * LANES : (b + 1) * LANES] for b in range(16)]
-        turned[rows + row] = jnp.concatenate(blocks, axis=0).T
-        for i in range(16):
-            value = turned[rows + row, pl.ds(i, 8, stride=16), :]
-            if scale is not None:
-                value = scale * value
-            target[rows + row, pl.ds(8 * i, 8), :] = value
-
-
-def turn_out(source, rows, target, turned, by_row, scale=None):
+        flat = jnp.concatenate(blocks, axis=0).T
+        values = []
+        for half in range(2):
+            eights = [flat[8 * k : 8 * k + 8] for k in range(half, 16, 2)]
+            turned = jnp.swapaxes(jnp.stack(eights), 0, 1)
+            values += [turned[i] for i in range(8)]
+        if scale is not None:
+            values = [scale * v for v in values]
+        store_row(target, rows + row, values)
+
+
+def turn_out(source, rows, target, by_row, scale=None):
     for row in range(rows, rows + 8):
-        for i in range(16):
-            value = source[row, pl.ds(8 * i, 8), :]
-            if scale is not None:
-                value = scale * value
-            turned[row, pl.ds(i, 8, stride=16), :] = value
-        blocks = turned[row].T
+        values = load_row(source, row)
+        if scale is not None:
+            values = [scale * v for v in values]
+        halves = [jnp.swapaxes(jnp.stack(values[h : h + 8]), 0, 1) for h in (0, 8)]
+        flat = jnp.concatenate([halves[k % 2][k // 2] for k in range(16)], axis=0)
+        blocks = flat.T
         for b in range(16):
             by_row[row, :, pl.ds(b * LANES, LANES)] = blocks[8 * b : 8 * b + 8]
     target[:, pl.ds(rows, 8), :] = jnp.swapaxes(by_row[pl.ds(rows, 8)], 0, 1)
@@ -109,7 +112,6 @@
     east,
     flow,
     press,
-    turned,
     sems,
     courant,
 ):
@@ -143,7 +145,7 @@
     ):
         for part in range(2):
             wait(n, part)
-            turn_in(field, 8 * part, target, turned, scale)
+            turn_in(field, 8 * part, target, scale)
     wait("coarse")
     coarsen(moist, albedo, keep, send)
 
@@ -383,7 +385,6 @@
     east,
     flow,
     press,
-    turned,
     by_row,
     ready_east,
     ready_flow,
@@ -419,7 +420,7 @@
         (east, ready_east, east_out),
     ):
         for rows in (0, 8):
-            turn_out(field, rows, ready, turned, by_row)
+            turn_out(field, rows, ready, by_row)
             some = pl.ds(rows, 8)
             copies.append(
                 pltpu.make_async_copy(
@@ -428,7 +429,7 @@
             )
             copies[-1].start()
     for rows in (0, 8):
-        turn_out(press, rows, press_out, turned, by_row, 1.0 / half[...])
+        turn_out(press, rows, press_out, by_row, 1.0 / half[...])
     for copy in copies:
         copy.wait()
 
@@ -506,7 +507,7 @@
         prepare_kernel,
         [HBM] * 6,
         [(coarse, VMEM)] * 2 + [(staged, VMEM)] * 3 + [((8, LANES), VMEM)],
-        [field, albedo.shape[1:], field, field, field, staged],
+        [field, albedo.shape[1:], field, field, field],
         (5, 4),
         [SMEM(courant.shape, F32)],
     )(
@@ -537,7 +538,7 @@
         functools.partial(joined_kernel, n_tiles),
         [VMEM] * 8,
         [(field, HBM)] * 2 + [(field, VMEM)],
-        [staged] * 4 + [(rows, 8, cols)] + [field] * 2,
+        [staged] * 3 + [(rows, 8, cols)] + [field] * 2,
         (4,),
     )(half, east, flow, press, low, high, from_mate, from_far)
     (press,) = call(

time: 43.9 us -> 42.8 us (0.975)
  Pallas kernels: 22.1 us -> 21 us
    pallas_call x1, Pallas kernels: 4.98 us -> 4.21 us  [shards(): call(functools.partial(joined_kernel, n_tiles), [VMEM] * 8, [(field, HBM)...]
  transfers between devices with their start and end apart: 4 -> 4, of which waited for: 1 -> 1; matrix products, arithmetic and copies ran while one was open for 0% -> 0% of each run, Pallas kernels for 35% -> 34%
where the time goes in v5:
time: 42.8 us; the launch traced here: 42.7 us
  Pallas kernels  21 us (49%)
  waiting for transfers between devices  11.4 us (27%)
  starting transfers between devices  9.58 us (22%)
  between operations  0.72 us (2%)
    ppermute x1, waiting for transfers between devices, shards(): other = lax.ppermute(send, 'group', swap)  11.4 us
    pallas_call x1, Pallas kernels, shards(): call(functools.partial(radiate_kernel, n_tiles * rows // 2, cols // 2), [...  10.2 us
    ppermute x1, starting transfers between devices, shards(): from_far = lax.ppermute(far, ('group', 'tile'), fars)  7.31 us
    pallas_call x1, Pallas kernels, shards(): call(functools.partial(joined_kernel, n_tiles), [VMEM] * 8, [(field, HBM)...  4.21 us
    pallas_call x1, Pallas kernels, shards(): call(prepare_kernel, [HBM] * 6, [(coarse, VMEM)] * 2 + [(staged, VMEM)] *...  3.04 us
    pallas_call x1, Pallas kernels, shards(): call(alone_kernel, [VMEM] * 4, [(series, VMEM)] * 4, [(rows + 2 * OFF, LA...  2.39 us
    ppermute x1, starting transfers between devices, shards(): heat_back = lax.ppermute(heat_other, 'group', swap)  1.51 us
    pallas_call x1, Pallas kernels, shards(): call(spread_kernel, [VMEM] * 3, [(field, HBM)], [field], (8,))  1.12 us
  transfers between devices with their start and end apart: 4, of which 1 were waited for; matrix products, arithmetic and copies ran while one was open for 0% of the time, Pallas kernels for 34%

profile of v5, /device:TPU:96, one launch (start us, length us, event | category | flops | bytes accessed | tf_op | source)
XLA Modules:
  0.0 42.7 jit_solution(15782162865971917331)
XLA Ops:
  0.6 3.0 %shard_map.112 = (f32[9,8,512]{2,1,0:T(8,128)S(1)}, f32[9,8,512]{2,1,0:T(8,128)S(1)}, f32[16,128,128]{2,1,0:T(8,128)S(1)}, f32[16,128,128]{2,1,0:T(8,128)S(1)}, ...) custom-call(f32[8]{0:T(128)} %courant_in.1, f32[8,16,2048]{2,1,0:T(8,128)} %bitcast.8, f32[16,2048]{1,0:T(8,128)} %bitcast.13, ...), custom_call_target="tpu_custom_call" | custom-call | flops 10000000 | bytes 10000000 | tf_op jit(solution)/shard_map/pallas_call | solution.py:506
  3.7 2.4 %shard_map.113 = (f32[12,128,128]{2,1,0:T(8,128)S(1)}, f32[12,128,128]{2,1,0:T(8,128)S(1)}, f32[12,128,128]{2,1,0:T(8,128)S(1)}, f32[12,128,128]{2,1,0:T(8,128)S(1)}) custom-call(f32[8,128]{1,0:T(8,128)S(1)} %get-tuple-element.18.half, f32[16,128,128]{2,1,0:T(8,128)S(1)} %get-tuple-element.19.east_0, f32[16,128,128]{2,1,0:T(8,128)S(1)} %get-tuple-element.20.flow_0, ...), custom_call_target="tpu_custom_call" | custom-call | flops 10000000 | bytes 10000000 | tf_op jit(solution)/shard_map/pallas_call | solution.py:521
  6.1 0.1 collective-permute-start
  6.2 7.3 %collective-permute-start.1 = (f32[12,128,128]{2,1,0:T(8,128)S(1)}, f32[12,128,128]{2,1,0:T(8,128)S(1)}, u32[]{:S(2)}, u32[]{:S(2)}) collective-permute-start(f32[12,128,128]{2,1,0:T(8,128)S(1)} %get-tuple-element.25), channel_id=1, source_target_pairs={{1,2},{2,1},{3,4},{4,3},{5,6},{6,5},{7,8},{8,7},{9,10},{10,9},{11,... | collective-permute-start | bytes 2359304 | tf_op jit(solution)/shard_map/ppermute | solution.py:527
  13.5 0.0 copy-start.1
  13.5 0.0 copy-start
  13.5 0.0 copy-start.2
  13.5 0.7 %collective-permute-start.2 = (f32[9,8,512]{2,1,0:T(8,128)S(1)}, f32[9,8,512]{2,1,0:T(8,128)S(1)}, u32[]{:S(2)}, u32[]{:S(2)}) collective-permute-start(f32[9,8,512]{2,1,0:T(8,128)S(1)} %get-tuple-element.30), channel_id=1, source_target_pairs={{0,64},{64,0},{1,65},{65,1},{2,66},{66,2},{3,67},{67,3},{4,68},{68... | collective-permute-start | bytes 442376 | tf_op jit(solution)/shard_map/ppermute | solution.py:519
  14.2 11.4 %collective-permute-done.2.other = f32[9,8,512]{2,1,0:T(8,128)S(1)} collective-permute-done((f32[9,8,512]{2,1,0:T(8,128)S(1)}, f32[9,8,512]{2,1,0:T(8,128)S(1)}, u32[]{:S(2)}, u32[]{:S(2)}) %collective-permute-start.2) | collective-permute-done | bytes 147488 | tf_op jit(solution)/shard_map/ppermute | solution.py:519
  25.6 0.0 copy-done.1
  25.6 0.0 copy-done
  25.6 0.0 copy-done.2
  25.6 10.2 %shard_map.115 = (f32[8,8,512]{2,1,0:T(8,128)S(1)}, f32[8,8,512]{2,1,0:T(8,128)S(1)}) custom-call(f32[2]{0:T(128)S(1)} %copy-done.2, f32[256]{0:T(256)S(1)} %copy-done, f32[256]{0:T(256)S(1)} %copy-done.1, f32[9,8,512]{2,1,0:T(8,128)S(1)} %get-tuple-element.29.own, f32[9,8,512]{2,1,0:T(8,128)S(1)} %collective-permute-done.2.other), custom_call_target="tpu_custom_call" | custom-call | flops 10000000 | bytes 10000000 | tf_op jit(solution)/shard_map/pallas_call | solution.py:530
  35.8 1.5 %collective-permute-start.3 = (f32[8,8,512]{2,1,0:T(8,128)S(1)}, f32[8,8,512]{2,1,0:T(8,128)S(1)}, u32[]{:S(2)}, u32[]{:S(2)}) collective-permute-start(f32[8,8,512]{2,1,0:T(8,128)S(1)} %get-tuple-element.32), channel_id=1, source_target_pairs={{0,64},{64,0},{1,65},{65,1},{2,66},{66,2},{3,67},{67,3},{4,68},{68... | collective-permute-start | bytes 393224 | tf_op jit(solution)/shard_map/ppermute | solution.py:535
  37.3 0.0 collective-permute-done.from_mate
  37.3 0.0 collective-permute-done.1.from_far
  37.3 4.2 %shard_map.114 = (f32[8,16,2048]{2,1,0:T(8,128)}, f32[8,16,2048]{2,1,0:T(8,128)}, f32[8,16,2048]{2,1,0:T(8,128)S(1)}) custom-call(f32[8,128]{1,0:T(8,128)S(1)} %get-tuple-element.18.half, f32[16,128,128]{2,1,0:T(8,128)S(1)} %get-tuple-element.19.east_0, f32[16,128,128]{2,1,0:T(8,128)S(1)} %get-tuple-element.20.flow_0, ...), custom_call_target="tpu_custom_call" | custom-call | flops 10000000 | bytes 10000000 | tf_op jit(solution)/shard_map/pallas_call | solution.py:537
  41.6 0.0 collective-permute-done.3.heat_back
  41.6 1.1 %shard_map.116 = f32[8,16,2048]{2,1,0:T(8,128)} custom-call(f32[8,16,2048]{2,1,0:T(8,128)S(1)} %get-tuple-element.28.press, f32[8,8,512]{2,1,0:T(8,128)S(1)} %get-tuple-element.31.heat_own, f32[8,8,512]{2,1,0:T(8,128)S(1)} %collective-permute-done.3.heat_back), custom_call_target="tpu_custom_call" | custom-call | flops 10000000 | bytes 10000000 | tf_op jit(solution)/shard_map/pallas_call | solution.py:544
Async XLA Ops:
  6.1 31.3 %collective-permute-start = (f32[12,128,128]{2,1,0:T(8,128)S(1)}, f32[12,128,128]{2,1,0:T(8,128)S(1)}, u32[]{:S(2)}, u32[]{:S(2)}) collective-permute-start(f32[12,128,128]{2,1,0:T(8,128)S(1)} %get-tuple-element.24), channel_id=1, source_target_pairs={{0,1},{1,0},{2,3},{3,2},{4,5},{5,4},{6,7},{7,6},{8,9},{9,8},{10,11... | collective-permute-start | bytes 2359304 | tf_op jit(solution)/shard_map/ppermute | solution.py:528
  6.2 31.2 %collective-permute-start.1 = (f32[12,128,128]{2,1,0:T(8,128)S(1)}, f32[12,128,128]{2,1,0:T(8,128)S(1)}, u32[]{:S(2)}, u32[]{:S(2)}) collective-permute-start(f32[12,128,128]{2,1,0:T(8,128)S(1)} %get-tuple-element.25), channel_id=1, source_target_pairs={{1,2},{2,1},{3,4},{4,3},{5,6},{6,5},{7,8},{8,7},{9,10},{10,9},{11,... | collective-permute-start | bytes 2359304 | tf_op jit(solution)/shard_map/ppermute | solution.py:527
  13.5 12.1 %copy-start.1 = (f32[256]{0:T(256)S(1)}, f32[256]{0:T(256)}, u32[]{:S(2)}) copy-start(f32[256]{0:T(256)} %weights.1) | copy-start | bytes 3076
  13.5 12.1 %copy-start = (f32[256]{0:T(256)S(1)}, f32[256]{0:T(256)}, u32[]{:S(2)}) copy-start(f32[256]{0:T(256)} %absorption.1) | copy-start | bytes 3076
  13.5 12.1 %copy-start.2 = (f32[2]{0:T(128)S(1)}, f32[2]{0:T(128)}, u32[]{:S(2)}) copy-start(f32[2]{0:T(128)} %sun.1) | copy-start | bytes 28
  13.5 12.1 %collective-permute-start.2 = (f32[9,8,512]{2,1,0:T(8,128)S(1)}, f32[9,8,512]{2,1,0:T(8,128)S(1)}, u32[]{:S(2)}, u32[]{:S(2)}) collective-permute-start(f32[9,8,512]{2,1,0:T(8,128)S(1)} %get-tuple-element.30), channel_id=1, source_target_pairs={{0,64},{64,0},{1,65},{65,1},{2,66},{66,2},{3,67},{67,3},{4,68},{68... | collective-permute-start | bytes 442376 | tf_op jit(solution)/shard_map/ppermute | solution.py:519
  35.8 5.7 %collective-permute-start.3 = (f32[8,8,512]{2,1,0:T(8,128)S(1)}, f32[8,8,512]{2,1,0:T(8,128)S(1)}, u32[]{:S(2)}, u32[]{:S(2)}) collective-permute-start(f32[8,8,512]{2,1,0:T(8,128)S(1)} %get-tuple-element.32), channel_id=1, source_target_pairs={{0,64},{64,0},{1,65},{65,1},{2,66},{66,2},{3,67},{67,3},{4,68},{68... | collective-permute-start | bytes 393224 | tf_op jit(solution)/shard_map/ppermute | solution.py:535

commit v6 on v5

--- a/solution.py
+++ b/solution.py
@@ -96,6 +96,9 @@
 
 def prepare_kernel(
     courant_in,
+    sun_in,
+    absorption_in,
+    weights_in,
     moist_in,
     albedo_in,
     east_in,
@@ -107,6 +110,9 @@
     flow_0,
     press_0,
     half_out,
+    sun_out,
+    absorption,
+    weights,
     moist,
     albedo,
     east,
@@ -114,9 +120,13 @@
     press,
     sems,
     courant,
+    sun,
 ):
     fields = [(flow_in, flow), (east_in, east), (press_in, press)]
-    copies = {("courant", 0): pltpu.make_async_copy(courant_in, courant, sems.at[0, 0])}
+    copies = {
+        ("small", 0): pltpu.make_async_copy(courant_in, courant, sems.at[0, 0]),
+        ("small", 1): pltpu.make_async_copy(sun_in, sun, sems.at[0, 2]),
+    }
     for n, (source, target) in enumerate(fields):
         for part in range(4):
             some = (pl.ds(part % 2 * 4, 4), pl.ds(part // 2 * 8, 8))
@@ -129,6 +139,8 @@
             moist_in.at[some], moist.at[some], sems.at[4, part]
         )
     copies["coarse", 4] = pltpu.make_async_copy(albedo_in, albedo, sems.at[0, 1])
+    copies["rates", 0] = pltpu.make_async_copy(absorption_in, absorption, sems.at[0, 3])
+    copies["rates", 1] = pltpu.make_async_copy(weights_in, weights, sems.at[5, 0])
     for copy in copies.values():
         copy.start()
 
@@ -137,9 +149,11 @@
             if name[: len(key)] == key:
                 copy.wait()
 
-    wait("courant")
+    wait("small")
     half = courant_half(courant)
     half_out[...] = half
+    for index in range(2):
+        sun_out[index] = jnp.full((8, LANES), sun[index], F32)
     for n, (field, target, scale) in enumerate(
         ((flow, flow_0, None), (east, east_0, None), (press, press_0, half))
     ):
@@ -148,10 +162,11 @@
             turn_in(field, 8 * part, target, scale)
     wait("coarse")
     coarsen(moist, albedo, keep, send)
+    wait("rates")
 
 
 def radiate_kernel(
-    rows_total, cols_total, sun, absorption, weights, own, other, heat_own, heat_other
+    rows_total, cols_total, absorption, weights, sun, own, other, heat_own, heat_other
 ):
     group = lax.axis_index("group")
     tile = lax.axis_index("tile")
@@ -161,7 +176,7 @@
     colatitude = 1.0 - (row.astype(F32) + 0.5) / rows_total
     hemisphere = 2.0 * group.astype(F32) - 1.0
     latitude = hemisphere * (0.5 * math.pi) * colatitude
-    declination = 0.41 * jnp.sin(jnp.full((8, LANES), sun[0], F32))
+    declination = 0.41 * jnp.sin(sun[0])
     sine = jnp.sin(latitude) * jnp.sin(declination)
     cosine = jnp.cos(latitude) * jnp.cos(declination)
     n_g = absorption.shape[0]
@@ -503,17 +518,30 @@
     series = (2 * SUB, LANES, LANES)
     heat = (8, 8, half_cols)
 
-    keep, send, east, flow, press, half = call(
+    keep, send, east, flow, press, half, sun, absorb, weights = call(
         prepare_kernel,
-        [HBM] * 6,
-        [(coarse, VMEM)] * 2 + [(staged, VMEM)] * 3 + [((8, LANES), VMEM)],
+        [HBM] * 9,
+        [(coarse, VMEM)] * 2
+        + [(staged, VMEM)] * 3
+        + [((8, LANES), VMEM), ((2, 8, LANES), VMEM)]
+        + [(absorption.shape, VMEM)] * 2,
         [field, albedo.shape[1:], field, field, field],
-        (5, 4),
-        [SMEM(courant.shape, F32)],
+        (6, 4),
+        [SMEM(courant.shape, F32), SMEM(sun_angles.shape, F32)],
     )(
         *(
             pltpu.with_memory_space_constraint(x, HBM)
-            for x in (courant, moist, albedo[0], east, flow, press)
+            for x in (
+                courant,
+                sun_angles,
+                absorption,
+                solar_weights,
+                moist,
+                albedo[0],
+                east,
+                flow,
+                press,
+            )
         )
     )
     other = lax.ppermute(send, "group", swap)
@@ -529,9 +557,9 @@
 
     heat_own, heat_other = call(
         functools.partial(radiate_kernel, n_tiles * rows // 2, cols // 2),
-        [SMEM] * 3 + [VMEM] * 2,
+        [SMEM] * 2 + [VMEM] * 3,
         [(heat, VMEM)] * 2,
-    )(sun_angles, absorption, solar_weights, keep, other)
+    )(absorb, weights, sun, keep, other)
     heat_back = lax.ppermute(heat_other, "group", swap)
 
     east, flow, press = call(

time: 42.8 us -> 42.7 us (level)
  no operation moved by 1% of the time
where the time goes in v6:
time: 42.7 us; the launch traced here: 42.6 us
  Pallas kernels  20.9 us (49%)
  waiting for transfers between devices  11.4 us (27%)
  starting transfers between devices  9.58 us (22%)
  between operations  0.69 us (2%)
    ppermute x1, waiting for transfers between devices, shards(): other = lax.ppermute(send, 'group', swap)  11.4 us
    pallas_call x1, Pallas kernels, shards(): call(functools.partial(radiate_kernel, n_tiles * rows // 2, cols // 2), [...  10.2 us
    ppermute x1, starting transfers between devices, shards(): from_far = lax.ppermute(far, ('group', 'tile'), fars)  7.31 us
    pallas_call x1, Pallas kernels, shards(): call(functools.partial(joined_kernel, n_tiles), [VMEM] * 8, [(field, HBM)...  4.14 us
    pallas_call x1, Pallas kernels, shards(): call(prepare_kernel, [HBM] * 9, [(coarse, VMEM)] * 2 + [(staged, VMEM)] *...  3.09 us
    pallas_call x1, Pallas kernels, shards(): call(alone_kernel, [VMEM] * 4, [(series, VMEM)] * 4, [(rows + 2 * OFF, LA...  2.39 us
    ppermute x1, starting transfers between devices, shards(): heat_back = lax.ppermute(heat_other, 'group', swap)  1.51 us
    pallas_call x1, Pallas kernels, shards(): call(spread_kernel, [VMEM] * 3, [(field, HBM)], [field], (8,))  1.12 us
  transfers between devices with their start and end apart: 4, of which 1 were waited for; matrix products, arithmetic and copies ran while one was open for 0% of the time, Pallas kernels for 34%

profile of v6, /device:TPU:96, one launch (start us, length us, event | category | flops | bytes accessed | tf_op | source)
XLA Modules:
  0.0 42.6 jit_solution(10587676350419412995)
XLA Ops:
  0.6 3.1 %shard_map.112 = (f32[9,8,512]{2,1,0:T(8,128)S(1)}, f32[9,8,512]{2,1,0:T(8,128)S(1)}, f32[16,128,128]{2,1,0:T(8,128)S(1)}, f32[16,128,128]{2,1,0:T(8,128)S(1)}, ...) custom-call(f32[8]{0:T(128)} %courant_in.1, ...), custom_call_target="tpu_custom_call" | custom-call | flops 10000000 | bytes 10000000 | tf_op jit(solution)/shard_map/pallas_call | solution.py:521
  3.7 2.4 %shard_map.113 = (f32[12,128,128]{2,1,0:T(8,128)S(1)}, f32[12,128,128]{2,1,0:T(8,128)S(1)}, f32[12,128,128]{2,1,0:T(8,128)S(1)}, f32[12,128,128]{2,1,0:T(8,128)S(1)}) custom-call(f32[8,128]{1,0:T(8,128)S(1)} %get-tuple-element.21.half, f32[16,128,128]{2,1,0:T(8,128)S(1)} %get-tuple-element.22.east_0, f32[16,128,128]{2,1,0:T(8,128)S(1)} %get-tuple-element.23.flow_0, ...), custom_call_target="tpu_custom_call" | custom-call | flops 10000000 | bytes 10000000 | tf_op jit(solution)/shard_map/pallas_call | solution.py:549
  6.1 0.1 collective-permute-start
  6.2 7.3 %collective-permute-start.1 = (f32[12,128,128]{2,1,0:T(8,128)S(1)}, f32[12,128,128]{2,1,0:T(8,128)S(1)}, u32[]{:S(2)}, u32[]{:S(2)}) collective-permute-start(f32[12,128,128]{2,1,0:T(8,128)S(1)} %get-tuple-element.28), channel_id=1, source_target_pairs={{1,2},{2,1},{3,4},{4,3},{5,6},{6,5},{7,8},{8,7},{9,10},{10,9},{11,... | collective-permute-start | bytes 2359304 | tf_op jit(solution)/shard_map/ppermute | solution.py:555
  13.5 0.7 %collective-permute-start.2 = (f32[9,8,512]{2,1,0:T(8,128)S(1)}, f32[9,8,512]{2,1,0:T(8,128)S(1)}, u32[]{:S(2)}, u32[]{:S(2)}) collective-permute-start(f32[9,8,512]{2,1,0:T(8,128)S(1)} %get-tuple-element.36), channel_id=1, source_target_pairs={{0,64},{64,0},{1,65},{65,1},{2,66},{66,2},{3,67},{67,3},{4,68},{68... | collective-permute-start | bytes 442376 | tf_op jit(solution)/shard_map/ppermute | solution.py:547
  14.2 11.4 %collective-permute-done.2.other = f32[9,8,512]{2,1,0:T(8,128)S(1)} collective-permute-done((f32[9,8,512]{2,1,0:T(8,128)S(1)}, f32[9,8,512]{2,1,0:T(8,128)S(1)}, u32[]{:S(2)}, u32[]{:S(2)}) %collective-permute-start.2) | collective-permute-done | bytes 147488 | tf_op jit(solution)/shard_map/ppermute | solution.py:547
  25.7 10.2 %shard_map.115 = (f32[8,8,512]{2,1,0:T(8,128)S(1)}, f32[8,8,512]{2,1,0:T(8,128)S(1)}) custom-call(f32[256]{0:T(256)S(1)} %get-tuple-element.32.absorption, f32[256]{0:T(256)S(1)} %get-tuple-element.33.weights, f32[2,8,128]{2,1,0:T(8,128)S(1)} %get-tuple-element.34.sun, f32[9,8,512]{2,1,0:T(8,128)S(1)} %get-tuple-element.35.own, ...), custom_call_target="tpu_custom_call" | custom-call | flops 10000000 | bytes 10000000 | tf_op jit(solution)/shard_map/pallas_call | solution.py:558
  35.8 1.5 %collective-permute-start.3 = (f32[8,8,512]{2,1,0:T(8,128)S(1)}, f32[8,8,512]{2,1,0:T(8,128)S(1)}, u32[]{:S(2)}, u32[]{:S(2)}) collective-permute-start(f32[8,8,512]{2,1,0:T(8,128)S(1)} %get-tuple-element.38), channel_id=1, source_target_pairs={{0,64},{64,0},{1,65},{65,1},{2,66},{66,2},{3,67},{67,3},{4,68},{68... | collective-permute-start | bytes 393224 | tf_op jit(solution)/shard_map/ppermute | solution.py:563
  37.3 0.0 collective-permute-done.from_mate
  37.3 0.0 collective-permute-done.1.from_far
  37.3 4.1 %shard_map.114 = (f32[8,16,2048]{2,1,0:T(8,128)}, f32[8,16,2048]{2,1,0:T(8,128)}, f32[8,16,2048]{2,1,0:T(8,128)S(1)}) custom-call(f32[8,128]{1,0:T(8,128)S(1)} %get-tuple-element.21.half, f32[16,128,128]{2,1,0:T(8,128)S(1)} %get-tuple-element.22.east_0, f32[16,128,128]{2,1,0:T(8,128)S(1)} %get-tuple-element.23.flow_0, ...), custom_call_target="tpu_custom_call" | custom-call | flops 10000000 | bytes 10000000 | tf_op jit(solution)/shard_map/pallas_call | solution.py:565
  41.5 0.0 collective-permute-done.3.heat_back
  41.5 1.1 %shard_map.116 = f32[8,16,2048]{2,1,0:T(8,128)} custom-call(f32[8,16,2048]{2,1,0:T(8,128)S(1)} %get-tuple-element.31.press, f32[8,8,512]{2,1,0:T(8,128)S(1)} %get-tuple-element.37.heat_own, f32[8,8,512]{2,1,0:T(8,128)S(1)} %collective-permute-done.3.heat_back), custom_call_target="tpu_custom_call" | custom-call | flops 10000000 | bytes 10000000 | tf_op jit(solution)/shard_map/pallas_call | solution.py:572
Async XLA Ops:
  6.1 31.2 %collective-permute-start = (f32[12,128,128]{2,1,0:T(8,128)S(1)}, f32[12,128,128]{2,1,0:T(8,128)S(1)}, u32[]{:S(2)}, u32[]{:S(2)}) collective-permute-start(f32[12,128,128]{2,1,0:T(8,128)S(1)} %get-tuple-element.27), channel_id=1, source_target_pairs={{0,1},{1,0},{2,3},{3,2},{4,5},{5,4},{6,7},{7,6},{8,9},{9,8},{10,11... | collective-permute-start | bytes 2359304 | tf_op jit(solution)/shard_map/ppermute | solution.py:556
  6.2 31.1 %collective-permute-start.1 = (f32[12,128,128]{2,1,0:T(8,128)S(1)}, f32[12,128,128]{2,1,0:T(8,128)S(1)}, u32[]{:S(2)}, u32[]{:S(2)}) collective-permute-start(f32[12,128,128]{2,1,0:T(8,128)S(1)} %get-tuple-element.28), channel_id=1, source_target_pairs={{1,2},{2,1},{3,4},{4,3},{5,6},{6,5},{7,8},{8,7},{9,10},{10,9},{11,... | collective-permute-start | bytes 2359304 | tf_op jit(solution)/shard_map/ppermute | solution.py:555
  13.5 12.1 %collective-permute-start.2 = (f32[9,8,512]{2,1,0:T(8,128)S(1)}, f32[9,8,512]{2,1,0:T(8,128)S(1)}, u32[]{:S(2)}, u32[]{:S(2)}) collective-permute-start(f32[9,8,512]{2,1,0:T(8,128)S(1)} %get-tuple-element.36), channel_id=1, source_target_pairs={{0,64},{64,0},{1,65},{65,1},{2,66},{66,2},{3,67},{67,3},{4,68},{68... | collective-permute-start | bytes 442376 | tf_op jit(solution)/shard_map/ppermute | solution.py:547
  35.8 5.7 %collective-permute-start.3 = (f32[8,8,512]{2,1,0:T(8,128)S(1)}, f32[8,8,512]{2,1,0:T(8,128)S(1)}, u32[]{:S(2)}, u32[]{:S(2)}) collective-permute-start(f32[8,8,512]{2,1,0:T(8,128)S(1)} %get-tuple-element.38), channel_id=1, source_target_pairs={{0,64},{64,0},{1,65},{65,1},{2,66},{66,2},{3,67},{67,3},{4,68},{68... | collective-permute-start | bytes 393224 | tf_op jit(solution)/shard_map/ppermute | solution.py:563

commit v7 on v6

--- a/solution.py
+++ b/solution.py
@@ -320,68 +320,38 @@
         ends()
 
 
-def spans(*pairs):
-    return [row for low, high in pairs for row in range(low, high + 1)]
-
-
-PRESS_SPANS = [
-    spans((-1, 16)),
-    spans((-3, 18)),
-    spans((-5, 6), (9, 20)),
-    spans((-5, 4), (11, 20)),
-    spans((-3, 2), (13, 18)),
-    spans((-1, 0), (15, 16)),
-]
-EAST_SPANS = [
-    spans((-1, 16)),
-    spans((-3, 6), (9, 18)),
-    spans((-5, 4), (11, 20)),
-    spans((-3, 2), (13, 18)),
-    spans((-1, 0), (15, 16)),
-    [],
-]
-FLOW_SPANS = [
-    spans((-2, 17)),
-    spans((-4, 19)),
-    spans((-6, 5), (10, 21)),
-    spans((-4, 3), (12, 19)),
-    spans((-2, 1), (14, 17)),
-    [],
-]
+PRESS_SPANS = [(-1, 10), (-3, 8), (-5, 6), (-5, 4), (-3, 2), (-1, 0)]
+EAST_SPANS = [(-1, 8), (-3, 6), (-5, 4), (-3, 2), (-1, 0), (0, -1)]
+FLOW_SPANS = [(-2, 9), (-4, 7), (-6, 5), (-4, 3), (-2, 1), (0, -1)]
 
 
 def alone_kernel(
-    half, east_0, flow_0, press_0, low_out, high_out, mate, far, east, flow, press
+    is_far, half, east_0, flow_0, press_0, own, send, east, flow, press
 ):
     even = lax.axis_index("tile") % 2 == 0
     rate = half[...] * half[...]
-    inner = range(16)
-
-    def record(slot, rows):
-        low, first, last, high = [rows.get(r) for r in (-1, 0, 15, 16)]
-        zero = [jnp.zeros((8, LANES), F32)] * 16
-        store_row(low_out, slot, low or zero)
-        store_row(high_out, slot, high or zero)
-
-        @pl.when(even)
-        def _():
-            store_row(mate, slot, last)
-            store_row(far, slot, first)
-
-        @pl.when(jnp.logical_not(even))
-        def _():
-            store_row(mate, slot, first)
-            store_row(far, slot, last)
-
-    state = [Rows(ref, 0, inner) for ref in (east_0, flow_0, press_0)]
-    work = [Rows(ref, -OFF) for ref in (east, flow, press)]
-    for step in range(SUB):
-        record(step, state[1])
-        substep(
-            state, work, PRESS_SPANS[step], FLOW_SPANS[step], EAST_SPANS[step], rate
-        )
-        state = work
-        record(SUB + step, state[2])
+
+    def run(place):
+        def span(pair):
+            return sorted(place(row) for row in range(pair[0], pair[1] + 1))
+
+        def record(slot, rows):
+            zero = [jnp.zeros((8, LANES), F32)] * 16
+            store_row(own, slot, rows.get(place(-1)) or zero)
+            store_row(send, slot, rows.get(place(0)))
+
+        state = [Rows(ref, 0, range(16)) for ref in (east_0, flow_0, press_0)]
+        work = [Rows(ref, -OFF) for ref in (east, flow, press)]
+        for step in range(SUB):
+            record(step, state[1])
+            spans = [s[step] for s in (PRESS_SPANS, FLOW_SPANS, EAST_SPANS)]
+            substep(state, work, *map(span, spans), rate)
+            state = work
+            record(SUB + step, state[2])
+
+    low = even if is_far else jnp.logical_not(even)
+    pl.when(low)(lambda: run(lambda row: row))
+    pl.when(jnp.logical_not(low))(lambda: run(lambda row: 15 - row))
 
 
 def joined_kernel(
@@ -390,8 +360,8 @@
     east_0,
     flow_0,
     press_0,
-    low_own,
-    high_own,
+    own_mate,
+    own_far,
     from_mate,
     from_far,
     east_out,
@@ -409,18 +379,17 @@
     even = tile % 2 == 0
     rate = half[...] * half[...]
     inner = range(16)
-    keep_low = jnp.where(tile == 0, 0.0, 1.0)
+    keep = jnp.where(tile == 0, 0.0, 1.0)
     turn = jnp.where(tile == n_tiles - 1, -1.0, 1.0)
 
     def border(slot, rows, sign):
-        mate, far = load_row(from_mate, slot), load_row(from_far, slot)
-        own_low, own_high = load_row(low_own, slot), load_row(high_own, slot)
-        rows.known[-1] = [
-            keep_low * o + jnp.where(even, f, m) for o, m, f in zip(own_low, mate, far)
+        mate = plus(load_row(own_mate, slot), load_row(from_mate, slot))
+        far = [
+            keep * o + sign * f
+            for o, f in zip(load_row(own_far, slot), load_row(from_far, slot))
         ]
-        rows.known[16] = [
-            o + sign * jnp.where(even, m, f) for o, m, f in zip(own_high, mate, far)
-        ]
+        rows.known[-1] = [jnp.where(even, f, m) for m, f in zip(mate, far)]
+        rows.known[16] = [jnp.where(even, m, f) for m, f in zip(mate, far)]
 
     state = [Rows(ref, 0, inner) for ref in (east_0, flow_0, press_0)]
     work = [Rows(ref, 0) for ref in (east, flow, press)]
@@ -546,13 +515,17 @@
     )
     other = lax.ppermute(send, "group", swap)
 
-    low, high, mate, far = call(
-        alone_kernel,
-        [VMEM] * 4,
-        [(series, VMEM)] * 4,
-        [(rows + 2 * OFF, LANES, LANES)] * 3,
-    )(half, east, flow, press)
+    def alone(is_far):
+        return call(
+            functools.partial(alone_kernel, is_far),
+            [VMEM] * 4,
+            [(series, VMEM)] * 2,
+            [(rows + 2 * OFF, LANES, LANES)] * 3,
+        )(half, east, flow, press)
+
+    own_far, far = alone(True)
     from_far = lax.ppermute(far, ("group", "tile"), fars)
+    own_mate, mate = alone(False)
     from_mate = lax.ppermute(mate, "tile", mates)
 
     heat_own, heat_other = call(
@@ -568,7 +541,7 @@
         [(field, HBM)] * 2 + [(field, VMEM)],
         [staged] * 3 + [(rows, 8, cols)] + [field] * 2,
         (4,),
-    )(half, east, flow, press, low, high, from_mate, from_far)
+    )(half, east, flow, press, own_mate, own_far, from_mate, from_far)
     (press,) = call(
         spread_kernel, [VMEM] * 3, [(field, HBM)], [field], (8,)
     )(press, heat_own, heat_back)

time: 42.7 us -> 42.8 us (level)
  starting transfers between devices: 9.58 us -> 9.13 us
    ppermute x1, starting transfers between devices: 7.31 us -> 6.68 us  [shards(): from_far = lax.ppermute(far, ('group', 'tile'), fars)]
    pallas_call x1 -> x2, Pallas kernels: 2.39 us -> 2.6 us  [alone(): call(functools.partial(alone_kernel, is_far), [VMEM] * 4, [(series, VMEM)...]
  transfers between devices with their start and end apart: 4 -> 4, of which waited for: 1 -> 1; matrix products, arithmetic and copies ran while one was open for 0% -> 0% of each run, Pallas kernels for 34% -> 37%
where the time goes in v7:
time: 42.8 us; the launch traced here: 42.7 us
  Pallas kernels  21.1 us (49%)
  waiting for transfers between devices  11.6 us (27%)
  starting transfers between devices  9.13 us (21%)
  between operations  0.86 us (2%)
    ppermute x1, waiting for transfers between devices, shards(): other = lax.ppermute(send, 'group', swap)  11.6 us
    pallas_call x1, Pallas kernels, shards(): call(functools.partial(radiate_kernel, n_tiles * rows // 2, cols // 2), [...  10.2 us
    ppermute x1, starting transfers between devices, shards(): from_far = lax.ppermute(far, ('group', 'tile'), fars)  6.68 us
    pallas_call x1, Pallas kernels, shards(): call(functools.partial(joined_kernel, n_tiles), [VMEM] * 8, [(field, HBM)...  4.13 us
    pallas_call x1, Pallas kernels, shards(): call(prepare_kernel, [HBM] * 9, [(coarse, VMEM)] * 2 + [(staged, VMEM)] *...  3.09 us
    pallas_call x2, Pallas kernels, alone(): call(functools.partial(alone_kernel, is_far), [VMEM] * 4, [(series, VMEM)...  2.6 us
    ppermute x1, starting transfers between devices, shards(): heat_back = lax.ppermute(heat_other, 'group', swap)  1.69 us
    pallas_call x1, Pallas kernels, shards(): call(spread_kernel, [VMEM] * 3, [(field, HBM)], [field], (8,))  1.12 us
  transfers between devices with their start and end apart: 4, of which 1 were waited for; matrix products, arithmetic and copies ran while one was open for 0% of the time, Pallas kernels for 37%

profile of v7, /device:TPU:96, one launch (start us, length us, event | category | flops | bytes accessed | tf_op | source)
XLA Modules:
  0.0 42.7 jit_solution(13250180096925251110)
XLA Ops:
  0.6 3.1 %shard_map.112 = (f32[9,8,512]{2,1,0:T(8,128)S(1)}, f32[9,8,512]{2,1,0:T(8,128)S(1)}, f32[16,128,128]{2,1,0:T(8,128)S(1)}, f32[16,128,128]{2,1,0:T(8,128)S(1)}, ...) custom-call(f32[8]{0:T(128)} %courant_in.1, ...), custom_call_target="tpu_custom_call" | custom-call | flops 10000000 | bytes 10000000 | tf_op jit(solution)/shard_map/pallas_call | solution.py:490
  3.7 1.3 %shard_map.114 = (f32[12,128,128]{2,1,0:T(8,128)S(1)}, f32[12,128,128]{2,1,0:T(8,128)S(1)}) custom-call(f32[8,128]{1,0:T(8,128)S(1)} %get-tuple-element.21.half, f32[16,128,128]{2,1,0:T(8,128)S(1)} %get-tuple-element.22.east_0, f32[16,128,128]{2,1,0:T(8,128)S(1)} %get-tuple-element.23.flow_0, f32[16,128,128]{2,1,0:T(8,128)S(1)} %get-tuple-element.24.press_0), custom_call_target="tpu_custom_call" | custom-call | flops 10000000 | bytes 10000000 | tf_op jit(solution)/shard_map/pallas_call | solution.py:519
  5.0 6.7 %collective-permute-start.1 = (f32[12,128,128]{2,1,0:T(8,128)S(1)}, f32[12,128,128]{2,1,0:T(8,128)S(1)}, u32[]{:S(2)}, u32[]{:S(2)}) collective-permute-start(f32[12,128,128]{2,1,0:T(8,128)S(1)} %get-tuple-element.28), channel_id=1, source_target_pairs={{1,2},{2,1},{3,4},{4,3},{5,6},{6,5},{7,8},{8,7},{9,10},{10,9},{11,... | collective-permute-start | bytes 2359304 | tf_op jit(solution)/shard_map/ppermute | solution.py:527
  11.7 1.3 %shard_map.113 = (f32[12,128,128]{2,1,0:T(8,128)S(1)}, f32[12,128,128]{2,1,0:T(8,128)S(1)}) custom-call(f32[8,128]{1,0:T(8,128)S(1)} %get-tuple-element.21.half, f32[16,128,128]{2,1,0:T(8,128)S(1)} %get-tuple-element.22.east_0, f32[16,128,128]{2,1,0:T(8,128)S(1)} %get-tuple-element.23.flow_0, f32[16,128,128]{2,1,0:T(8,128)S(1)} %get-tuple-element.24.press_0), custom_call_target="tpu_custom_call" | custom-call | flops 10000000 | bytes 10000000 | tf_op jit(solution)/shard_map/pallas_call | solution.py:519
  13.0 0.1 collective-permute-start
  13.1 0.7 %collective-permute-start.2 = (f32[9,8,512]{2,1,0:T(8,128)S(1)}, f32[9,8,512]{2,1,0:T(8,128)S(1)}, u32[]{:S(2)}, u32[]{:S(2)}) collective-permute-start(f32[9,8,512]{2,1,0:T(8,128)S(1)} %get-tuple-element.36), channel_id=1, source_target_pairs={{0,64},{64,0},{1,65},{65,1},{2,66},{66,2},{3,67},{67,3},{4,68},{68... | collective-permute-start | bytes 442376 | tf_op jit(solution)/shard_map/ppermute | solution.py:516
  13.8 11.6 %collective-permute-done.2.other = f32[9,8,512]{2,1,0:T(8,128)S(1)} collective-permute-done((f32[9,8,512]{2,1,0:T(8,128)S(1)}, f32[9,8,512]{2,1,0:T(8,128)S(1)}, u32[]{:S(2)}, u32[]{:S(2)}) %collective-permute-start.2) | collective-permute-done | bytes 147488 | tf_op jit(solution)/shard_map/ppermute | solution.py:516
  25.4 10.2 %shard_map.116 = (f32[8,8,512]{2,1,0:T(8,128)S(1)}, f32[8,8,512]{2,1,0:T(8,128)S(1)}) custom-call(f32[256]{0:T(256)S(1)} %get-tuple-element.32.absorption, f32[256]{0:T(256)S(1)} %get-tuple-element.33.weights, f32[2,8,128]{2,1,0:T(8,128)S(1)} %get-tuple-element.34.sun, f32[9,8,512]{2,1,0:T(8,128)S(1)} %get-tuple-element.35.own, ...), custom_call_target="tpu_custom_call" | custom-call | flops 10000000 | bytes 10000000 | tf_op jit(solution)/shard_map/pallas_call | solution.py:531
  35.6 1.7 %collective-permute-start.3 = (f32[8,8,512]{2,1,0:T(8,128)S(1)}, f32[8,8,512]{2,1,0:T(8,128)S(1)}, u32[]{:S(2)}, u32[]{:S(2)}) collective-permute-start(f32[8,8,512]{2,1,0:T(8,128)S(1)} %get-tuple-element.38), channel_id=1, source_target_pairs={{0,64},{64,0},{1,65},{65,1},{2,66},{66,2},{3,67},{67,3},{4,68},{68... | collective-permute-start | bytes 393224 | tf_op jit(solution)/shard_map/ppermute | solution.py:536
  37.3 0.0 collective-permute-done.1.from_far
  37.3 0.0 collective-permute-done.from_mate
  37.3 4.1 %shard_map.115 = (f32[8,16,2048]{2,1,0:T(8,128)}, f32[8,16,2048]{2,1,0:T(8,128)}, f32[8,16,2048]{2,1,0:T(8,128)S(1)}) custom-call(f32[8,128]{1,0:T(8,128)S(1)} %get-tuple-element.21.half, f32[16,128,128]{2,1,0:T(8,128)S(1)} %get-tuple-element.22.east_0, f32[16,128,128]{2,1,0:T(8,128)S(1)} %get-tuple-element.23.flow_0, ...), custom_call_target="tpu_custom_call" | custom-call | flops 10000000 | bytes 10000000 | tf_op jit(solution)/shard_map/pallas_call | solution.py:538
  41.4 0.0 collective-permute-done.3.heat_back
  41.4 1.1 %shard_map.117 = f32[8,16,2048]{2,1,0:T(8,128)} custom-call(f32[8,16,2048]{2,1,0:T(8,128)S(1)} %get-tuple-element.31.press, f32[8,8,512]{2,1,0:T(8,128)S(1)} %get-tuple-element.37.heat_own, f32[8,8,512]{2,1,0:T(8,128)S(1)} %collective-permute-done.3.heat_back), custom_call_target="tpu_custom_call" | custom-call | flops 10000000 | bytes 10000000 | tf_op jit(solution)/shard_map/pallas_call | solution.py:545
Async XLA Ops:
  5.0 32.3 %collective-permute-start.1 = (f32[12,128,128]{2,1,0:T(8,128)S(1)}, f32[12,128,128]{2,1,0:T(8,128)S(1)}, u32[]{:S(2)}, u32[]{:S(2)}) collective-permute-start(f32[12,128,128]{2,1,0:T(8,128)S(1)} %get-tuple-element.28), channel_id=1, source_target_pairs={{1,2},{2,1},{3,4},{4,3},{5,6},{6,5},{7,8},{8,7},{9,10},{10,9},{11,... | collective-permute-start | bytes 2359304 | tf_op jit(solution)/shard_map/ppermute | solution.py:527
  13.0 24.2 %collective-permute-start = (f32[12,128,128]{2,1,0:T(8,128)S(1)}, f32[12,128,128]{2,1,0:T(8,128)S(1)}, u32[]{:S(2)}, u32[]{:S(2)}) collective-permute-start(f32[12,128,128]{2,1,0:T(8,128)S(1)} %get-tuple-element.27), channel_id=1, source_target_pairs={{0,1},{1,0},{2,3},{3,2},{4,5},{5,4},{6,7},{7,6},{8,9},{9,8},{10,11... | collective-permute-start | bytes 2359304 | tf_op jit(solution)/shard_map/ppermute | solution.py:529
  13.1 12.3 %collective-permute-start.2 = (f32[9,8,512]{2,1,0:T(8,128)S(1)}, f32[9,8,512]{2,1,0:T(8,128)S(1)}, u32[]{:S(2)}, u32[]{:S(2)}) collective-permute-start(f32[9,8,512]{2,1,0:T(8,128)S(1)} %get-tuple-element.36), channel_id=1, source_target_pairs={{0,64},{64,0},{1,65},{65,1},{2,66},{66,2},{3,67},{67,3},{4,68},{68... | collective-permute-start | bytes 442376 | tf_op jit(solution)/shard_map/ppermute | solution.py:516
  35.6 5.8 %collective-permute-start.3 = (f32[8,8,512]{2,1,0:T(8,128)S(1)}, f32[8,8,512]{2,1,0:T(8,128)S(1)}, u32[]{:S(2)}, u32[]{:S(2)}) collective-permute-start(f32[8,8,512]{2,1,0:T(8,128)S(1)} %get-tuple-element.38), channel_id=1, source_target_pairs={{0,64},{64,0},{1,65},{65,1},{2,66},{66,2},{3,67},{67,3},{4,68},{68... | collective-permute-start | bytes 393224 | tf_op jit(solution)/shard_map/ppermute | solution.py:536

commit v8 on v7

--- a/solution.py
+++ b/solution.py
@@ -166,7 +166,7 @@
 
 
 def radiate_kernel(
-    rows_total, cols_total, absorption, weights, sun, own, other, heat_own, heat_other
+    rows_total, cols_total, first, absorption, weights, sun, own, other, heat_own, heat_other
 ):
     group = lax.axis_index("group")
     tile = lax.axis_index("tile")
@@ -181,8 +181,10 @@
     cosine = jnp.cos(latitude) * jnp.cos(declination)
     n_g = absorption.shape[0]
 
-    for block in range(own.shape[-1] // LANES):
+    for place in range(heat_own.shape[-1] // LANES):
+        block = first + place
         cols = pl.ds(block * LANES, LANES)
+        out_cols = pl.ds(place * LANES, LANES)
         column = block * LANES + lane // 2 + 64 * (lane % 2)
         longitude = 2.0 * math.pi * (column.astype(F32) + 0.5) / cols_total
         mu = sine + cosine * jnp.cos(longitude - sun[1])
@@ -214,8 +216,8 @@
         net = [scale * (down[j] - surface * up[j]) for j in range(9)]
         for level in range(8):
             heat = net[level] - net[level + 1]
-            heat_own[level, :, cols] = jnp.where(lit, heat, 0.0)
-            heat_other[level, :, cols] = jnp.where(lit, 0.0, heat)
+            heat_own[level, :, out_cols] = jnp.where(lit, heat, 0.0)
+            heat_other[level, :, out_cols] = jnp.where(lit, 0.0, heat)
 
 
 def courant_half(courant):
@@ -418,15 +420,18 @@
         copy.wait()
 
 
-def spread_kernel(press, heat_own, heat_back, out, ready, sems):
+def spread_kernel(press, own_1, own_2, back_1, back_2, out, ready, sems):
     even_lane = lane_iota() % 2 == 0
     even_row = sub_iota() % 2 == 0
-    blocks = heat_own.shape[-1] // LANES
+    places = [
+        (part, place)
+        for part in (own_1, own_2, back_1, back_2)
+        for place in range(part.shape[-1] // LANES)
+    ]
     copies = []
     for level in range(8):
-        for block in range(2 * blocks):
-            part = heat_own if block < blocks else heat_back
-            value = part[level, :, pl.ds(block % blocks * LANES, LANES)]
+        for block, (part, place) in enumerate(places):
+            value = part[level, :, pl.ds(place * LANES, LANES)]
             left = jnp.where(even_lane, value, pltpu.roll(value, 1, 1))
             right = jnp.where(even_lane, pltpu.roll(value, LANES - 1, 1), value)
             for side, heat in enumerate((left, right)):
@@ -485,7 +490,6 @@
     coarse = (9, 8, half_cols)
     staged = (rows, LANES, LANES)
     series = (2 * SUB, LANES, LANES)
-    heat = (8, 8, half_cols)
 
     keep, send, east, flow, press, half, sun, absorb, weights = call(
         prepare_kernel,
@@ -528,12 +532,19 @@
     own_mate, mate = alone(False)
     from_mate = lax.ppermute(mate, "tile", mates)
 
-    heat_own, heat_other = call(
-        functools.partial(radiate_kernel, n_tiles * rows // 2, cols // 2),
-        [SMEM] * 2 + [VMEM] * 3,
-        [(heat, VMEM)] * 2,
-    )(absorb, weights, sun, keep, other)
-    heat_back = lax.ppermute(heat_other, "group", swap)
+    def radiate(first, count):
+        shape = (8, 8, count * LANES)
+        return call(
+            functools.partial(radiate_kernel, n_tiles * rows // 2, cols // 2, first),
+            [SMEM] * 2 + [VMEM] * 3,
+            [(shape, VMEM)] * 2,
+        )(absorb, weights, sun, keep, other)
+
+    early = half_cols // LANES - 1
+    own_1, other_1 = radiate(0, early)
+    back_1 = lax.ppermute(other_1, "group", swap)
+    own_2, other_2 = radiate(early, 1)
+    back_2 = lax.ppermute(other_2, "group", swap)
 
     east, flow, press = call(
         functools.partial(joined_kernel, n_tiles),
@@ -543,8 +554,8 @@
         (4,),
     )(half, east, flow, press, own_mate, own_far, from_mate, from_far)
     (press,) = call(
-        spread_kernel, [VMEM] * 3, [(field, HBM)], [field], (8,)
-    )(press, heat_own, heat_back)
+        spread_kernel, [VMEM] * 5, [(field, HBM)], [field], (8,)
+    )(press, own_1, own_2, back_1, back_2)
     return east[None], flow[None], press[None]
 
 

time: 42.8 us -> 44.1 us (1.030)
  starting transfers between devices: 9.13 us -> 9.8 us
  Pallas kernels: 21.1 us -> 21.7 us
    ppermute x1 -> x2, starting transfers between devices: 1.69 us -> 2.37 us  [the longest x1 1.51 us: shards(): back_1 = lax.ppermute(other_1, 'group', swap)]
    pallas_call x2 -> x3, Pallas kernels: 11.3 us -> 11.9 us  [the longest x2 10.8 us: radiate(): call(functools.partial(radiate_kernel, n_tiles * rows // 2, cols // 2, fi...]
  transfers between devices with their start and end apart: 4 -> 5, of which waited for: 1 -> 1; matrix products, arithmetic and copies ran while one was open for 0% -> 0% of each run, Pallas kernels for 37% -> 37%
where the time goes in v8:
time: 44.1 us; the launch traced here: 44 us
  Pallas kernels  21.7 us (49%)
  waiting for transfers between devices  11.6 us (26%)
  starting transfers between devices  9.8 us (22%)
  between operations  0.88 us (2%)
    ppermute x1, waiting for transfers between devices, shards(): other = lax.ppermute(send, 'group', swap)  11.6 us
    pallas_call x2, Pallas kernels, radiate(): call(functools.partial(radiate_kernel, n_tiles * rows // 2, cols // 2, fi...  10.8 us
    ppermute x1, starting transfers between devices, shards(): from_far = lax.ppermute(far, ('group', 'tile'), fars)  6.68 us
    pallas_call x1, Pallas kernels, shards(): call(functools.partial(joined_kernel, n_tiles), [VMEM] * 8, [(field, HBM)...  4.12 us
    pallas_call x1, Pallas kernels, shards(): call(prepare_kernel, [HBM] * 9, [(coarse, VMEM)] * 2 + [(staged, VMEM)] *...  3.09 us
    pallas_call x2, Pallas kernels, alone(): call(functools.partial(alone_kernel, is_far), [VMEM] * 4, [(series, VMEM)...  2.6 us
    ppermute x1, starting transfers between devices, shards(): back_1 = lax.ppermute(other_1, 'group', swap)  1.51 us
    pallas_call x1, Pallas kernels, shards(): call(spread_kernel, [VMEM] * 5, [(field, HBM)], [field], (8,))  1.11 us
  transfers between devices with their start and end apart: 5, of which 1 were waited for; matrix products, arithmetic and copies ran while one was open for 0% of the time, Pallas kernels for 37%

profile of v8, /device:TPU:96, one launch (start us, length us, event | category | flops | bytes accessed | tf_op | source)
XLA Modules:
  0.0 44.0 jit_solution(2511920821292890278)
XLA Ops:
  0.6 3.1 %shard_map.112 = (f32[9,8,512]{2,1,0:T(8,128)S(1)}, f32[9,8,512]{2,1,0:T(8,128)S(1)}, f32[16,128,128]{2,1,0:T(8,128)S(1)}, f32[16,128,128]{2,1,0:T(8,128)S(1)}, ...) custom-call(f32[8]{0:T(128)} %courant_in.1, ...), custom_call_target="tpu_custom_call" | custom-call | flops 10000000 | bytes 10000000 | tf_op jit(solution)/shard_map/pallas_call | solution.py:494
  3.7 1.3 %shard_map.114 = (f32[12,128,128]{2,1,0:T(8,128)S(1)}, f32[12,128,128]{2,1,0:T(8,128)S(1)}) custom-call(f32[8,128]{1,0:T(8,128)S(1)} %get-tuple-element.23.half, f32[16,128,128]{2,1,0:T(8,128)S(1)} %get-tuple-element.24.east_0, f32[16,128,128]{2,1,0:T(8,128)S(1)} %get-tuple-element.25.flow_0, f32[16,128,128]{2,1,0:T(8,128)S(1)} %get-tuple-element.26.press_0), custom_call_target="tpu_custom_call" | custom-call | flops 10000000 | bytes 10000000 | tf_op jit(solution)/shard_map/pallas_call | solution.py:523
  5.0 6.7 %collective-permute-start.1 = (f32[12,128,128]{2,1,0:T(8,128)S(1)}, f32[12,128,128]{2,1,0:T(8,128)S(1)}, u32[]{:S(2)}, u32[]{:S(2)}) collective-permute-start(f32[12,128,128]{2,1,0:T(8,128)S(1)} %get-tuple-element.30), channel_id=1, source_target_pairs={{1,2},{2,1},{3,4},{4,3},{5,6},{6,5},{7,8},{8,7},{9,10},{10,9},{11,... | collective-permute-start | bytes 2359304 | tf_op jit(solution)/shard_map/ppermute | solution.py:531
  11.7 1.3 %shard_map.113 = (f32[12,128,128]{2,1,0:T(8,128)S(1)}, f32[12,128,128]{2,1,0:T(8,128)S(1)}) custom-call(f32[8,128]{1,0:T(8,128)S(1)} %get-tuple-element.23.half, f32[16,128,128]{2,1,0:T(8,128)S(1)} %get-tuple-element.24.east_0, f32[16,128,128]{2,1,0:T(8,128)S(1)} %get-tuple-element.25.flow_0, f32[16,128,128]{2,1,0:T(8,128)S(1)} %get-tuple-element.26.press_0), custom_call_target="tpu_custom_call" | custom-call | flops 10000000 | bytes 10000000 | tf_op jit(solution)/shard_map/pallas_call | solution.py:523
  13.0 0.1 collective-permute-start
  13.1 0.7 %collective-permute-start.2 = (f32[9,8,512]{2,1,0:T(8,128)S(1)}, f32[9,8,512]{2,1,0:T(8,128)S(1)}, u32[]{:S(2)}, u32[]{:S(2)}) collective-permute-start(f32[9,8,512]{2,1,0:T(8,128)S(1)} %get-tuple-element.38), channel_id=1, source_target_pairs={{0,64},{64,0},{1,65},{65,1},{2,66},{66,2},{3,67},{67,3},{4,68},{68... | collective-permute-start | bytes 442376 | tf_op jit(solution)/shard_map/ppermute | solution.py:520
  13.8 11.6 %collective-permute-done.2.other = f32[9,8,512]{2,1,0:T(8,128)S(1)} collective-permute-done((f32[9,8,512]{2,1,0:T(8,128)S(1)}, f32[9,8,512]{2,1,0:T(8,128)S(1)}, u32[]{:S(2)}, u32[]{:S(2)}) %collective-permute-start.2) | collective-permute-done | bytes 147488 | tf_op jit(solution)/shard_map/ppermute | solution.py:520
  25.4 7.8 %shard_map.116 = (f32[8,8,384]{2,1,0:T(8,128)S(1)}, f32[8,8,384]{2,1,0:T(8,128)S(1)}) custom-call(f32[256]{0:T(256)S(1)} %get-tuple-element.34.absorption, f32[256]{0:T(256)S(1)} %get-tuple-element.35.weights, f32[2,8,128]{2,1,0:T(8,128)S(1)} %get-tuple-element.36.sun, f32[9,8,512]{2,1,0:T(8,128)S(1)} %get-tuple-element.37.own, ...), custom_call_target="tpu_custom_call" | custom-call | flops 10000000 | bytes 10000000 | tf_op jit(solution)/shard_map/pallas_call | solution.py:537
  33.2 1.5 %collective-permute-start.3 = (f32[8,8,384]{2,1,0:T(8,128)S(1)}, f32[8,8,384]{2,1,0:T(8,128)S(1)}, u32[]{:S(2)}, u32[]{:S(2)}) collective-permute-start(f32[8,8,384]{2,1,0:T(8,128)S(1)} %get-tuple-element.41), channel_id=1, source_target_pairs={{0,64},{64,0},{1,65},{65,1},{2,66},{66,2},{3,67},{67,3},{4,68},{68... | collective-permute-start | bytes 294920 | tf_op jit(solution)/shard_map/ppermute | solution.py:545
  34.7 3.0 %shard_map.117 = (f32[8,8,128]{2,1,0:T(8,128)S(1)}, f32[8,8,128]{2,1,0:T(8,128)S(1)}) custom-call(f32[256]{0:T(256)S(1)} %get-tuple-element.34.absorption, f32[256]{0:T(256)S(1)} %get-tuple-element.35.weights, f32[2,8,128]{2,1,0:T(8,128)S(1)} %get-tuple-element.36.sun, f32[9,8,512]{2,1,0:T(8,128)S(1)} %get-tuple-element.37.own, ...), custom_call_target="tpu_custom_call" | custom-call | flops 10000000 | bytes 10000000 | tf_op jit(solution)/shard_map/pallas_call | solution.py:537
  37.7 0.9 %collective-permute-start.4 = (f32[8,8,128]{2,1,0:T(8,128)S(1)}, f32[8,8,128]{2,1,0:T(8,128)S(1)}, u32[]{:S(2)}, u32[]{:S(2)}) collective-permute-start(f32[8,8,128]{2,1,0:T(8,128)S(1)} %get-tuple-element.42), channel_id=1, source_target_pairs={{0,64},{64,0},{1,65},{65,1},{2,66},{66,2},{3,67},{67,3},{4,68},{68... | collective-permute-start | bytes 98312 | tf_op jit(solution)/shard_map/ppermute | solution.py:547
  38.6 0.0 collective-permute-done.1.from_far
  38.6 0.0 collective-permute-done.from_mate
  38.6 4.1 %shard_map.115 = (f32[8,16,2048]{2,1,0:T(8,128)}, f32[8,16,2048]{2,1,0:T(8,128)}, f32[8,16,2048]{2,1,0:T(8,128)S(1)}) custom-call(f32[8,128]{1,0:T(8,128)S(1)} %get-tuple-element.23.half, f32[16,128,128]{2,1,0:T(8,128)S(1)} %get-tuple-element.24.east_0, f32[16,128,128]{2,1,0:T(8,128)S(1)} %get-tuple-element.25.flow_0, ...), custom_call_target="tpu_custom_call" | custom-call | flops 10000000 | bytes 10000000 | tf_op jit(solution)/shard_map/pallas_call | solution.py:549
  42.7 0.0 collective-permute-done.4.back_2
  42.7 0.0 collective-permute-done.3.back_1
  42.7 1.1 %shard_map.118 = f32[8,16,2048]{2,1,0:T(8,128)} custom-call(f32[8,16,2048]{2,1,0:T(8,128)S(1)} %get-tuple-element.33.press, f32[8,8,384]{2,1,0:T(8,128)S(1)} %get-tuple-element.39.own_1, f32[8,8,128]{2,1,0:T(8,128)S(1)} %get-tuple-element.40.own_2, f32[8,8,384]{2,1,0:T(8,128)S(1)} %collective-permute-done.3.back_1, ...), custom_call_target="tpu_custom_call" | custom-call | flops 10000000 | bytes 10000000 | tf_op jit(solution)/shard_map/pallas_call | solution.py:556
Async XLA Ops:
  5.0 33.5 %collective-permute-start.1 = (f32[12,128,128]{2,1,0:T(8,128)S(1)}, f32[12,128,128]{2,1,0:T(8,128)S(1)}, u32[]{:S(2)}, u32[]{:S(2)}) collective-permute-start(f32[12,128,128]{2,1,0:T(8,128)S(1)} %get-tuple-element.30), channel_id=1, source_target_pairs={{1,2},{2,1},{3,4},{4,3},{5,6},{6,5},{7,8},{8,7},{9,10},{10,9},{11,... | collective-permute-start | bytes 2359304 | tf_op jit(solution)/shard_map/ppermute | solution.py:531
  13.0 25.5 %collective-permute-start = (f32[12,128,128]{2,1,0:T(8,128)S(1)}, f32[12,128,128]{2,1,0:T(8,128)S(1)}, u32[]{:S(2)}, u32[]{:S(2)}) collective-permute-start(f32[12,128,128]{2,1,0:T(8,128)S(1)} %get-tuple-element.29), channel_id=1, source_target_pairs={{0,1},{1,0},{2,3},{3,2},{4,5},{5,4},{6,7},{7,6},{8,9},{9,8},{10,11... | collective-permute-start | bytes 2359304 | tf_op jit(solution)/shard_map/ppermute | solution.py:533
  13.1 12.3 %collective-permute-start.2 = (f32[9,8,512]{2,1,0:T(8,128)S(1)}, f32[9,8,512]{2,1,0:T(8,128)S(1)}, u32[]{:S(2)}, u32[]{:S(2)}) collective-permute-start(f32[9,8,512]{2,1,0:T(8,128)S(1)} %get-tuple-element.38), channel_id=1, source_target_pairs={{0,64},{64,0},{1,65},{65,1},{2,66},{66,2},{3,67},{67,3},{4,68},{68... | collective-permute-start | bytes 442376 | tf_op jit(solution)/shard_map/ppermute | solution.py:520
  33.2 9.5 %collective-permute-start.3 = (f32[8,8,384]{2,1,0:T(8,128)S(1)}, f32[8,8,384]{2,1,0:T(8,128)S(1)}, u32[]{:S(2)}, u32[]{:S(2)}) collective-permute-start(f32[8,8,384]{2,1,0:T(8,128)S(1)} %get-tuple-element.41), channel_id=1, source_target_pairs={{0,64},{64,0},{1,65},{65,1},{2,66},{66,2},{3,67},{67,3},{4,68},{68... | collective-permute-start | bytes 294920 | tf_op jit(solution)/shard_map/ppermute | solution.py:545
  37.7 5.0 %collective-permute-start.4 = (f32[8,8,128]{2,1,0:T(8,128)S(1)}, f32[8,8,128]{2,1,0:T(8,128)S(1)}, u32[]{:S(2)}, u32[]{:S(2)}) collective-permute-start(f32[8,8,128]{2,1,0:T(8,128)S(1)} %get-tuple-element.42), channel_id=1, source_target_pairs={{0,64},{64,0},{1,65},{65,1},{2,66},{66,2},{3,67},{67,3},{4,68},{68... | collective-permute-start | bytes 98312 | tf_op jit(solution)/shard_map/ppermute | solution.py:547
